TPU v7x, 32 devices: a whole 2x2x4 slice. The times are simulated.
32 devices in a mesh: rep: 2 (over y), seq: 4 (over z), head: 2 (over x), sub: 2 (over core).
Axes of the slice: x: 2, y: 2, z: 4, core: 2. Of those that a mesh axis runs over, the one named last changes fastest.
Arguments:
- query_in: bfloat16 [8192, 2048], P(('rep', 'seq', 'sub'), 'head'), parts along dimension 0, may hold values from -6 to 6
- key_in: bfloat16 [8192, 2048], P(('rep', 'seq', 'sub'), 'head'), parts along dimension 0, may hold values from -6 to 6
- value_in: bfloat16 [8192, 2048], P(('rep', 'seq', 'sub'), 'head'), parts along dimension 0, may hold values from -6 to 6
- grad_in: bfloat16 [8192, 2048], P(('rep', 'seq', 'sub'), 'head'), parts along dimension 0, may hold values from -0.0078125 to 0.0078125
Outputs:
- query_gradient: bfloat16 [8192, 2048], P(('rep', 'seq', 'sub'), 'head'), parts along dimension 0
- key_gradient: bfloat16 [8192, 2048], P(('rep', 'seq', 'sub'), 'head'), parts along dimension 0
- value_gradient: bfloat16 [8192, 2048], P(('rep', 'seq', 'sub'), 'head'), parts along dimension 0
There are 2 independent parts, one for each index of `rep`. A program takes and returns all parts, laid end to end along the dimension named above; each array names one. Nothing has to cross between parts.
All inputs are finite; a program needn't handle non-finite values.
Results may differ from a plain program's by a relative error of at most 0.0075.
Values sent between devices are 32-bit elements; how exact they have to be, the bound alone decides.
No kernel may reach another device: no remote copies, remote signals or barrier semaphores. Data moves between devices by JAX's collectives and lax.ppermute only.
A program may use at most 128 MiB of HBM per device.

v0:
```python
import jax
import jax.numpy as jnp
from jax import lax
from jax.sharding import PartitionSpec as P

DH = 128


def prefix(part, axis, combine, identity, reverse):
    count = lax.axis_size(axis)
    place = lax.axis_index(axis)
    ahead = count - 1 - place if reverse else place
    gathered = lax.all_gather(part, axis)
    state = jnp.zeros_like(part) + jnp.asarray(identity, part.dtype)

    def one(step, state):
        source = count - 1 - step if reverse else step
        return combine(state, lax.dynamic_index_in_dim(gathered, source, 0, False))

    return lax.fori_loop(0, ahead, one, state)


def add_states(earlier, later):
    return earlier + later


def state_query_product(form, data, state):
    upper_part = state.astype(jnp.bfloat16)
    lower_part = (state - upper_part.astype(jnp.float32)).astype(jnp.bfloat16)
    first = jnp.einsum(form, data, upper_part, preferred_element_type=jnp.float32)
    return first + jnp.einsum(form, data, lower_part, preferred_element_type=jnp.float32)


def body(query_in, key_in, value_in, grad_in):
    row_count = query_in.shape[0]
    head_count = query_in.shape[1] // DH

    def by_head(array):
        return array.reshape(row_count, head_count, DH)

    query_by_head = by_head(query_in)
    key_by_head = by_head(key_in)
    value_by_head = by_head(value_in)
    gradient_by_head = by_head(grad_in)
    local_state = jnp.einsum(
        "xnm,xnw->nmw", key_by_head, value_by_head, preferred_element_type=jnp.float32
    )
    local_state_gradient = jnp.einsum(
        "xnm,xnw->nmw", query_by_head, gradient_by_head, preferred_element_type=jnp.float32
    )
    prefix_state = prefix(
        local_state, ("seq", "sub"), add_states, jnp.zeros_like(local_state), False
    )
    suffix_state_gradient = prefix(
        local_state_gradient, ("seq", "sub"), add_states, jnp.zeros_like(local_state_gradient), True
    )
    causal = jnp.arange(row_count)[:, None] >= jnp.arange(row_count)[None, :]
    score_gradient = jnp.where(
        causal,
        jnp.einsum(
            "thd,shd->hts", gradient_by_head, value_by_head, preferred_element_type=jnp.float32
        ),
        0.0,
    ).astype(jnp.bfloat16)
    attention_logits = jnp.where(
        causal,
        jnp.einsum("thd,shd->hts", query_by_head, key_by_head, preferred_element_type=jnp.float32),
        0.0,
    ).astype(jnp.bfloat16)
    query_gradient = jnp.einsum(
        "kev,vkl->ekl", score_gradient, key_by_head, preferred_element_type=jnp.float32
    )
    query_gradient = query_gradient + state_query_product(
        "clo,lwo->clw", gradient_by_head, prefix_state
    )
    key_gradient = jnp.einsum(
        "oyk,yov->kov", score_gradient, query_by_head, preferred_element_type=jnp.float32
    )
    key_gradient = key_gradient + state_query_product(
        "jmq,mgq->jmg", value_by_head, suffix_state_gradient
    )
    value_gradient = jnp.einsum(
        "oyk,yov->kov", attention_logits, gradient_by_head, preferred_element_type=jnp.float32
    )
    value_gradient = value_gradient + state_query_product(
        "idx,dxa->ida", key_by_head, suffix_state_gradient
    )
    return (
        query_gradient.astype(jnp.bfloat16).reshape(row_count, head_count * DH),
        key_gradient.astype(jnp.bfloat16).reshape(row_count, head_count * DH),
        value_gradient.astype(jnp.bfloat16).reshape(row_count, head_count * DH),
    )


def solution(mesh):
    placed = (
        P(("rep", "seq", "sub"), "head"),
        P(("rep", "seq", "sub"), "head"),
        P(("rep", "seq", "sub"), "head"),
        P(("rep", "seq", "sub"), "head"),
    )
    return jax.shard_map(
        body,
        mesh=mesh,
        in_specs=placed,
        out_specs=(
            P(("rep", "seq", "sub"), "head"),
            P(("rep", "seq", "sub"), "head"),
            P(("rep", "seq", "sub"), "head"),
        ),
        check_vma=False,
    )
```

profile of v0, /device:TPU:0, one launch (start us, length us, event | category | flops | bytes accessed | tf_op | source)
XLA Modules:
  0.0 152.5 jit_solution(5666386843135638229)
XLA Ops:
  8.4 2.5 %fusion.15 = f32[8,128,128]{2,1,0:T(8,128)} fusion(bf16[512,1024]{1,0:T(8,128)(2,1)} %param.9, bf16[512,1024]{1,0:T(8,128)(2,1)S(1)} %copy-done), kind=kOutput, calls=%fused_computation.19 | convolution fusion | flops 134217728 | bytes 2621440 | tf_op jit(solution)/shard_map/xnm,xnw->nmw/dot_general | solution.py:45
  11.0 1.5 copy.50
  12.5 1.3 fusion.8
  14.0 3.4 %select_convert_fusion.1 = bf16[8,512,512]{2,1,0:T(8,128)(2,1)} fusion(pred[512,512]{1,0:T(8,128)(4,1)S(1)} %iota_compare_fusion, bf16[512,8,128]{0,2,1:T(8,128)(2,1)S(1)} %bitcast.110, bf16[512,1024]{1,0:T(8,128)(2,1)S(1)} %copy-done), kind=kOutput, calls=%fused_computation.3 | convolution fusion | flops 541065216 | bytes 6553600 | tf_op jit(solution)/shard_map/thd,shd->hts/dot_general | solution.py:60
  17.3 43.6 %all-gather.5.cloned.1.call-done = f32[64,128,128]{2,1,0:T(8,128)} async-done(((f32[8,128,128]{2,1,0:T(8,128)}), f32[64,128,128]{2,1,0:T(8,128)}) %all-gather.5.cloned.1.call-update) | async-done | bytes 4194320 | tf_op jit(solution)/shard_map/all_gather | solution.py:13
  61.0 1.8 %fusion.44 = f32[8,128,512]{2,1,0:T(8,128)} fusion(bf16[512,8,128]{0,2,1:T(8,128)(2,1)S(1)} %bitcast.111, f32[8,128,128]{2,1,0:T(8,128)S(1)} %get-tuple-element.82), kind=kOutput, calls=%fused_computation.49 | convolution fusion | flops 134348800 | bytes 3670016 | tf_op jit(solution)/shard_map/clo,lwo->clw/dot_general | solution.py:30
  62.8 1.7 %fusion.42 = f32[8,128,512]{2,1,0:T(8,128)} fusion(bf16[512,8,128]{0,2,1:T(8,128)(2,1)S(1)} %bitcast.112, f32[8,128,128]{2,1,0:T(8,128)S(1)} %get-tuple-element.82), kind=kOutput, calls=%fused_computation.47 | convolution fusion | flops 134742016 | bytes 3670016 | tf_op jit(solution)/shard_map/clo,lwo->clw/dot_general | solution.py:31
  64.6 44.5 %all-gather.7.cloned.1.call-done = f32[64,128,128]{2,1,0:T(8,128)} async-done(((f32[8,128,128]{2,1,0:T(8,128)}), f32[64,128,128]{2,1,0:T(8,128)}) %all-gather.7.cloned.1.call-update) | async-done | bytes 4194320 | tf_op jit(solution)/shard_map/all_gather | solution.py:13
  109.1 8.3 %while.23 = (s32[]{:T(128)}, f32[8,128,128]{2,1,0:T(8,128)S(1)}, s32[]{:T(128)}, f32[8,8,128,128]{3,2,1,0:T(8,128)}, s32[]{:T(128)}, /*index=5*/s32[]{:T(128)}, s32[]{:T(128)}, s32[]{:T(128)}) while((s32[]{:T(128)}, f32[8,128,128]{2,1,0:T(8,128)S(1)}, s32[]{:T(128)}, f32[8,8,128,128]{3,2,1,0:T(8,128)}, s32[]{:T(128)}, /*index=5*/s32[]{:T(128)}, ...), condition=%wide.region_3.4_spmd, body=%wide.region_2.3_spmd.sunk | while | flops 131078 | bytes 1573007 | solution.py:20
  109.1 1.2 bitcast_add_fusion.8
  110.3 1.2 bitcast_add_fusion.8
  111.5 1.2 bitcast_add_fusion.8
  112.7 1.2 bitcast_add_fusion.8
  113.9 1.2 bitcast_add_fusion.8
  117.4 1.8 %fusion.24 = f32[8,128,512]{2,1,0:T(8,128)} fusion(f32[8,128,128]{2,1,0:T(8,128)S(1)} %get-tuple-element.83, bf16[512,1024]{1,0:T(8,128)(2,1)S(1)} %copy-done), kind=kOutput, calls=%fused_computation.28 | convolution fusion | flops 134348800 | bytes 3670016 | tf_op jit(solution)/shard_map/jmq,mgq->jmg/dot_general | solution.py:30
  119.2 1.7 %fusion.22 = f32[8,128,512]{2,1,0:T(8,128)} fusion(f32[8,128,128]{2,1,0:T(8,128)S(1)} %get-tuple-element.83, bf16[512,1024]{1,0:T(8,128)(2,1)S(1)} %copy-done), kind=kOutput, calls=%fused_computation.26 | convolution fusion | flops 134742016 | bytes 3670016 | tf_op jit(solution)/shard_map/jmq,mgq->jmg/dot_general | solution.py:31
  121.0 1.8 %fusion.20 = f32[8,128,512]{2,1,0:T(8,128)} fusion(f32[8,128,128]{2,1,0:T(8,128)S(1)} %get-tuple-element.83, bf16[512,1024]{1,0:T(8,128)(2,1)S(1)} %copy-done.2), kind=kOutput, calls=%fused_computation.24 | convolution fusion | flops 134348800 | bytes 3670016 | tf_op jit(solution)/shard_map/idx,dxa->ida/dot_general | solution.py:30
  122.8 1.8 %fusion.18 = f32[8,128,512]{2,1,0:T(8,128)} fusion(f32[8,128,128]{2,1,0:T(8,128)S(1)} %get-tuple-element.83, bf16[512,1024]{1,0:T(8,128)(2,1)S(1)} %copy-done.2), kind=kOutput, calls=%fused_computation.22 | convolution fusion | flops 134742016 | bytes 3670016 | tf_op jit(solution)/shard_map/idx,dxa->ida/dot_general | solution.py:31
  125.3 2.5 %fusion.7 = bf16[512,8,128]{0,2,1:T(8,128)(2,1)} fusion(f32[8,128,512]{2,1,0:T(8,128)S(1)} %copy-done.4, f32[8,128,512]{2,1,0:T(8,128)S(1)} %copy-done.5, bf16[8,512,512]{2,1,0:T(8,128)(2,1)S(1)} %copy-done.1, bf16[512,1024]{1,0:T(8,128)(2,1)S(1)} %copy-done.2), kind=kOutput, calls=%fused_computation.13 | convolution fusion | flops 538443776 | bytes 10485760 | tf_op jit(solution)/shard_map/kev,vkl->ekl/dot_general | solution.py:70
  127.8 2.4 %copy.44 = bf16[512,1024]{1,0:T(8,128)(2,1)} copy(bf16[512,1024]{0,1:T(8,128)(2,1)} %bitcast.115) | data formatting | bytes 2097152
  130.2 5.3 %fusion.6 = bf16[512,8,128]{0,2,1:T(8,128)(2,1)} fusion(f32[8,128,512]{2,1,0:T(8,128)} %fusion.24, f32[8,128,512]{2,1,0:T(8,128)} %fusion.22, bf16[8,512,512]{2,1,0:T(8,128)(2,1)} %select_convert_fusion.1, bf16[512,1024]{1,0:T(8,128)(2,1)S(1)} %copy-done.7), kind=kOutput, calls=%fused_computation.11 | convolution fusion | flops 538443776 | bytes 10485760 | tf_op jit(solution)/shard_map/oyk,yov->kov/dot_general | solution.py:76
  135.5 2.4 %copy.45 = bf16[512,1024]{1,0:T(8,128)(2,1)} copy(bf16[512,1024]{0,1:T(8,128)(2,1)} %bitcast.114) | data formatting | bytes 2097152
  137.8 5.6 %fusion.5 = bf16[512,8,128]{0,2,1:T(8,128)(2,1)} fusion(f32[8,128,512]{2,1,0:T(8,128)} %fusion.20, f32[8,128,512]{2,1,0:T(8,128)} %fusion.18, bf16[512,8,128]{0,2,1:T(8,128)(2,1)S(1)} %bitcast.113, pred[512,512]{1,0:T(8,128)(4,1)S(1)} %iota_compare_fusion, bf16[512,1024]{1,0:T(8,128)(2,1)} %param.8, bf16[512,1024]{1,0:T(8,128)(2,1)S(1)} %copy-done.3), kind=kOutput, calls=%fused_computation.9 | convolution fusion | flops 1079508992 | bytes 8650752 | tf_op jit(solution)/shard_map/oyk,yov->kov/dot_general | solution.py:82
  143.4 2.3 %copy.46 = bf16[512,1024]{1,0:T(8,128)(2,1)} copy(bf16[512,1024]{0,1:T(8,128)(2,1)} %bitcast.118) | data formatting | bytes 2097152
  (26 shorter events, 4.5 us)
Async XLA Ops:
  7.2 1.2 copy-start
  7.2 5.3 %copy-start.6 = (bf16[512,1024]{1,0:T(8,128)(2,1)S(1)}, bf16[512,1024]{1,0:T(8,128)(2,1)}, u32[]{:S(2)}) copy-start(bf16[512,1024]{1,0:T(8,128)(2,1)} %param.8) | copy-start | bytes 3145732
  7.2 53.8 %all-gather.5.cloned.1.call-start = ((), (), s32[]{:S(2)}) async-start(), calls=%async_computation | async-start | bytes 4718592 | tf_op jit(solution)/shard_map/all_gather | solution.py:13
  11.0 98.1 %all-gather.7.cloned.1.call-start = ((), (), s32[]{:S(2)}) async-start(), calls=%async_computation.1 | async-start | bytes 4718592 | tf_op jit(solution)/shard_map/all_gather | solution.py:13
  119.2 1.8 %copy-start.2 = (bf16[512,1024]{1,0:T(8,128)(2,1)S(1)}, bf16[512,1024]{1,0:T(8,128)(2,1)}, u32[]{:S(2)}) copy-start(bf16[512,1024]{1,0:T(8,128)(2,1)} %param.9) | copy-start | bytes 3145732
  119.2 5.4 %copy-start.5 = (f32[8,128,512]{2,1,0:T(8,128)S(1)}, f32[8,128,512]{2,1,0:T(8,128)}, u32[]{:S(2)}) copy-start(f32[8,128,512]{2,1,0:T(8,128)} %fusion.42) | copy-start | bytes 6291460
  121.0 3.7 %copy-start.1 = (bf16[8,512,512]{2,1,0:T(8,128)(2,1)S(1)}, bf16[8,512,512]{2,1,0:T(8,128)(2,1)}, u32[]{:S(2)}) copy-start(bf16[8,512,512]{2,1,0:T(8,128)(2,1)} %select_convert_fusion.1) | copy-start | bytes 12582916
  122.8 2.5 %copy-start.4 = (f32[8,128,512]{2,1,0:T(8,128)S(1)}, f32[8,128,512]{2,1,0:T(8,128)}, u32[]{:S(2)}) copy-start(f32[8,128,512]{2,1,0:T(8,128)} %fusion.44) | copy-start | bytes 6291460
  127.8 2.4 %copy-start.7 = (bf16[512,1024]{1,0:T(8,128)(2,1)S(1)}, bf16[512,1024]{1,0:T(8,128)(2,1)}, u32[]{:S(2)}) copy-start(bf16[512,1024]{1,0:T(8,128)(2,1)} %param.8) | copy-start | bytes 3145732
  135.5 2.4 %copy-start.3 = (bf16[512,1024]{1,0:T(8,128)(2,1)S(1)}, bf16[512,1024]{1,0:T(8,128)(2,1)}, u32[]{:S(2)}) copy-start(bf16[512,1024]{1,0:T(8,128)(2,1)} %param.9) | copy-start | bytes 3145732
Sparse Core Ops, SparseCore 0:
  11.1 49.8 all-gather.4
  63.1 45.8 all-gather.6
where the time goes:
time: 153 us; the launch traced here: 152 us
  waiting for transfers between devices  88.2 us (58%)
  matrix products  31.3 us (20%)
  between operations  14.1 us (9%)
  local copies, waits for them, and re-layouts  10.4 us (7%)
  other arithmetic  8.26 us (5%)
    all_gather x2, waiting for transfers between devices, prefix(): gathered = lax.all_gather(part, axis)  88.1 us
    unnamed x19, local copies, waits for them, and re-layouts  8.84 us
    add x7, other arithmetic, add_states(): return earlier + later  8.18 us
    dot_general x1, matrix products, body(): jnp.einsum('oyk,yov->kov', attention_logits, gradient_by_head, preferred_...  5.56 us
    dot_general x3, matrix products, state_query_product(): jnp.einsum(form, data, upper_part, preferred_element_type=jnp.float32)  5.42 us
    dot_general x3, matrix products, state_query_product(): jnp.einsum(form, data, lower_part, preferred_element_type=jnp.float32)  5.32 us
    dot_general x1, matrix products, body(): jnp.einsum('oyk,yov->kov', score_gradient, query_by_head, preferred_eleme...  5.29 us
    dot_general x1, matrix products, body(): jnp.einsum('thd,shd->hts', gradient_by_head, value_by_head, preferred_ele...  3.37 us
  transfers between devices with their start and end apart: 2, of which 2 were waited for; matrix products, arithmetic and copies ran while one was open for 6% of the time, Pallas kernels for 0%

commit v1 on v0

v1 whole, which is shorter than its diff:
```python
import functools

import jax
import jax.numpy as jnp
from jax import lax
from jax.experimental import pallas as pl
from jax.experimental.pallas import tpu as pltpu
from jax.sharding import PartitionSpec as P

DH = 128
F32 = jnp.float32
BF16 = jnp.bfloat16
VMEM = pl.BlockSpec(memory_space=pltpu.VMEM)
HBM = pl.BlockSpec(memory_space=pltpu.HBM)
SMEM = pl.BlockSpec(memory_space=pltpu.SMEM)


def product(left, right, left_axis, right_axis):
    return lax.dot_general(
        left, right, (((left_axis,), (right_axis,)), ((), ())), preferred_element_type=F32
    )


def head_columns(head):
    return slice(head * DH, (head + 1) * DH)


def states_kernel(core, q_hbm, k_hbm, v_hbm, g_hbm, q, k, v, g, give, keep, sems):
    copies = [
        pltpu.make_async_copy(source, target, sems.at[i])
        for i, (source, target) in enumerate(zip((q_hbm, k_hbm, v_hbm, g_hbm), (q, k, v, g)))
    ]
    heads = give.shape[0]
    for c in (0, 3, 1, 2):
        copies[c].start()
    is_first = core[0] == 0
    copies[0].wait()
    copies[3].wait()

    def state(left, right, out):
        for h in range(heads):
            c = head_columns(h)
            out[h] = product(left[:, c], right[:, c], 0, 0)

    @pl.when(is_first)
    def _():
        state(q, g, give)

    @pl.when(jnp.logical_not(is_first))
    def _():
        state(q, g, keep)

    copies[1].wait()
    copies[2].wait()

    @pl.when(is_first)
    def _():
        state(k, v, keep)

    @pl.when(jnp.logical_not(is_first))
    def _():
        state(k, v, give)


def states(core, q, k, v, g):
    rows, width = q.shape
    heads = width // DH
    return pl.pallas_call(
        states_kernel,
        in_specs=[SMEM] + [HBM] * 4,
        out_specs=[VMEM] * 6,
        out_shape=[pltpu.VMEM(q.shape, BF16)] * 4 + [pltpu.VMEM((heads, DH, DH), F32)] * 2,
        scratch_shapes=[pltpu.SemaphoreType.DMA((4,))],
        compiler_params=pltpu.CompilerParams(vmem_limit_bytes=8 << 20),
        name="states",
    )(core, *[pltpu.with_memory_space_constraint(x, pltpu.HBM) for x in (q, k, v, g)])


def intra_kernel(first, q, k, v, g, dq, dk, dv):
    rows = q.shape[0]
    row = lax.broadcasted_iota(jnp.int32, (rows, rows), 0)
    col = lax.broadcasted_iota(jnp.int32, (rows, rows), 1)
    for h in range(dq.shape[1] // DH):
        c, o = head_columns(first + h), head_columns(h)
        qh, kh, vh, gh = q[:, c], k[:, c], v[:, c], g[:, c]
        grad_scores = jnp.where(row >= col, product(gh, vh, 1, 1), 0.0).astype(BF16)
        dq[:, o] = product(grad_scores, kh, 1, 0)
        dk[:, o] = product(grad_scores, qh, 0, 0)
        attn_scores = jnp.where(row <= col, product(kh, qh, 1, 1), 0.0).astype(BF16)
        dv[:, o] = product(attn_scores, gh, 1, 0)


def intra(first, heads, q, k, v, g):
    return pl.pallas_call(
        functools.partial(intra_kernel, first),
        in_specs=[VMEM] * 4,
        out_specs=[VMEM] * 3,
        out_shape=[pltpu.VMEM((q.shape[0], heads * DH), F32)] * 3,
        compiler_params=pltpu.CompilerParams(vmem_limit_bytes=16 << 20),
        name="intra",
    )(q, k, v, g)


def final_kernel(core, k, v, g, mine, other, dqi, dki, dvi, dq_hbm, dk_hbm, dv_hbm, dq, dk, dv, sems):
    heads = mine.shape[0]
    is_first = core[0] == 0
    copies = []
    for h in range(heads):
        c = head_columns(h)
        prefix = jnp.where(is_first, mine[h], other[h]).astype(BF16)
        suffix = jnp.where(is_first, other[h], mine[h]).astype(BF16)
        dq[:, c] = (dqi[:, c] + product(g[:, c], prefix, 1, 1)).astype(BF16)
        dk[:, c] = (dki[:, c] + product(v[:, c], suffix, 1, 1)).astype(BF16)
        dv[:, c] = (dvi[:, c] + product(k[:, c], suffix, 1, 0)).astype(BF16)
        if h % 2 == 1 or h == heads - 1:
            cc = slice((h - h % 2) * DH, (h + 1) * DH)
            for i, (source, target) in enumerate(((dq, dq_hbm), (dk, dk_hbm), (dv, dv_hbm))):
                copy = pltpu.make_async_copy(source.at[:, cc], target.at[:, cc], sems.at[i, h // 2])
                copy.start()
                copies.append(copy)
    for copy in copies:
        copy.wait()


def final(core, k, v, g, mine, other, dqi, dki, dvi):
    shape = jax.ShapeDtypeStruct(k.shape, BF16)
    heads = mine.shape[0]
    return pl.pallas_call(
        final_kernel,
        in_specs=[SMEM] + [VMEM] * 8,
        out_specs=[HBM] * 3,
        out_shape=[shape] * 3,
        scratch_shapes=[pltpu.VMEM(k.shape, BF16)] * 3
        + [pltpu.SemaphoreType.DMA((3, (heads + 1) // 2))],
        compiler_params=pltpu.CompilerParams(vmem_limit_bytes=16 << 20),
        name="final",
    )(core, k, v, g, mine, other, dqi, dki, dvi)


def body(query_in, key_in, value_in, grad_in):
    chips = lax.axis_size("seq")
    core = lax.axis_index("sub").astype(jnp.int32).reshape(1)
    heads = query_in.shape[1] // DH
    swap = [(0, 1), (1, 0)]
    q, k, v, g, give, keep = states(core, query_in, key_in, value_in, grad_in)
    total = keep + lax.ppermute(give, "sub", swap)
    mine = None
    arrived = None
    for step in range(chips - 1):
        pairs = [
            (2 * step, 2 * step + 2),
            (2 * (chips - 1 - step) + 1, 2 * (chips - 2 - step) + 1),
        ]
        sent = total if arrived is None else total + arrived
        arrived = lax.ppermute(sent, ("seq", "sub"), pairs)
        mine = arrived if mine is None else mine + arrived
    other = lax.ppermute(mine + keep, "sub", swap)
    dqi, dki, dvi = intra(0, heads, q, k, v, g)
    return tuple(final(core, k, v, g, mine, other, dqi, dki, dvi))


def solution(mesh):
    placed = P(("rep", "seq", "sub"), "head")
    return jax.shard_map(
        body, mesh=mesh, in_specs=(placed,) * 4, out_specs=(placed,) * 3, check_vma=False
    )
```

time: 153 us -> 43.8 us (0.29)
  waiting for transfers between devices: 88.2 us -> 8.19 us
  matrix products: 31.3 us -> 0 us
  starting transfers between devices: 0.08 us -> 23.6 us
  between operations: 14.1 us -> 0.72 us
  Pallas kernels: 0 us -> 10.7 us
  local copies, waits for them, and re-layouts: 10.4 us -> 0 us
  other arithmetic: 8.26 us -> 0.35 us
    all_gather x2 -> x0, waiting for transfers between devices: 88.1 us -> none  [prefix(): gathered = lax.all_gather(part, axis)]
    dot_general x12 -> x0, matrix products: 31.3 us -> none  [the longest x1 5.56 us: body(): jnp.einsum('oyk,yov->kov', attention_logits, gradient_by_head, preferred_...]
    ppermute x0 -> x5, starting transfers between devices: none -> 23.6 us  [the longest x1 16.8 us: body(): other = lax.ppermute(mine + keep, 'sub', swap)]
    pallas_call x0 -> x3, Pallas kernels: none -> 10.7 us  [the longest x1 5.73 us: intra(): pl.pallas_call(functools.partial(intra_kernel, first), in_specs=[VMEM] *...]
    unnamed x19 -> x0, local copies, waits for them, and re-layouts: 8.84 us -> none
    ppermute x0 -> x5, waiting for transfers between devices: none -> 8.19 us  [the longest x3 6.65 us: body(): arrived = lax.ppermute(sent, ('seq', 'sub'), pairs)]
    add x7 -> x4, other arithmetic: 8.18 us -> 0.35 us  [the longest x2 0.15 us: body(): sent = total if arrived is None else total + arrived]
  transfers between devices with their start and end apart: 2 -> 5, of which waited for: 2 -> 2; matrix products, arithmetic and copies ran while one was open for 6% -> 0% of each run, Pallas kernels for 0% -> 13%
where the time goes in v1:
time: 43.8 us; the launch traced here: 43.6 us
  starting transfers between devices  23.6 us (54%)
  Pallas kernels  10.7 us (24%)
  waiting for transfers between devices  8.19 us (19%)
  between operations  0.72 us (2%)
    ppermute x1, starting transfers between devices, body(): other = lax.ppermute(mine + keep, 'sub', swap)  16.8 us
    ppermute x3, waiting for transfers between devices, body(): arrived = lax.ppermute(sent, ('seq', 'sub'), pairs)  6.65 us
    ppermute x3, starting transfers between devices, body(): arrived = lax.ppermute(sent, ('seq', 'sub'), pairs)  6.26 us
    pallas_call x1, Pallas kernels, intra(): pl.pallas_call(functools.partial(intra_kernel, first), in_specs=[VMEM] *...  5.73 us
    pallas_call x1, Pallas kernels, states(): pl.pallas_call(states_kernel, in_specs=[SMEM] + [HBM] * 4, out_specs=[VME...  2.73 us
    pallas_call x1, Pallas kernels, final(): pl.pallas_call(final_kernel, in_specs=[SMEM] + [VMEM] * 8, out_specs=[HBM...  2.29 us
    ppermute x1, waiting for transfers between devices, body(): total = keep + lax.ppermute(give, 'sub', swap)  1.54 us
  transfers between devices with their start and end apart: 5, of which 2 were waited for; matrix products, arithmetic and copies ran while one was open for 0% of the time, Pallas kernels for 13%

profile of v1, /device:TPU:0, one launch (start us, length us, event | category | flops | bytes accessed | tf_op | source)
XLA Modules:
  0.0 43.6 jit_solution(3622311879795942261)
XLA Ops:
  0.6 2.7 %states.1 = (bf16[512,1024]{1,0:T(8,128)(2,1)S(1)}, bf16[512,1024]{1,0:T(8,128)(2,1)S(1)}, bf16[512,1024]{1,0:T(8,128)(2,1)S(1)}, bf16[512,1024]{1,0:T(8,128)(2,...) custom-call(s32[1]{0:T(128)} %bitcast.core, bf16[512,1024]{1,0:T(8,128)(2,1)} %q_hbm.1, ...), custom_call_target="tpu_custom_call" | custom-call | tf_op jit(solution)/shard_map/states/pallas_call | solution.py:68
  3.4 0.5 %collective-permute-start = (f32[8,128,128]{2,1,0:T(8,128)S(1)}, f32[8,128,128]{2,1,0:T(8,128)S(1)}, u32[]{:S(2)}, u32[]{:S(2)}) collective-permute-start(f32[8,128,128]{2,1,0:T(8,128)S(1)} %get-tuple-element.16), channel_id=1, source_target_pairs={{0,1},{1,0},{2,3},{3,2},{4,5},{5,4},{6,7},{7,6},{8,9},{9,8},{10,11... | collective-permute-start | bytes 1572872 | tf_op jit(solution)/shard_map/ppermute | solution.py:146
  3.9 1.5 %collective-permute-done = f32[8,128,128]{2,1,0:T(8,128)S(1)} collective-permute-done((f32[8,128,128]{2,1,0:T(8,128)S(1)}, f32[8,128,128]{2,1,0:T(8,128)S(1)}, u32[]{:S(2)}, u32[]{:S(2)}) %collective-permute-start) | collective-permute-done | bytes 524320 | tf_op jit(solution)/shard_map/ppermute | solution.py:146
  5.4 0.1 add.18
  5.5 4.9 %collective-permute-start.1 = (f32[8,128,128]{2,1,0:T(8,128)S(1)}, f32[8,128,128]{2,1,0:T(8,128)S(1)}, u32[]{:S(2)}, u32[]{:S(2)}) collective-permute-start(f32[8,128,128]{2,1,0:T(8,128)S(1)} %add.18), channel_id=1, source_target_pairs={{0,4},{13,9},{2,6},{15,11},{16,20},{29,25},{18,22},{31,27}} | collective-permute-start | bytes 1572872 | tf_op jit(solution)/shard_map/ppermute | solution.py:155
  10.4 6.6 %collective-permute-done.1 = f32[8,128,128]{2,1,0:T(8,128)S(1)} collective-permute-done((f32[8,128,128]{2,1,0:T(8,128)S(1)}, f32[8,128,128]{2,1,0:T(8,128)S(1)}, u32[]{:S(2)}, u32[]{:S(2)}) %collective-permute-start.1) | collective-permute-done | bytes 524320 | tf_op jit(solution)/shard_map/ppermute | solution.py:155
  17.0 0.1 add.19
  17.1 0.7 %collective-permute-start.2 = (f32[8,128,128]{2,1,0:T(8,128)S(1)}, f32[8,128,128]{2,1,0:T(8,128)S(1)}, u32[]{:S(2)}, u32[]{:S(2)}) collective-permute-start(f32[8,128,128]{2,1,0:T(8,128)S(1)} %add.19), channel_id=1, source_target_pairs={{4,8},{9,5},{6,10},{11,7},{20,24},{25,21},{22,26},{27,23}} | collective-permute-start | bytes 1572872 | tf_op jit(solution)/shard_map/ppermute | solution.py:155
  17.8 0.0 collective-permute-done.2
  17.8 0.1 add.21
  17.9 0.7 %collective-permute-start.3 = (f32[8,128,128]{2,1,0:T(8,128)S(1)}, f32[8,128,128]{2,1,0:T(8,128)S(1)}, u32[]{:S(2)}, u32[]{:S(2)}) collective-permute-start(f32[8,128,128]{2,1,0:T(8,128)S(1)} %add.21), channel_id=1, source_target_pairs={{8,12},{5,1},{10,14},{7,3},{24,28},{21,17},{26,30},{23,19}} | collective-permute-start | bytes 1572872 | tf_op jit(solution)/shard_map/ppermute | solution.py:155
  18.6 0.0 collective-permute-done.3
  18.6 0.1 fusion
  18.7 16.8 %collective-permute-start.4 = (f32[8,128,128]{2,1,0:T(8,128)S(1)}, f32[8,128,128]{2,1,0:T(8,128)S(1)}, u32[]{:S(2)}, u32[]{:S(2)}) collective-permute-start(f32[8,128,128]{2,1,0:T(8,128)S(1)} %get-tuple-element.21), channel_id=1, source_target_pairs={{0,1},{1,0},{2,3},{3,2},{4,5},{5,4},{6,7},{7,6},{8,9},{9,8},{10,11... | collective-permute-start | bytes 1572872 | tf_op jit(solution)/shard_map/ppermute | solution.py:157
  35.6 5.7 %intra.1 = (f32[512,1024]{1,0:T(8,128)S(1)}, f32[512,1024]{1,0:T(8,128)S(1)}, f32[512,1024]{1,0:T(8,128)S(1)}) custom-call(bf16[512,1024]{1,0:T(8,128)(2,1)S(1)} %get-tuple-element.17.q, bf16[512,1024]{1,0:T(8,128)(2,1)S(1)} %get-tuple-element.12.k, bf16[512,1024]{1,0:T(8,128)(2,1)S(1)} %get-tuple-element.13.v, bf16[512,1024]{1,0:T(8,128)(2,1)S(1)} %get-tuple-element.14.g), custom_call_target="tpu_custom_call" | custom-call | tf_op jit(solution)/shard_map/intra/pallas_call | solution.py:94
  41.3 0.0 collective-permute-done.4.other
  41.3 2.3 %final.1 = (bf16[512,1024]{1,0:T(8,128)(2,1)}, bf16[512,1024]{1,0:T(8,128)(2,1)}, bf16[512,1024]{1,0:T(8,128)(2,1)}) custom-call(s32[1]{0:T(128)} %bitcast.core, bf16[512,1024]{1,0:T(8,128)(2,1)S(1)} %get-tuple-element.12.k, bf16[512,1024]{1,0:T(8,128)(2,1)S(1)} %get-tuple-element.13.v, bf16[512,1024]{1,0:T(8,128)(2,1)S(1)} %get-tuple-element.14.g, ...), custom_call_target="tpu_custom_call" | custom-call | tf_op jit(solution)/shard_map/final/pallas_call | solution.py:128
Async XLA Ops:
  3.4 2.1 %collective-permute-start = (f32[8,128,128]{2,1,0:T(8,128)S(1)}, f32[8,128,128]{2,1,0:T(8,128)S(1)}, u32[]{:S(2)}, u32[]{:S(2)}) collective-permute-start(f32[8,128,128]{2,1,0:T(8,128)S(1)} %get-tuple-element.16), channel_id=1, source_target_pairs={{0,1},{1,0},{2,3},{3,2},{4,5},{5,4},{6,7},{7,6},{8,9},{9,8},{10,11... | collective-permute-start | bytes 1572872 | tf_op jit(solution)/shard_map/ppermute | solution.py:146
  5.5 11.5 %collective-permute-start.1 = (f32[8,128,128]{2,1,0:T(8,128)S(1)}, f32[8,128,128]{2,1,0:T(8,128)S(1)}, u32[]{:S(2)}, u32[]{:S(2)}) collective-permute-start(f32[8,128,128]{2,1,0:T(8,128)S(1)} %add.18), channel_id=1, source_target_pairs={{0,4},{13,9},{2,6},{15,11},{16,20},{29,25},{18,22},{31,27}} | collective-permute-start | bytes 1572872 | tf_op jit(solution)/shard_map/ppermute | solution.py:155
  17.1 0.7 %collective-permute-start.2 = (f32[8,128,128]{2,1,0:T(8,128)S(1)}, f32[8,128,128]{2,1,0:T(8,128)S(1)}, u32[]{:S(2)}, u32[]{:S(2)}) collective-permute-start(f32[8,128,128]{2,1,0:T(8,128)S(1)} %add.19), channel_id=1, source_target_pairs={{4,8},{9,5},{6,10},{11,7},{20,24},{25,21},{22,26},{27,23}} | collective-permute-start | bytes 1572872 | tf_op jit(solution)/shard_map/ppermute | solution.py:155
  17.9 0.7 %collective-permute-start.3 = (f32[8,128,128]{2,1,0:T(8,128)S(1)}, f32[8,128,128]{2,1,0:T(8,128)S(1)}, u32[]{:S(2)}, u32[]{:S(2)}) collective-permute-start(f32[8,128,128]{2,1,0:T(8,128)S(1)} %add.21), channel_id=1, source_target_pairs={{8,12},{5,1},{10,14},{7,3},{24,28},{21,17},{26,30},{23,19}} | collective-permute-start | bytes 1572872 | tf_op jit(solution)/shard_map/ppermute | solution.py:155
  18.7 22.5 %collective-permute-start.4 = (f32[8,128,128]{2,1,0:T(8,128)S(1)}, f32[8,128,128]{2,1,0:T(8,128)S(1)}, u32[]{:S(2)}, u32[]{:S(2)}) collective-permute-start(f32[8,128,128]{2,1,0:T(8,128)S(1)} %get-tuple-element.21), channel_id=1, source_target_pairs={{0,1},{1,0},{2,3},{3,2},{4,5},{5,4},{6,7},{7,6},{8,9},{9,8},{10,11... | collective-permute-start | bytes 1572872 | tf_op jit(solution)/shard_map/ppermute | solution.py:157

commit v2 on v1

v2 whole, which is shorter than its diff:
```python
import functools

import jax
import jax.numpy as jnp
from jax import lax
from jax.experimental import pallas as pl
from jax.experimental.pallas import tpu as pltpu
from jax.sharding import PartitionSpec as P

DH = 128
F32 = jnp.float32
BF16 = jnp.bfloat16
VMEM = pl.BlockSpec(memory_space=pltpu.VMEM)
HBM = pl.BlockSpec(memory_space=pltpu.HBM)
SMEM = pl.BlockSpec(memory_space=pltpu.SMEM)


def product(left, right, left_axis, right_axis):
    return lax.dot_general(
        left, right, (((left_axis,), (right_axis,)), ((), ())), preferred_element_type=F32
    )


def head_columns(head):
    return slice(head * DH, (head + 1) * DH)


def states_kernel(core, q_hbm, k_hbm, v_hbm, g_hbm, q, k, v, g, *rest):
    parts = (len(rest) - 1) // 2
    give, keep, sems = rest[:parts], rest[parts : 2 * parts], rest[-1]
    copies = [
        pltpu.make_async_copy(source, target, sems.at[i])
        for i, (source, target) in enumerate(zip((q_hbm, k_hbm, v_hbm, g_hbm), (q, k, v, g)))
    ]
    for c in (0, 3, 1, 2):
        copies[c].start()
    is_first = core[0] == 0

    def state(left, right, outs):
        h = 0
        for out in outs:
            for i in range(out.shape[0]):
                c = head_columns(h)
                out[i] = product(left[:, c], right[:, c], 0, 0)
                h += 1

    for left, right, give_first in ((0, 3, True), (1, 2, False)):
        copies[left].wait()
        copies[right].wait()
        pair = (q, k, v, g)[left], (q, k, v, g)[right]

        @pl.when(is_first)
        def _():
            state(*pair, give if give_first else keep)

        @pl.when(jnp.logical_not(is_first))
        def _():
            state(*pair, keep if give_first else give)


def states(core, parts, q, k, v, g):
    outs = [pltpu.VMEM((n, DH, DH), F32) for n in parts] * 2
    result = pl.pallas_call(
        states_kernel,
        in_specs=[SMEM] + [HBM] * 4,
        out_specs=[VMEM] * (4 + len(outs)),
        out_shape=[pltpu.VMEM(q.shape, BF16)] * 4 + outs,
        scratch_shapes=[pltpu.SemaphoreType.DMA((4,))],
        compiler_params=pltpu.CompilerParams(vmem_limit_bytes=8 << 20),
        name="states",
    )(core, *[pltpu.with_memory_space_constraint(x, pltpu.HBM) for x in (q, k, v, g)])
    return result[:4], result[4 : 4 + len(parts)], result[4 + len(parts) :]


def intra_kernel(first, q, k, v, g, dq, dk, dv):
    rows = q.shape[0]
    row = lax.broadcasted_iota(jnp.int32, (rows, rows), 0)
    col = lax.broadcasted_iota(jnp.int32, (rows, rows), 1)
    for h in range(dq.shape[1] // DH):
        c, o = head_columns(first + h), head_columns(h)
        qh, kh, vh, gh = q[:, c], k[:, c], v[:, c], g[:, c]
        grad_scores = jnp.where(row >= col, product(gh, vh, 1, 1), 0.0).astype(BF16)
        dq[:, o] = product(grad_scores, kh, 1, 0)
        dk[:, o] = product(grad_scores, qh, 0, 0)
        attn_scores = jnp.where(row <= col, product(kh, qh, 1, 1), 0.0).astype(BF16)
        dv[:, o] = product(attn_scores, gh, 1, 0)


def intra(first, heads, q, k, v, g):
    return pl.pallas_call(
        functools.partial(intra_kernel, first),
        in_specs=[VMEM] * 4,
        out_specs=[VMEM] * 3,
        out_shape=[pltpu.VMEM((q.shape[0], heads * DH), F32)] * 3,
        compiler_params=pltpu.CompilerParams(vmem_limit_bytes=16 << 20),
        name="intra",
    )(q, k, v, g)


def final_kernel(parts, core, k, v, g, *rest):
    count = len(parts)
    mine, other, rest = rest[:count], rest[count : 2 * count], rest[2 * count :]
    local, rest = rest[: 3 * count], rest[3 * count :]
    (targets, outs, sems) = rest[:3], rest[3:6], rest[6]
    is_first = core[0] == 0
    copies = []
    first = 0
    for p in range(count):
        for i in range(parts[p]):
            c, o = head_columns(first + i), head_columns(i)
            prefix = jnp.where(is_first, mine[p][i], other[p][i]).astype(BF16)
            suffix = jnp.where(is_first, other[p][i], mine[p][i]).astype(BF16)
            outs[0][:, c] = (local[3 * p][:, o] + product(g[:, c], prefix, 1, 1)).astype(BF16)
            outs[1][:, c] = (local[3 * p + 1][:, o] + product(v[:, c], suffix, 1, 1)).astype(BF16)
            outs[2][:, c] = (local[3 * p + 2][:, o] + product(k[:, c], suffix, 1, 0)).astype(BF16)
            if i % 2 == 1 or i == parts[p] - 1:
                cc = slice((first + i - i % 2) * DH, (first + i + 1) * DH)
                for n in range(3):
                    copy = pltpu.make_async_copy(
                        outs[n].at[:, cc], targets[n].at[:, cc], sems.at[n, first + i]
                    )
                    copy.start()
                    copies.append(copy)
        first += parts[p]
    for copy in copies:
        copy.wait()


def final(core, parts, k, v, g, mine, other, local):
    shape = jax.ShapeDtypeStruct(k.shape, BF16)
    return pl.pallas_call(
        functools.partial(final_kernel, parts),
        in_specs=[SMEM] + [VMEM] * (3 + 5 * len(parts)),
        out_specs=[HBM] * 3,
        out_shape=[shape] * 3,
        scratch_shapes=[pltpu.VMEM(k.shape, BF16)] * 3
        + [pltpu.SemaphoreType.DMA((3, sum(parts)))],
        compiler_params=pltpu.CompilerParams(vmem_limit_bytes=16 << 20),
        name="final",
    )(core, k, v, g, *mine, *other, *local)


def after(values, *events):
    values = tuple(values)
    return lax.optimization_barrier(values + tuple(events))[: len(values)]


def move(value, chips, hops):
    pairs = []
    for a, b in hops:
        pairs += [(2 * a, 2 * b), (2 * (chips - 1 - a) + 1, 2 * (chips - 1 - b) + 1)]
    return lax.ppermute(value, ("seq", "sub"), pairs)


def body(query_in, key_in, value_in, grad_in):
    chips = lax.axis_size("seq")
    core = lax.axis_index("sub").astype(jnp.int32).reshape(1)
    heads = query_in.shape[1] // DH
    parts = (heads // 2, heads - heads // 2)
    swap = [(0, 1), (1, 0)]
    args, give, keep = states(core, parts, query_in, key_in, value_in, grad_in)
    got = [lax.ppermute(x, "sub", swap) for x in give]
    total_a, total_b = (x + y for x, y in zip(keep, got))
    last = chips - 1
    mine_a = arrived_a = move(total_a, chips, [(0, 1)])
    mine_b = arrived_b = move(total_b, chips, [(0, 1), (last - 1, last)])
    local_a = intra(0, parts[0], *after(args, total_a, total_b))
    (arrived_a,) = after((arrived_a,), local_a[0])
    for hop in range(1, last):
        sent_a = total_a + arrived_a
        arrived_a = move(sent_a, chips, [(hop, hop + 1)])
        if hop < last - 1:
            (arrived_b,) = after((arrived_b,), sent_a)
            sent_b = total_b + arrived_b
            if hop == last - 2:
                mine_b = mine_b + move(sent_b, chips, [(hop, last)])
            arrived_b = move(sent_b, chips, [(hop, hop + 1)])
            if hop < last - 2:
                mine_b = mine_b + arrived_b
        if hop < last - 1:
            mine_a = mine_a + arrived_a
    local_b = intra(parts[0], parts[1], *after(args, sent_a))
    arrived_a, arrived_b = after((arrived_a, arrived_b), local_b[0])
    mine_a = mine_a + arrived_a
    mine_b = mine_b + arrived_b
    other_b = lax.ppermute(mine_b + keep[1], "sub", swap)
    other_a = lax.ppermute(mine_a + keep[0], "sub", swap)
    q, k, v, g = args
    return tuple(
        final(core, parts, k, v, g, (mine_a, mine_b), (other_a, other_b), (*local_a, *local_b))
    )


def solution(mesh):
    placed = P(("rep", "seq", "sub"), "head")
    return jax.shard_map(
        body, mesh=mesh, in_specs=(placed,) * 4, out_specs=(placed,) * 3, check_vma=False
    )
```

time: 43.8 us -> 34.3 us (0.78)
  the two profiles are of different devices: /device:TPU:0 before, /device:TPU:31 now
where the time goes in v2:
time: 34.3 us; the launch traced here: 34 us
  starting transfers between devices  18.2 us (53%)
  Pallas kernels  11.1 us (32%)
  waiting for transfers between devices  3.6 us (10%)
  between operations  0.77 us (2%)
  other arithmetic  0.35 us (1%)
    ppermute x1, starting transfers between devices, body(): other_b = lax.ppermute(mine_b + keep[1], 'sub', swap)  11.2 us
    ppermute x6, starting transfers between devices, move(): return lax.ppermute(value, ('seq', 'sub'), pairs)  6.1 us
    pallas_call x2, Pallas kernels, intra(): pl.pallas_call(functools.partial(intra_kernel, first), in_specs=[VMEM] *...  5.99 us
    pallas_call x1, Pallas kernels, states(): pl.pallas_call(states_kernel, in_specs=[SMEM] + [HBM] * 4, out_specs=[VME...  2.72 us
    pallas_call x1, Pallas kernels, final(): pl.pallas_call(functools.partial(final_kernel, parts), in_specs=[SMEM] +...  2.4 us
    ppermute x2, waiting for transfers between devices, body(): got = [lax.ppermute(x, 'sub', swap) for x in give]  1.09 us
    ppermute x1, waiting for transfers between devices, body(): other_b = lax.ppermute(mine_b + keep[1], 'sub', swap)  1.01 us
    ppermute x6, waiting for transfers between devices, move(): return lax.ppermute(value, ('seq', 'sub'), pairs)  0.99 us
  transfers between devices with their start and end apart: 10, of which 4 were waited for; matrix products, arithmetic and copies ran while one was open for 1% of the time, Pallas kernels for 18%

profile of v2, /device:TPU:31, one launch (start us, length us, event | category | flops | bytes accessed | tf_op | source)
XLA Modules:
  0.0 34.0 jit_solution(14565609616784732367)
XLA Ops:
  0.6 2.7 %states.1 = (bf16[512,1024]{1,0:T(8,128)(2,1)S(1)}, bf16[512,1024]{1,0:T(8,128)(2,1)S(1)}, bf16[512,1024]{1,0:T(8,128)(2,1)S(1)}, bf16[512,1024]{1,0:T(8,128)(2,...) custom-call(s32[1]{0:T(128)} %bitcast.core, ...), custom_call_target="tpu_custom_call" | custom-call | tf_op jit(solution)/shard_map/states/pallas_call | solution.py:63
  3.4 0.7 %collective-permute-start = (f32[4,128,128]{2,1,0:T(8,128)S(1)}, f32[4,128,128]{2,1,0:T(8,128)S(1)}, u32[]{:S(2)}, u32[]{:S(2)}) collective-permute-start(f32[4,128,128]{2,1,0:T(8,128)S(1)} %get-tuple-element.33), channel_id=1, source_target_pairs={{0,1},{1,0},{2,3},{3,2},{4,5},{5,4},{6,7},{7,6},{8,9},{9,8},{10,11... | collective-permute-start | bytes 786440 | tf_op jit(solution)/shard_map/ppermute | solution.py:162
  4.1 0.1 collective-permute-start.2
  4.2 1.1 %collective-permute-done = f32[4,128,128]{2,1,0:T(8,128)S(1)} collective-permute-done((f32[4,128,128]{2,1,0:T(8,128)S(1)}, f32[4,128,128]{2,1,0:T(8,128)S(1)}, u32[]{:S(2)}, u32[]{:S(2)}) %collective-permute-start) | collective-permute-done | bytes 262176 | tf_op jit(solution)/shard_map/ppermute | solution.py:162
  5.3 2.1 %collective-permute-start.1 = (f32[4,128,128]{2,1,0:T(8,128)S(1)}, f32[4,128,128]{2,1,0:T(8,128)S(1)}, u32[]{:S(2)}, u32[]{:S(2)}) collective-permute-start(f32[4,128,128]{2,1,0:T(8,128)S(1)} %add.33), channel_id=1, source_target_pairs={{0,4},{13,9},{2,6},{15,11},{16,20},{29,25},{18,22},{31,27}} | collective-permute-start | bytes 786440 | tf_op jit(solution)/shard_map/ppermute | solution.py:152
  7.4 0.0 collective-permute-done.2
  7.5 1.3 %collective-permute-start.5 = (f32[4,128,128]{2,1,0:T(8,128)S(1)}, f32[4,128,128]{2,1,0:T(8,128)S(1)}, u32[]{:S(2)}, u32[]{:S(2)}) collective-permute-start(f32[4,128,128]{2,1,0:T(8,128)S(1)} %add.34), channel_id=1, source_target_pairs={{0,4},{13,9},{8,12},{5,1},{2,6},{15,11},{10,14},{7,3},{16,20},{29,... | collective-permute-start | bytes 786440 | tf_op jit(solution)/shard_map/ppermute | solution.py:152
  8.8 3.0 %intra.2 = (f32[512,512]{1,0:T(8,128)S(1)}, f32[512,512]{1,0:T(8,128)S(1)}, f32[512,512]{1,0:T(8,128)S(1)}) custom-call(bf16[512,1024]{1,0:T(8,128)(2,1)S(1)} %get-tuple-element.44.q, bf16[512,1024]{1,0:T(8,128)(2,1)S(1)} %get-tuple-element.45.k, bf16[512,1024]{1,0:T(8,128)(2,1)S(1)} %get-tuple-element.46.v, bf16[512,1024]{1,0:T(8,128)(2,1)S(1)} %get-tuple-element.47.g), custom_call_target="tpu_custom_call" | custom-call | tf_op jit(solution)/shard_map/intra/pallas_call | solution.py:90
  11.8 0.0 collective-permute-done.1
  11.8 0.7 %collective-permute-start.3 = (f32[4,128,128]{2,1,0:T(8,128)S(1)}, f32[4,128,128]{2,1,0:T(8,128)S(1)}, u32[]{:S(2)}, u32[]{:S(2)}) collective-permute-start(f32[4,128,128]{2,1,0:T(8,128)S(1)} %add.35), channel_id=1, source_target_pairs={{4,8},{9,5},{6,10},{11,7},{20,24},{25,21},{22,26},{27,23}} | collective-permute-start | bytes 786440 | tf_op jit(solution)/shard_map/ppermute | solution.py:152
  12.5 1.0 %collective-permute-done.5 = f32[4,128,128]{2,1,0:T(8,128)S(1)} collective-permute-done((f32[4,128,128]{2,1,0:T(8,128)S(1)}, f32[4,128,128]{2,1,0:T(8,128)S(1)}, u32[]{:S(2)}, u32[]{:S(2)}) %collective-permute-start.5) | collective-permute-done | bytes 262176 | tf_op jit(solution)/shard_map/ppermute | solution.py:152
  13.6 0.7 %collective-permute-start.6 = (f32[4,128,128]{2,1,0:T(8,128)S(1)}, f32[4,128,128]{2,1,0:T(8,128)S(1)}, u32[]{:S(2)}, u32[]{:S(2)}) collective-permute-start(f32[4,128,128]{2,1,0:T(8,128)S(1)} %add.38), channel_id=1, source_target_pairs={{4,8},{9,5},{6,10},{11,7},{20,24},{25,21},{22,26},{27,23}} | collective-permute-start | bytes 786440 | tf_op jit(solution)/shard_map/ppermute | solution.py:152
  14.2 0.0 collective-permute-done.3
  14.3 0.7 %collective-permute-start.4 = (f32[4,128,128]{2,1,0:T(8,128)S(1)}, f32[4,128,128]{2,1,0:T(8,128)S(1)}, u32[]{:S(2)}, u32[]{:S(2)}) collective-permute-start(f32[4,128,128]{2,1,0:T(8,128)S(1)} %add.37), channel_id=1, source_target_pairs={{8,12},{5,1},{10,14},{7,3},{24,28},{21,17},{26,30},{23,19}} | collective-permute-start | bytes 786440 | tf_op jit(solution)/shard_map/ppermute | solution.py:152
  15.0 0.7 %collective-permute-start.7 = (f32[4,128,128]{2,1,0:T(8,128)S(1)}, f32[4,128,128]{2,1,0:T(8,128)S(1)}, u32[]{:S(2)}, u32[]{:S(2)}) collective-permute-start(f32[4,128,128]{2,1,0:T(8,128)S(1)} %add.38), channel_id=1, source_target_pairs={{4,12},{9,1},{6,14},{11,3},{20,28},{25,17},{22,30},{27,19}} | collective-permute-start | bytes 786440 | tf_op jit(solution)/shard_map/ppermute | solution.py:152
  15.7 3.0 %intra.3 = (f32[512,512]{1,0:T(8,128)S(1)}, f32[512,512]{1,0:T(8,128)S(1)}, f32[512,512]{1,0:T(8,128)S(1)}) custom-call(bf16[512,1024]{1,0:T(8,128)(2,1)S(1)} %get-tuple-element.44.q, bf16[512,1024]{1,0:T(8,128)(2,1)S(1)} %get-tuple-element.45.k, bf16[512,1024]{1,0:T(8,128)(2,1)S(1)} %get-tuple-element.46.v, bf16[512,1024]{1,0:T(8,128)(2,1)S(1)} %get-tuple-element.47.g), custom_call_target="tpu_custom_call" | custom-call | tf_op jit(solution)/shard_map/intra/pallas_call | solution.py:90
  18.7 0.0 collective-permute-done.7
  18.7 0.1 fusion
  18.8 11.2 %collective-permute-start.9 = (f32[4,128,128]{2,1,0:T(8,128)S(1)}, f32[4,128,128]{2,1,0:T(8,128)S(1)}, u32[]{:S(2)}, u32[]{:S(2)}) collective-permute-start(f32[4,128,128]{2,1,0:T(8,128)S(1)} %get-tuple-element.55), channel_id=1, source_target_pairs={{0,1},{1,0},{2,3},{3,2},{4,5},{5,4},{6,7},{7,6},{8,9},{9,8},{10,11... | collective-permute-start | bytes 786440 | tf_op jit(solution)/shard_map/ppermute | solution.py:186
  30.0 0.1 fusion.1
  30.1 0.1 collective-permute-start.8
  30.1 1.0 %collective-permute-done.9.rest_3_ = f32[4,128,128]{2,1,0:T(8,128)S(1)} collective-permute-done((f32[4,128,128]{2,1,0:T(8,128)S(1)}, f32[4,128,128]{2,1,0:T(8,128)S(1)}, u32[]{:S(2)}, u32[]{:S(2)}) %collective-permute-start.9) | collective-permute-done | bytes 262176 | tf_op jit(solution)/shard_map/ppermute | solution.py:186
  31.1 0.5 %collective-permute-done.8.rest_2_ = f32[4,128,128]{2,1,0:T(8,128)S(1)} collective-permute-done((f32[4,128,128]{2,1,0:T(8,128)S(1)}, f32[4,128,128]{2,1,0:T(8,128)S(1)}, u32[]{:S(2)}, u32[]{:S(2)}) %collective-permute-start.8) | collective-permute-done | bytes 262176 | tf_op jit(solution)/shard_map/ppermute | solution.py:187
  31.7 2.4 %final.1 = (bf16[512,1024]{1,0:T(8,128)(2,1)}, bf16[512,1024]{1,0:T(8,128)(2,1)}, bf16[512,1024]{1,0:T(8,128)(2,1)}) custom-call(s32[1]{0:T(128)} %bitcast.core, bf16[512,1024]{1,0:T(8,128)(2,1)S(1)} %get-tuple-element.45.k, bf16[512,1024]{1,0:T(8,128)(2,1)S(1)} %get-tuple-element.46.v, bf16[512,1024]{1,0:T(8,128)(2,1)S(1)} %get-tuple-element.47.g, ...), custom_call_target="tpu_custom_call" | custom-call | tf_op jit(solution)/shard_map/final/pallas_call | solution.py:131
  (7 shorter events, 0.2 us)
Async XLA Ops:
  3.4 1.9 %collective-permute-start = (f32[4,128,128]{2,1,0:T(8,128)S(1)}, f32[4,128,128]{2,1,0:T(8,128)S(1)}, u32[]{:S(2)}, u32[]{:S(2)}) collective-permute-start(f32[4,128,128]{2,1,0:T(8,128)S(1)} %get-tuple-element.33), channel_id=1, source_target_pairs={{0,1},{1,0},{2,3},{3,2},{4,5},{5,4},{6,7},{7,6},{8,9},{9,8},{10,11... | collective-permute-start | bytes 786440 | tf_op jit(solution)/shard_map/ppermute | solution.py:162
  4.1 3.3 %collective-permute-start.2 = (f32[4,128,128]{2,1,0:T(8,128)S(1)}, f32[4,128,128]{2,1,0:T(8,128)S(1)}, u32[]{:S(2)}, u32[]{:S(2)}) collective-permute-start(f32[4,128,128]{2,1,0:T(8,128)S(1)} %get-tuple-element.36), channel_id=1, source_target_pairs={{0,1},{1,0},{2,3},{3,2},{4,5},{5,4},{6,7},{7,6},{8,9},{9,8},{10,11... | collective-permute-start | bytes 786440 | tf_op jit(solution)/shard_map/ppermute | solution.py:162
  5.3 6.5 %collective-permute-start.1 = (f32[4,128,128]{2,1,0:T(8,128)S(1)}, f32[4,128,128]{2,1,0:T(8,128)S(1)}, u32[]{:S(2)}, u32[]{:S(2)}) collective-permute-start(f32[4,128,128]{2,1,0:T(8,128)S(1)} %add.33), channel_id=1, source_target_pairs={{0,4},{13,9},{2,6},{15,11},{16,20},{29,25},{18,22},{31,27}} | collective-permute-start | bytes 786440 | tf_op jit(solution)/shard_map/ppermute | solution.py:152
  7.5 6.0 %collective-permute-start.5 = (f32[4,128,128]{2,1,0:T(8,128)S(1)}, f32[4,128,128]{2,1,0:T(8,128)S(1)}, u32[]{:S(2)}, u32[]{:S(2)}) collective-permute-start(f32[4,128,128]{2,1,0:T(8,128)S(1)} %add.34), channel_id=1, source_target_pairs={{0,4},{13,9},{8,12},{5,1},{2,6},{15,11},{10,14},{7,3},{16,20},{29,... | collective-permute-start | bytes 786440 | tf_op jit(solution)/shard_map/ppermute | solution.py:152
  11.8 2.4 %collective-permute-start.3 = (f32[4,128,128]{2,1,0:T(8,128)S(1)}, f32[4,128,128]{2,1,0:T(8,128)S(1)}, u32[]{:S(2)}, u32[]{:S(2)}) collective-permute-start(f32[4,128,128]{2,1,0:T(8,128)S(1)} %add.35), channel_id=1, source_target_pairs={{4,8},{9,5},{6,10},{11,7},{20,24},{25,21},{22,26},{27,23}} | collective-permute-start | bytes 786440 | tf_op jit(solution)/shard_map/ppermute | solution.py:152
  13.6 5.1 %collective-permute-start.6 = (f32[4,128,128]{2,1,0:T(8,128)S(1)}, f32[4,128,128]{2,1,0:T(8,128)S(1)}, u32[]{:S(2)}, u32[]{:S(2)}) collective-permute-start(f32[4,128,128]{2,1,0:T(8,128)S(1)} %add.38), channel_id=1, source_target_pairs={{4,8},{9,5},{6,10},{11,7},{20,24},{25,21},{22,26},{27,23}} | collective-permute-start | bytes 786440 | tf_op jit(solution)/shard_map/ppermute | solution.py:152
  14.3 4.4 %collective-permute-start.4 = (f32[4,128,128]{2,1,0:T(8,128)S(1)}, f32[4,128,128]{2,1,0:T(8,128)S(1)}, u32[]{:S(2)}, u32[]{:S(2)}) collective-permute-start(f32[4,128,128]{2,1,0:T(8,128)S(1)} %add.37), channel_id=1, source_target_pairs={{8,12},{5,1},{10,14},{7,3},{24,28},{21,17},{26,30},{23,19}} | collective-permute-start | bytes 786440 | tf_op jit(solution)/shard_map/ppermute | solution.py:152
  15.0 3.7 %collective-permute-start.7 = (f32[4,128,128]{2,1,0:T(8,128)S(1)}, f32[4,128,128]{2,1,0:T(8,128)S(1)}, u32[]{:S(2)}, u32[]{:S(2)}) collective-permute-start(f32[4,128,128]{2,1,0:T(8,128)S(1)} %add.38), channel_id=1, source_target_pairs={{4,12},{9,1},{6,14},{11,3},{20,28},{25,17},{22,30},{27,19}} | collective-permute-start | bytes 786440 | tf_op jit(solution)/shard_map/ppermute | solution.py:152
  18.8 12.4 %collective-permute-start.9 = (f32[4,128,128]{2,1,0:T(8,128)S(1)}, f32[4,128,128]{2,1,0:T(8,128)S(1)}, u32[]{:S(2)}, u32[]{:S(2)}) collective-permute-start(f32[4,128,128]{2,1,0:T(8,128)S(1)} %get-tuple-element.55), channel_id=1, source_target_pairs={{0,1},{1,0},{2,3},{3,2},{4,5},{5,4},{6,7},{7,6},{8,9},{9,8},{10,11... | collective-permute-start | bytes 786440 | tf_op jit(solution)/shard_map/ppermute | solution.py:186
  30.1 1.6 %collective-permute-start.8 = (f32[4,128,128]{2,1,0:T(8,128)S(1)}, f32[4,128,128]{2,1,0:T(8,128)S(1)}, u32[]{:S(2)}, u32[]{:S(2)}) collective-permute-start(f32[4,128,128]{2,1,0:T(8,128)S(1)} %get-tuple-element.57), channel_id=1, source_target_pairs={{0,1},{1,0},{2,3},{3,2},{4,5},{5,4},{6,7},{7,6},{8,9},{9,8},{10,11... | collective-permute-start | bytes 786440 | tf_op jit(solution)/shard_map/ppermute | solution.py:187

commit v3 on v2

v3 whole, which is shorter than its diff:
```python
import functools

import jax
import jax.numpy as jnp
from jax import lax
from jax.experimental import pallas as pl
from jax.experimental.pallas import tpu as pltpu
from jax.sharding import PartitionSpec as P

DH = 128
LITTLE = pl.CostEstimate(flops=1, transcendentals=0, bytes_accessed=1)
PIECES = (1, 2, 5)
F32 = jnp.float32
BF16 = jnp.bfloat16
VMEM = pl.BlockSpec(memory_space=pltpu.VMEM)
HBM = pl.BlockSpec(memory_space=pltpu.HBM)
SMEM = pl.BlockSpec(memory_space=pltpu.SMEM)


def product(left, right, left_axis, right_axis):
    return lax.dot_general(
        left, right, (((left_axis,), (right_axis,)), ((), ())), preferred_element_type=F32
    )


def head_columns(head):
    return slice(head * DH, (head + 1) * DH)


def states_kernel(aliased, place, q_hbm, k_hbm, v_hbm, g_hbm, *rest):
    rest = rest[aliased:]
    q, k, v, g = rest[:4]
    parts = (len(rest) - 5) // 2
    keep, give, sems = rest[4 : 4 + parts], rest[4 + parts : 4 + 2 * parts], rest[-1]
    copies = [
        pltpu.make_async_copy(source, target, sems.at[i])
        for i, (source, target) in enumerate(zip((q_hbm, k_hbm, v_hbm, g_hbm), (q, k, v, g)))
    ]
    is_first = place[0] == 0

    def state(left, right, outs):
        h = 0
        for out in outs:
            for i in range(out.shape[0]):
                c = head_columns(h)
                out[i] = product(left[:, c], right[:, c], 0, 0)
                h += 1

    @pl.when(place[1] == 1)
    def _():
        for c in (0, 3, 1, 2):
            copies[c].start()
        for left, right, give_first in ((0, 3, True), (1, 2, False)):
            copies[left].wait()
            copies[right].wait()
            pair = (q, k, v, g)[left], (q, k, v, g)[right]

            @pl.when(is_first)
            def _():
                state(*pair, give if give_first else keep)

            @pl.when(jnp.logical_not(is_first))
            def _():
                state(*pair, keep if give_first else give)


def states(core, active, parts, args, filled=()):
    place = jnp.stack([core, active.astype(jnp.int32)])
    outs = [pltpu.VMEM((n, DH, DH), F32) for n in parts]
    result = pl.pallas_call(
        functools.partial(states_kernel, len(filled)),
        in_specs=[SMEM] + [HBM] * 4 + [VMEM] * len(filled),
        out_specs=[VMEM] * (4 + 2 * len(outs)),
        out_shape=[pltpu.VMEM(args[0].shape, BF16)] * 4 + outs + outs,
        scratch_shapes=[pltpu.SemaphoreType.DMA((4,))],
        input_output_aliases={5 + i: i for i in range(len(filled))},
        compiler_params=pltpu.CompilerParams(vmem_limit_bytes=8 << 20),
        name="states",
        cost_estimate=LITTLE,
    )(place, *[pltpu.with_memory_space_constraint(x, pltpu.HBM) for x in args], *filled)
    return result[: 4 + len(parts)], result[4 + len(parts) :]


def intra_kernel(first, q, k, v, g, dq, dk, dv):
    rows = q.shape[0]
    row = lax.broadcasted_iota(jnp.int32, (rows, rows), 0)
    col = lax.broadcasted_iota(jnp.int32, (rows, rows), 1)
    for h in range(dq.shape[1] // DH):
        c, o = head_columns(first + h), head_columns(h)
        qh, kh, vh, gh = q[:, c], k[:, c], v[:, c], g[:, c]
        grad_scores = jnp.where(row >= col, product(gh, vh, 1, 1), 0.0).astype(BF16)
        dq[:, o] = product(grad_scores, kh, 1, 0)
        dk[:, o] = product(grad_scores, qh, 0, 0)
        attn_scores = jnp.where(row <= col, product(kh, qh, 1, 1), 0.0).astype(BF16)
        dv[:, o] = product(attn_scores, gh, 1, 0)


def intra(first, heads, q, k, v, g):
    return pl.pallas_call(
        functools.partial(intra_kernel, first),
        in_specs=[VMEM] * 4,
        out_specs=[VMEM] * 3,
        out_shape=[pltpu.VMEM((q.shape[0], heads * DH), F32)] * 3,
        compiler_params=pltpu.CompilerParams(vmem_limit_bytes=16 << 20),
        name="intra",
        cost_estimate=LITTLE,
    )(q, k, v, g)


def final_kernel(parts, pieces, core, k, v, g, *rest):
    count = len(parts)
    mine, other, rest = rest[:count], rest[count : 2 * count], rest[2 * count :]
    local, rest = rest[: 3 * len(pieces)], rest[3 * len(pieces) :]
    (targets, outs, sems) = rest[:3], rest[3:6], rest[6]
    is_first = core[0] == 0
    of_part = [(p, i) for p, n in enumerate(parts) for i in range(n)]
    of_piece = [(p, i) for p, n in enumerate(pieces) for i in range(n)]
    heads = len(of_part)
    copies = []
    for h in range(heads):
        (part, i), (piece, j) = of_part[h], of_piece[h]
        c, o = head_columns(h), head_columns(j)
        prefix = jnp.where(is_first, mine[part][i], other[part][i]).astype(BF16)
        suffix = jnp.where(is_first, other[part][i], mine[part][i]).astype(BF16)
        local_q, local_k, local_v = (x[:, o] for x in local[3 * piece : 3 * piece + 3])
        outs[0][:, c] = (local_q + product(g[:, c], prefix, 1, 1)).astype(BF16)
        outs[1][:, c] = (local_k + product(v[:, c], suffix, 1, 1)).astype(BF16)
        outs[2][:, c] = (local_v + product(k[:, c], suffix, 1, 0)).astype(BF16)
        if h % 2 == 1 or h == heads - 1:
            cc = slice((h - h % 2) * DH, (h + 1) * DH)
            for n in range(3):
                copy = pltpu.make_async_copy(
                    outs[n].at[:, cc], targets[n].at[:, cc], sems.at[n, h // 2]
                )
                copy.start()
                copies.append(copy)
    for copy in copies:
        copy.wait()


def final(core, parts, pieces, k, v, g, mine, other, local):
    shape = jax.ShapeDtypeStruct(k.shape, BF16)
    return pl.pallas_call(
        functools.partial(final_kernel, parts, pieces),
        in_specs=[SMEM] + [VMEM] * (3 + 2 * len(parts) + 3 * len(pieces)),
        out_specs=[HBM] * 3,
        out_shape=[shape] * 3,
        scratch_shapes=[pltpu.VMEM(k.shape, BF16)] * 3
        + [pltpu.SemaphoreType.DMA((3, (sum(parts) + 1) // 2))],
        compiler_params=pltpu.CompilerParams(vmem_limit_bytes=16 << 20),
        name="final",
        cost_estimate=LITTLE,
    )(core.reshape(1), k, v, g, *mine, *other, *[x for piece in local for x in piece])


def after(values, *events):
    values = tuple(values)
    return lax.optimization_barrier(values + tuple(events))[: len(values)]


def move(value, chips, hops):
    pairs = []
    for a, b in hops:
        pairs += [(2 * a, 2 * b), (2 * (chips - 1 - a) + 1, 2 * (chips - 1 - b) + 1)]
    return lax.ppermute(value, ("seq", "sub"), pairs)


def swap(value, chips=None):
    if chips is None:
        return lax.ppermute(value, "sub", [(0, 1), (1, 0)])
    pairs = [pair for c in chips for pair in ((2 * c, 2 * c + 1), (2 * c + 1, 2 * c))]
    return lax.ppermute(value, ("seq", "sub"), pairs)


def body(*args):
    chips = lax.axis_size("seq")
    last = chips - 1
    ends, middle = (0, last), range(1, last)
    core = lax.axis_index("sub").astype(jnp.int32)
    chip = lax.axis_index("seq")
    at_end = jnp.logical_or(chip == 0, chip == last)
    heads = args[0].shape[1] // DH
    parts = (heads // 2, heads - heads // 2)
    pieces = PIECES if heads == 8 else (1, 1, heads - 2)

    filled, give = states(core, at_end, parts, args)
    got_a, got_b = (swap(x, ends) for x in give)
    first_a, first_b = filled[4] + got_a, filled[5] + got_b
    arrived_a, arrived_b = (move(x, chips, [(0, 1)]) for x in (first_a, first_b))
    filled, give = states(
        core, jnp.logical_not(at_end), parts, args, after(filled, first_a, first_b)
    )
    args, keep = filled[:4], filled[4:]
    total_a, total_b = (x + y + swap(z, middle) for x, y, z in zip(keep, (got_a, got_b), give))
    mine_a, mine_b = arrived_a, arrived_b
    carried_b = move(total_b, chips, [(last - 1, last)])
    local = [intra(0, pieces[0], *after(args, total_a, total_b))]
    (arrived_a,) = after((arrived_a,), local[0][0])
    (arrived_b,) = after((arrived_b,), carried_b)
    mine_b = mine_b + carried_b
    for hop in range(1, last):
        sent_a = total_a + arrived_a
        arrived_a = move(sent_a, chips, [(hop, hop + 1)])
        if hop < last - 1:
            mine_a = mine_a + arrived_a
            if hop == last - 2:
                local.append(intra(pieces[0], pieces[1], *after(args, sent_a)))
                (arrived_b,) = after((arrived_b,), local[1][0])
            else:
                (arrived_b,) = after((arrived_b,), sent_a)
            sent_b = total_b + arrived_b
            if hop == last - 2:
                mine_b = mine_b + move(sent_b, chips, [(hop, last)])
            arrived_b = move(sent_b, chips, [(hop, hop + 1)])
            if hop < last - 2:
                mine_b = mine_b + arrived_b
    local.append(intra(sum(pieces[:2]), pieces[2], *after(args, sent_a)))
    arrived_a, arrived_b = after((arrived_a, arrived_b), local[2][0])
    mine_a = mine_a + arrived_a
    mine_b = mine_b + arrived_b
    other_b = swap(mine_b + keep[1])
    other_a = swap(mine_a + keep[0])
    q, k, v, g = args
    return tuple(final(core, parts, pieces, k, v, g, (mine_a, mine_b), (other_a, other_b), local))


def solution(mesh):
    placed = P(("rep", "seq", "sub"), "head")
    return jax.shard_map(
        body, mesh=mesh, in_specs=(placed,) * 4, out_specs=(placed,) * 3, check_vma=False
    )
```

time: 34.3 us -> 43.3 us (1.26)
  the two profiles are of different devices: /device:TPU:31 before, /device:TPU:0 now
where the time goes in v3:
time: 43.3 us; the launch traced here: 42.5 us
  starting transfers between devices  24.5 us (57%)
  Pallas kernels  12.3 us (28%)
  waiting for transfers between devices  4.17 us (10%)
  between operations  1.01 us (2%)
  other arithmetic  0.52 us (1%)
    ppermute x2, starting transfers between devices, swap(): return lax.ppermute(value, 'sub', [(0, 1), (1, 0)])  10.4 us
    ppermute x7, starting transfers between devices, move(): return lax.ppermute(value, ('seq', 'sub'), pairs)  8.42 us
    pallas_call x3, Pallas kernels, intra(): pl.pallas_call(functools.partial(intra_kernel, first), in_specs=[VMEM] *...  6.24 us
    ppermute x4, starting transfers between devices, swap(): return lax.ppermute(value, ('seq', 'sub'), pairs)  5.68 us
    pallas_call x2, Pallas kernels, states(): pl.pallas_call(functools.partial(states_kernel, len(filled)), in_specs=[S...  3.86 us
    pallas_call x1, Pallas kernels, final(): pl.pallas_call(functools.partial(final_kernel, parts, pieces), in_specs=[...  2.2 us
    ppermute x2, waiting for transfers between devices, swap(): return lax.ppermute(value, 'sub', [(0, 1), (1, 0)])  1.52 us
    ppermute x4, waiting for transfers between devices, swap(): return lax.ppermute(value, ('seq', 'sub'), pairs)  1.42 us
  transfers between devices with their start and end apart: 13, of which 5 were waited for; matrix products, arithmetic and copies ran while one was open for 1% of the time, Pallas kernels for 15%

profile of v3, /device:TPU:0, one launch (start us, length us, event | category | flops | bytes accessed | tf_op | source)
XLA Modules:
  0.0 42.5 jit_solution(3496105128647326676)
XLA Ops:
  0.7 3.3 %states.2 = (bf16[512,1024]{1,0:T(8,128)(2,1)S(1)}, bf16[512,1024]{1,0:T(8,128)(2,1)S(1)}, bf16[512,1024]{1,0:T(8,128)(2,1)S(1)}, bf16[512,1024]{1,0:T(8,128)(2,...) custom-call(s32[2]{0:T(128)S(1)} %get-tuple-element.104.place, ...), custom_call_target="tpu_custom_call" | custom-call | flops 1 | bytes 1 | tf_op jit(solution)/shard_map/states/pallas_call | solution.py:70
  4.0 2.4 %collective-permute-start = (f32[4,128,128]{2,1,0:T(8,128)S(1)}, f32[4,128,128]{2,1,0:T(8,128)S(1)}, u32[]{:S(2)}, u32[]{:S(2)}) collective-permute-start(f32[4,128,128]{2,1,0:T(8,128)S(1)} %get-tuple-element.57), channel_id=1, source_target_pairs={{0,1},{1,0},{12,13},{13,12},{2,3},{3,2},{14,15},{15,14},{16,17},{1... | collective-permute-start | bytes 786440 | tf_op jit(solution)/shard_map/ppermute | solution.py:172
  6.4 2.0 %collective-permute-start.1 = (f32[4,128,128]{2,1,0:T(8,128)S(1)}, f32[4,128,128]{2,1,0:T(8,128)S(1)}, u32[]{:S(2)}, u32[]{:S(2)}) collective-permute-start(f32[4,128,128]{2,1,0:T(8,128)S(1)} %get-tuple-element.58), channel_id=1, source_target_pairs={{0,1},{1,0},{12,13},{13,12},{2,3},{3,2},{14,15},{15,14},{16,17},{1... | collective-permute-start | bytes 786440 | tf_op jit(solution)/shard_map/ppermute | solution.py:172
  8.4 1.4 %collective-permute-done.1 = f32[4,128,128]{2,1,0:T(8,128)S(1)} collective-permute-done((f32[4,128,128]{2,1,0:T(8,128)S(1)}, f32[4,128,128]{2,1,0:T(8,128)S(1)}, u32[]{:S(2)}, u32[]{:S(2)}) %collective-permute-start.1) | collective-permute-done | bytes 262176 | tf_op jit(solution)/shard_map/ppermute | solution.py:172
  9.8 0.6 %states.3 = (bf16[512,1024]{1,0:T(8,128)(2,1)S(1)}, bf16[512,1024]{1,0:T(8,128)(2,1)S(1)}, bf16[512,1024]{1,0:T(8,128)(2,1)S(1)}, bf16[512,1024]{1,0:T(8,128)(2,...) custom-call(s32[2]{0:T(128)S(1)} %get-tuple-element.103.place, ...), custom_call_target="tpu_custom_call", output_to_operand_aliasing={{0}: (5, {}), {1}: (6, {}), {2}: (7, {}), {3}: (8, {}), {4}... | custom-call | flops 1 | bytes 1 | tf_op jit(solution)/shard_map/states/pallas_call | solution.py:70
  10.4 0.7 %collective-permute-start.4 = (f32[4,128,128]{2,1,0:T(8,128)S(1)}, f32[4,128,128]{2,1,0:T(8,128)S(1)}, u32[]{:S(2)}, u32[]{:S(2)}) collective-permute-start(f32[4,128,128]{2,1,0:T(8,128)S(1)} %get-tuple-element.72), channel_id=1, source_target_pairs={{4,5},{5,4},{8,9},{9,8},{6,7},{7,6},{10,11},{11,10},{20,21},{21,20... | collective-permute-start | bytes 786440 | tf_op jit(solution)/shard_map/ppermute | solution.py:172
  11.1 0.7 %collective-permute-start.3 = (f32[4,128,128]{2,1,0:T(8,128)S(1)}, f32[4,128,128]{2,1,0:T(8,128)S(1)}, u32[]{:S(2)}, u32[]{:S(2)}) collective-permute-start(f32[4,128,128]{2,1,0:T(8,128)S(1)} %get-tuple-element.69), channel_id=1, source_target_pairs={{4,5},{5,4},{8,9},{9,8},{6,7},{7,6},{10,11},{11,10},{20,21},{21,20... | collective-permute-start | bytes 786440 | tf_op jit(solution)/shard_map/ppermute | solution.py:172
  11.8 3.6 %collective-permute-start.2 = (f32[4,128,128]{2,1,0:T(8,128)S(1)}, f32[4,128,128]{2,1,0:T(8,128)S(1)}, u32[]{:S(2)}, u32[]{:S(2)}) collective-permute-start(f32[4,128,128]{2,1,0:T(8,128)S(1)} %add.48), channel_id=1, source_target_pairs={{0,4},{13,9},{2,6},{15,11},{16,20},{29,25},{18,22},{31,27}} | collective-permute-start | bytes 786440 | tf_op jit(solution)/shard_map/ppermute | solution.py:165
  15.4 1.3 %collective-permute-start.7 = (f32[4,128,128]{2,1,0:T(8,128)S(1)}, f32[4,128,128]{2,1,0:T(8,128)S(1)}, u32[]{:S(2)}, u32[]{:S(2)}) collective-permute-start(f32[4,128,128]{2,1,0:T(8,128)S(1)} %add.49), channel_id=1, source_target_pairs={{0,4},{13,9},{2,6},{15,11},{16,20},{29,25},{18,22},{31,27}} | collective-permute-start | bytes 786440 | tf_op jit(solution)/shard_map/ppermute | solution.py:165
  16.7 0.7 %collective-permute-start.8 = (f32[4,128,128]{2,1,0:T(8,128)S(1)}, f32[4,128,128]{2,1,0:T(8,128)S(1)}, u32[]{:S(2)}, u32[]{:S(2)}) collective-permute-start(f32[4,128,128]{2,1,0:T(8,128)S(1)} %add_add_fusion.2), channel_id=1, source_target_pairs={{8,12},{5,1},{10,14},{7,3},{24,28},{21,17},{26,30},{23,19}} | collective-permute-start | bytes 786440 | tf_op jit(solution)/shard_map/ppermute | solution.py:165
  17.5 0.9 %intra.3 = (f32[512,128]{1,0:T(8,128)S(1)}, f32[512,128]{1,0:T(8,128)S(1)}, f32[512,128]{1,0:T(8,128)S(1)}) custom-call(bf16[512,1024]{1,0:T(8,128)(2,1)S(1)} %get-tuple-element.86.q, bf16[512,1024]{1,0:T(8,128)(2,1)S(1)} %get-tuple-element.87.k, bf16[512,1024]{1,0:T(8,128)(2,1)S(1)} %get-tuple-element.88.v, bf16[512,1024]{1,0:T(8,128)(2,1)S(1)} %get-tuple-element.89.g), custom_call_target="tpu_custom_call" | custom-call | flops 1 | bytes 1 | tf_op jit(solution)/shard_map/intra/pallas_call | solution.py:99
  18.4 0.8 %collective-permute-done.2 = f32[4,128,128]{2,1,0:T(8,128)S(1)} collective-permute-done((f32[4,128,128]{2,1,0:T(8,128)S(1)}, f32[4,128,128]{2,1,0:T(8,128)S(1)}, u32[]{:S(2)}, u32[]{:S(2)}) %collective-permute-start.2) | collective-permute-done | bytes 262176 | tf_op jit(solution)/shard_map/ppermute | solution.py:165
  19.3 0.7 %collective-permute-start.5 = (f32[4,128,128]{2,1,0:T(8,128)S(1)}, f32[4,128,128]{2,1,0:T(8,128)S(1)}, u32[]{:S(2)}, u32[]{:S(2)}) collective-permute-start(f32[4,128,128]{2,1,0:T(8,128)S(1)} %add.54), channel_id=1, source_target_pairs={{4,8},{9,5},{6,10},{11,7},{20,24},{25,21},{22,26},{27,23}} | collective-permute-start | bytes 786440 | tf_op jit(solution)/shard_map/ppermute | solution.py:165
  20.0 1.6 %intra.4 = (f32[512,256]{1,0:T(8,128)S(1)}, f32[512,256]{1,0:T(8,128)S(1)}, f32[512,256]{1,0:T(8,128)S(1)}) custom-call(bf16[512,1024]{1,0:T(8,128)(2,1)S(1)} %get-tuple-element.86.q, bf16[512,1024]{1,0:T(8,128)(2,1)S(1)} %get-tuple-element.87.k, bf16[512,1024]{1,0:T(8,128)(2,1)S(1)} %get-tuple-element.88.v, bf16[512,1024]{1,0:T(8,128)(2,1)S(1)} %get-tuple-element.89.g), custom_call_target="tpu_custom_call" | custom-call | flops 1 | bytes 1 | tf_op jit(solution)/shard_map/intra/pallas_call | solution.py:99
  21.6 0.4 %collective-permute-done.7 = f32[4,128,128]{2,1,0:T(8,128)S(1)} collective-permute-done((f32[4,128,128]{2,1,0:T(8,128)S(1)}, f32[4,128,128]{2,1,0:T(8,128)S(1)}, u32[]{:S(2)}, u32[]{:S(2)}) %collective-permute-start.7) | collective-permute-done | bytes 262176 | tf_op jit(solution)/shard_map/ppermute | solution.py:165
  22.1 0.7 %collective-permute-start.6 = (f32[4,128,128]{2,1,0:T(8,128)S(1)}, f32[4,128,128]{2,1,0:T(8,128)S(1)}, u32[]{:S(2)}, u32[]{:S(2)}) collective-permute-start(f32[4,128,128]{2,1,0:T(8,128)S(1)} %add.56), channel_id=1, source_target_pairs={{8,12},{5,1},{10,14},{7,3},{24,28},{21,17},{26,30},{23,19}} | collective-permute-start | bytes 786440 | tf_op jit(solution)/shard_map/ppermute | solution.py:165
  22.8 0.7 %collective-permute-start.9 = (f32[4,128,128]{2,1,0:T(8,128)S(1)}, f32[4,128,128]{2,1,0:T(8,128)S(1)}, u32[]{:S(2)}, u32[]{:S(2)}) collective-permute-start(f32[4,128,128]{2,1,0:T(8,128)S(1)} %add.57), channel_id=1, source_target_pairs={{4,8},{9,5},{6,10},{11,7},{20,24},{25,21},{22,26},{27,23}} | collective-permute-start | bytes 786440 | tf_op jit(solution)/shard_map/ppermute | solution.py:165
  23.5 0.9 %collective-permute-start.10 = (f32[4,128,128]{2,1,0:T(8,128)S(1)}, f32[4,128,128]{2,1,0:T(8,128)S(1)}, u32[]{:S(2)}, u32[]{:S(2)}) collective-permute-start(f32[4,128,128]{2,1,0:T(8,128)S(1)} %add.57), channel_id=1, source_target_pairs={{4,12},{9,1},{6,14},{11,3},{20,28},{25,17},{22,30},{27,19}} | collective-permute-start | bytes 786440 | tf_op jit(solution)/shard_map/ppermute | solution.py:165
  24.4 3.7 %intra.5 = (f32[512,640]{1,0:T(8,128)S(1)}, f32[512,640]{1,0:T(8,128)S(1)}, f32[512,640]{1,0:T(8,128)S(1)}) custom-call(bf16[512,1024]{1,0:T(8,128)(2,1)S(1)} %get-tuple-element.86.q, bf16[512,1024]{1,0:T(8,128)(2,1)S(1)} %get-tuple-element.87.k, bf16[512,1024]{1,0:T(8,128)(2,1)S(1)} %get-tuple-element.88.v, bf16[512,1024]{1,0:T(8,128)(2,1)S(1)} %get-tuple-element.89.g), custom_call_target="tpu_custom_call" | custom-call | flops 1 | bytes 1 | tf_op jit(solution)/shard_map/intra/pallas_call | solution.py:99
  28.2 10.3 %collective-permute-start.12 = (f32[4,128,128]{2,1,0:T(8,128)S(1)}, f32[4,128,128]{2,1,0:T(8,128)S(1)}, u32[]{:S(2)}, u32[]{:S(2)}) collective-permute-start(f32[4,128,128]{2,1,0:T(8,128)S(1)} %get-tuple-element.99), channel_id=1, source_target_pairs={{0,1},{1,0},{2,3},{3,2},{4,5},{5,4},{6,7},{7,6},{8,9},{9,8},{10,11... | collective-permute-start | bytes 786440 | tf_op jit(solution)/shard_map/ppermute | solution.py:170
  38.6 0.1 collective-permute-start.11
  38.6 1.0 %collective-permute-done.12.rest_3_ = f32[4,128,128]{2,1,0:T(8,128)S(1)} collective-permute-done((f32[4,128,128]{2,1,0:T(8,128)S(1)}, f32[4,128,128]{2,1,0:T(8,128)S(1)}, u32[]{:S(2)}, u32[]{:S(2)}) %collective-permute-start.12) | collective-permute-done | bytes 262176 | tf_op jit(solution)/shard_map/ppermute | solution.py:170
  39.7 0.5 %collective-permute-done.11.rest_2_ = f32[4,128,128]{2,1,0:T(8,128)S(1)} collective-permute-done((f32[4,128,128]{2,1,0:T(8,128)S(1)}, f32[4,128,128]{2,1,0:T(8,128)S(1)}, u32[]{:S(2)}, u32[]{:S(2)}) %collective-permute-start.11) | collective-permute-done | bytes 262176 | tf_op jit(solution)/shard_map/ppermute | solution.py:170
  40.2 2.2 %final.1 = (bf16[512,1024]{1,0:T(8,128)(2,1)}, bf16[512,1024]{1,0:T(8,128)(2,1)}, bf16[512,1024]{1,0:T(8,128)(2,1)}) custom-call(s32[1]{0:T(128)} %bitcast.core, bf16[512,1024]{1,0:T(8,128)(2,1)S(1)} %get-tuple-element.87.k, bf16[512,1024]{1,0:T(8,128)(2,1)S(1)} %get-tuple-element.88.v, bf16[512,1024]{1,0:T(8,128)(2,1)S(1)} %get-tuple-element.89.g, ...), custom_call_target="tpu_custom_call" | custom-call | flops 1 | bytes 1 | tf_op jit(solution)/shard_map/final/pallas_call | solution.py:143
  (18 shorter events, 0.5 us)
Async XLA Ops:
  4.0 4.3 %collective-permute-start = (f32[4,128,128]{2,1,0:T(8,128)S(1)}, f32[4,128,128]{2,1,0:T(8,128)S(1)}, u32[]{:S(2)}, u32[]{:S(2)}) collective-permute-start(f32[4,128,128]{2,1,0:T(8,128)S(1)} %get-tuple-element.57), channel_id=1, source_target_pairs={{0,1},{1,0},{12,13},{13,12},{2,3},{3,2},{14,15},{15,14},{16,17},{1... | collective-permute-start | bytes 786440 | tf_op jit(solution)/shard_map/ppermute | solution.py:172
  6.4 3.4 %collective-permute-start.1 = (f32[4,128,128]{2,1,0:T(8,128)S(1)}, f32[4,128,128]{2,1,0:T(8,128)S(1)}, u32[]{:S(2)}, u32[]{:S(2)}) collective-permute-start(f32[4,128,128]{2,1,0:T(8,128)S(1)} %get-tuple-element.58), channel_id=1, source_target_pairs={{0,1},{1,0},{12,13},{13,12},{2,3},{3,2},{14,15},{15,14},{16,17},{1... | collective-permute-start | bytes 786440 | tf_op jit(solution)/shard_map/ppermute | solution.py:172
  10.4 6.2 %collective-permute-start.4 = (f32[4,128,128]{2,1,0:T(8,128)S(1)}, f32[4,128,128]{2,1,0:T(8,128)S(1)}, u32[]{:S(2)}, u32[]{:S(2)}) collective-permute-start(f32[4,128,128]{2,1,0:T(8,128)S(1)} %get-tuple-element.72), channel_id=1, source_target_pairs={{4,5},{5,4},{8,9},{9,8},{6,7},{7,6},{10,11},{11,10},{20,21},{21,20... | collective-permute-start | bytes 786440 | tf_op jit(solution)/shard_map/ppermute | solution.py:172
  11.1 6.3 %collective-permute-start.3 = (f32[4,128,128]{2,1,0:T(8,128)S(1)}, f32[4,128,128]{2,1,0:T(8,128)S(1)}, u32[]{:S(2)}, u32[]{:S(2)}) collective-permute-start(f32[4,128,128]{2,1,0:T(8,128)S(1)} %get-tuple-element.69), channel_id=1, source_target_pairs={{4,5},{5,4},{8,9},{9,8},{6,7},{7,6},{10,11},{11,10},{20,21},{21,20... | collective-permute-start | bytes 786440 | tf_op jit(solution)/shard_map/ppermute | solution.py:172
  11.8 7.4 %collective-permute-start.2 = (f32[4,128,128]{2,1,0:T(8,128)S(1)}, f32[4,128,128]{2,1,0:T(8,128)S(1)}, u32[]{:S(2)}, u32[]{:S(2)}) collective-permute-start(f32[4,128,128]{2,1,0:T(8,128)S(1)} %add.48), channel_id=1, source_target_pairs={{0,4},{13,9},{2,6},{15,11},{16,20},{29,25},{18,22},{31,27}} | collective-permute-start | bytes 786440 | tf_op jit(solution)/shard_map/ppermute | solution.py:165
  15.4 6.7 %collective-permute-start.7 = (f32[4,128,128]{2,1,0:T(8,128)S(1)}, f32[4,128,128]{2,1,0:T(8,128)S(1)}, u32[]{:S(2)}, u32[]{:S(2)}) collective-permute-start(f32[4,128,128]{2,1,0:T(8,128)S(1)} %add.49), channel_id=1, source_target_pairs={{0,4},{13,9},{2,6},{15,11},{16,20},{29,25},{18,22},{31,27}} | collective-permute-start | bytes 786440 | tf_op jit(solution)/shard_map/ppermute | solution.py:165
  16.7 5.3 %collective-permute-start.8 = (f32[4,128,128]{2,1,0:T(8,128)S(1)}, f32[4,128,128]{2,1,0:T(8,128)S(1)}, u32[]{:S(2)}, u32[]{:S(2)}) collective-permute-start(f32[4,128,128]{2,1,0:T(8,128)S(1)} %add_add_fusion.2), channel_id=1, source_target_pairs={{8,12},{5,1},{10,14},{7,3},{24,28},{21,17},{26,30},{23,19}} | collective-permute-start | bytes 786440 | tf_op jit(solution)/shard_map/ppermute | solution.py:165
  19.3 2.8 %collective-permute-start.5 = (f32[4,128,128]{2,1,0:T(8,128)S(1)}, f32[4,128,128]{2,1,0:T(8,128)S(1)}, u32[]{:S(2)}, u32[]{:S(2)}) collective-permute-start(f32[4,128,128]{2,1,0:T(8,128)S(1)} %add.54), channel_id=1, source_target_pairs={{4,8},{9,5},{6,10},{11,7},{20,24},{25,21},{22,26},{27,23}} | collective-permute-start | bytes 786440 | tf_op jit(solution)/shard_map/ppermute | solution.py:165
  22.1 6.0 %collective-permute-start.6 = (f32[4,128,128]{2,1,0:T(8,128)S(1)}, f32[4,128,128]{2,1,0:T(8,128)S(1)}, u32[]{:S(2)}, u32[]{:S(2)}) collective-permute-start(f32[4,128,128]{2,1,0:T(8,128)S(1)} %add.56), channel_id=1, source_target_pairs={{8,12},{5,1},{10,14},{7,3},{24,28},{21,17},{26,30},{23,19}} | collective-permute-start | bytes 786440 | tf_op jit(solution)/shard_map/ppermute | solution.py:165
  22.8 5.2 %collective-permute-start.9 = (f32[4,128,128]{2,1,0:T(8,128)S(1)}, f32[4,128,128]{2,1,0:T(8,128)S(1)}, u32[]{:S(2)}, u32[]{:S(2)}) collective-permute-start(f32[4,128,128]{2,1,0:T(8,128)S(1)} %add.57), channel_id=1, source_target_pairs={{4,8},{9,5},{6,10},{11,7},{20,24},{25,21},{22,26},{27,23}} | collective-permute-start | bytes 786440 | tf_op jit(solution)/shard_map/ppermute | solution.py:165
  23.5 4.6 %collective-permute-start.10 = (f32[4,128,128]{2,1,0:T(8,128)S(1)}, f32[4,128,128]{2,1,0:T(8,128)S(1)}, u32[]{:S(2)}, u32[]{:S(2)}) collective-permute-start(f32[4,128,128]{2,1,0:T(8,128)S(1)} %add.57), channel_id=1, source_target_pairs={{4,12},{9,1},{6,14},{11,3},{20,28},{25,17},{22,30},{27,19}} | collective-permute-start | bytes 786440 | tf_op jit(solution)/shard_map/ppermute | solution.py:165
  28.2 11.5 %collective-permute-start.12 = (f32[4,128,128]{2,1,0:T(8,128)S(1)}, f32[4,128,128]{2,1,0:T(8,128)S(1)}, u32[]{:S(2)}, u32[]{:S(2)}) collective-permute-start(f32[4,128,128]{2,1,0:T(8,128)S(1)} %get-tuple-element.99), channel_id=1, source_target_pairs={{0,1},{1,0},{2,3},{3,2},{4,5},{5,4},{6,7},{7,6},{8,9},{9,8},{10,11... | collective-permute-start | bytes 786440 | tf_op jit(solution)/shard_map/ppermute | solution.py:170
  38.6 1.6 %collective-permute-start.11 = (f32[4,128,128]{2,1,0:T(8,128)S(1)}, f32[4,128,128]{2,1,0:T(8,128)S(1)}, u32[]{:S(2)}, u32[]{:S(2)}) collective-permute-start(f32[4,128,128]{2,1,0:T(8,128)S(1)} %get-tuple-element.101), channel_id=1, source_target_pairs={{0,1},{1,0},{2,3},{3,2},{4,5},{5,4},{6,7},{7,6},{8,9},{9,8},{10,11... | collective-permute-start | bytes 786440 | tf_op jit(solution)/shard_map/ppermute | solution.py:170

commit v4 on v2

v4 whole, which is shorter than its diff:
```python
import functools

import jax
import jax.numpy as jnp
from jax import lax
from jax.experimental import pallas as pl
from jax.experimental.pallas import tpu as pltpu
from jax.sharding import PartitionSpec as P

DH = 128
CHUNKS = 4
PLAN = (1, 1, 1, 0, 1, 1, 1, 2)
F32 = jnp.float32
BF16 = jnp.bfloat16
VMEM = pl.BlockSpec(memory_space=pltpu.VMEM)
HBM = pl.BlockSpec(memory_space=pltpu.HBM)
SMEM = pl.BlockSpec(memory_space=pltpu.SMEM)


def product(left, right, left_axis, right_axis):
    return lax.dot_general(
        left, right, (((left_axis,), (right_axis,)), ((), ())), preferred_element_type=F32
    )


def head_columns(head):
    return slice(head * DH, (head + 1) * DH)


def states_kernel(core, q_hbm, k_hbm, v_hbm, g_hbm, q, k, v, g, *rest):
    parts = (len(rest) - 1) // 2
    give, keep, sems = rest[:parts], rest[parts : 2 * parts], rest[-1]
    copies = [
        pltpu.make_async_copy(source, target, sems.at[i])
        for i, (source, target) in enumerate(zip((q_hbm, k_hbm, v_hbm, g_hbm), (q, k, v, g)))
    ]
    for c in (0, 3, 1, 2):
        copies[c].start()
    is_first = core[0] == 0

    def state(left, right, outs):
        h = 0
        for out in outs:
            for i in range(out.shape[0]):
                c = head_columns(h)
                out[i] = product(left[:, c], right[:, c], 0, 0)
                h += 1

    for left, right, give_first in ((0, 3, True), (1, 2, False)):
        copies[left].wait()
        copies[right].wait()
        pair = (q, k, v, g)[left], (q, k, v, g)[right]

        @pl.when(is_first)
        def _():
            state(*pair, give if give_first else keep)

        @pl.when(jnp.logical_not(is_first))
        def _():
            state(*pair, keep if give_first else give)


def states(core, parts, q, k, v, g):
    outs = [pltpu.VMEM((n, DH, DH), F32) for n in parts] * 2
    result = pl.pallas_call(
        states_kernel,
        in_specs=[SMEM] + [HBM] * 4,
        out_specs=[VMEM] * (4 + len(outs)),
        out_shape=[pltpu.VMEM(q.shape, BF16)] * 4 + outs,
        scratch_shapes=[pltpu.SemaphoreType.DMA((4,))],
        compiler_params=pltpu.CompilerParams(vmem_limit_bytes=8 << 20),
        name="states",
    )(core, *[pltpu.with_memory_space_constraint(x, pltpu.HBM) for x in (q, k, v, g)])
    return result[:4], result[4 : 4 + len(parts)], result[4 + len(parts) :]


def intra_kernel(first, q, k, v, g, dq, dk, dv):
    rows = q.shape[0]
    row = lax.broadcasted_iota(jnp.int32, (rows, rows), 0)
    col = lax.broadcasted_iota(jnp.int32, (rows, rows), 1)
    for h in range(dq.shape[1] // DH):
        c, o = head_columns(first + h), head_columns(h)
        qh, kh, vh, gh = q[:, c], k[:, c], v[:, c], g[:, c]
        grad_scores = jnp.where(row >= col, product(gh, vh, 1, 1), 0.0).astype(BF16)
        dq[:, o] = product(grad_scores, kh, 1, 0)
        dk[:, o] = product(grad_scores, qh, 0, 0)
        attn_scores = jnp.where(row <= col, product(kh, qh, 1, 1), 0.0).astype(BF16)
        dv[:, o] = product(attn_scores, gh, 1, 0)


def intra(first, heads, q, k, v, g):
    return pl.pallas_call(
        functools.partial(intra_kernel, first),
        in_specs=[VMEM] * 4,
        out_specs=[VMEM] * 3,
        out_shape=[pltpu.VMEM((q.shape[0], heads * DH), F32)] * 3,
        compiler_params=pltpu.CompilerParams(vmem_limit_bytes=16 << 20),
        name="intra",
    )(q, k, v, g)


def final_kernel(parts, pieces, core, k, v, g, *rest):
    count = len(parts)
    mine, other, rest = rest[:count], rest[count : 2 * count], rest[2 * count :]
    local, rest = rest[: 3 * len(pieces)], rest[3 * len(pieces) :]
    (targets, outs, sems) = rest[:3], rest[3:6], rest[6]
    is_first = core[0] == 0
    of_part = [(p, i) for p, n in enumerate(parts) for i in range(n)]
    of_piece = [(p, i) for p, n in enumerate(pieces) for i in range(n)]
    heads = len(of_part)
    copies = []
    for h in range(heads):
        (part, i), (piece, j) = of_part[h], of_piece[h]
        c, o = head_columns(h), head_columns(j)
        prefix = jnp.where(is_first, mine[part][i], other[part][i]).astype(BF16)
        suffix = jnp.where(is_first, other[part][i], mine[part][i]).astype(BF16)
        local_q, local_k, local_v = (x[:, o] for x in local[3 * piece : 3 * piece + 3])
        outs[0][:, c] = (local_q + product(g[:, c], prefix, 1, 1)).astype(BF16)
        outs[1][:, c] = (local_k + product(v[:, c], suffix, 1, 1)).astype(BF16)
        outs[2][:, c] = (local_v + product(k[:, c], suffix, 1, 0)).astype(BF16)
        if h % 2 == 1 or h == heads - 1:
            cc = slice((h - h % 2) * DH, (h + 1) * DH)
            for n in range(3):
                copy = pltpu.make_async_copy(
                    outs[n].at[:, cc], targets[n].at[:, cc], sems.at[n, h // 2]
                )
                copy.start()
                copies.append(copy)
    for copy in copies:
        copy.wait()


def final(core, parts, pieces, k, v, g, mine, other, local):
    shape = jax.ShapeDtypeStruct(k.shape, BF16)
    return pl.pallas_call(
        functools.partial(final_kernel, parts, pieces),
        in_specs=[SMEM] + [VMEM] * (3 + 2 * len(parts) + 3 * len(pieces)),
        out_specs=[HBM] * 3,
        out_shape=[shape] * 3,
        scratch_shapes=[pltpu.VMEM(k.shape, BF16)] * 3
        + [pltpu.SemaphoreType.DMA((3, (sum(parts) + 1) // 2))],
        compiler_params=pltpu.CompilerParams(vmem_limit_bytes=16 << 20),
        name="final",
    )(core, k, v, g, *mine, *other, *[x for piece in local for x in piece])


def after(values, *events):
    values = tuple(values)
    return lax.optimization_barrier(values + tuple(events))[: len(values)]


def hop(value, chips, a, b):
    sends = {2 * a: 2 * b, 2 * (chips - 1 - a) + 1: 2 * (chips - 1 - b) + 1}
    pairs = list(sends.items())
    for c in range(chips):
        free = [d for d in (2 * c, 2 * c + 1) if d not in sends]
        open_ = [d for d in (2 * c, 2 * c + 1) if d not in sends.values()]
        pairs += zip(free, open_)
    return lax.ppermute(value, ("seq", "sub"), pairs)


def swap(value):
    return lax.ppermute(value, "sub", [(0, 1), (1, 0)])


def body(*args):
    chips = lax.axis_size("seq")
    core, chip = lax.axis_index("sub").astype(jnp.int32), lax.axis_index("seq")
    rank = jnp.where(core == 0, chip, chips - 1 - chip)
    heads = args[0].shape[1] // DH
    chunks = min(CHUNKS, heads)
    parts = tuple(heads * (c + 1) // chunks - heads * c // chunks for c in range(chunks))
    core = core.reshape(1)
    arrives = [rank == step for step in range(chips)]
    core, *rest = lax.optimization_barrier((core, *arrives, *args))
    arrives, args = rest[:chips], rest[chips:]
    args, give, keep = states(core, parts, *args)
    total = [x + swap(y) for x, y in zip(keep, give)]
    mine = [jnp.zeros_like(x) for x in total]
    arrived = [hop(x, chips, 0, 1) for x in total]
    slots = (chips - 2) * chunks
    plan = PLAN if (heads, slots) == (sum(PLAN), len(PLAN)) else (0,) * (slots - 1) + (heads,)
    local, pieces = [], []
    event = total[-1]
    for step in range(1, chips - 1):
        for c in range(chunks):
            (arrived[c],) = after(arrived[c : c + 1], event)
            mine[c] = jnp.where(arrives[step], arrived[c], mine[c])
            sent = total[c] + arrived[c]
            arrived[c] = hop(sent, chips, step, step + 1)
            event = sent
            now = plan[(step - 1) * chunks + c]
            if now:
                local.append(intra(sum(pieces), now, *after(args, sent)))
                pieces.append(now)
                event = local[-1][0]
    other = []
    for c in range(chunks):
        (arrived[c],) = after(arrived[c : c + 1], event)
        mine[c] = jnp.where(arrives[chips - 1], arrived[c], mine[c])
        event = mine[c] + keep[c]
        other.append(swap(event))
    q, k, v, g = args
    return tuple(final(core, parts, tuple(pieces), k, v, g, mine, other, local))


def solution(mesh):
    placed = P(("rep", "seq", "sub"), "head")
    return jax.shard_map(
        body, mesh=mesh, in_specs=(placed,) * 4, out_specs=(placed,) * 3, check_vma=False
    )
```

time: 34.3 us -> 43.4 us (1.27)
  the two profiles are of different devices: /device:TPU:31 before, /device:TPU:25 now
where the time goes in v4:
time: 43.4 us; the launch traced here: 43 us
  starting transfers between devices  25.7 us (59%)
  Pallas kernels  12.2 us (28%)
  waiting for transfers between devices  3.73 us (9%)
  between operations  1 us (2%)
    ppermute x12, starting transfers between devices, hop(): return lax.ppermute(value, ('seq', 'sub'), pairs)  13.8 us
    ppermute x8, starting transfers between devices, swap(): return lax.ppermute(value, 'sub', [(0, 1), (1, 0)])  11.9 us
    pallas_call x7, Pallas kernels, intra(): pl.pallas_call(functools.partial(intra_kernel, first), in_specs=[VMEM] *...  7.27 us
    pallas_call x1, Pallas kernels, states(): pl.pallas_call(states_kernel, in_specs=[SMEM] + [HBM] * 4, out_specs=[VME...  2.73 us
    pallas_call x1, Pallas kernels, final(): pl.pallas_call(functools.partial(final_kernel, parts, pieces), in_specs=[...  2.2 us
    ppermute x12, waiting for transfers between devices, hop(): return lax.ppermute(value, ('seq', 'sub'), pairs)  2.06 us
    ppermute x8, waiting for transfers between devices, swap(): return lax.ppermute(value, 'sub', [(0, 1), (1, 0)])  1.67 us
  transfers between devices with their start and end apart: 20, of which 6 were waited for; matrix products, arithmetic and copies ran while one was open for 1% of the time, Pallas kernels for 17%

profile of v4, /device:TPU:25, one launch (start us, length us, event | category | flops | bytes accessed | tf_op | source)
XLA Modules:
  0.0 43.0 jit_solution(2204894562437100010)
XLA Ops:
  0.6 2.7 %states.1 = (bf16[512,1024]{1,0:T(8,128)(2,1)S(1)}, bf16[512,1024]{1,0:T(8,128)(2,1)S(1)}, bf16[512,1024]{1,0:T(8,128)(2,1)S(1)}, bf16[512,1024]{1,0:T(8,128)(2,...) custom-call(s32[1]{0:T(128)} %bitcast.core, ...), custom_call_target="tpu_custom_call" | custom-call | tf_op jit(solution)/shard_map/states/pallas_call | solution.py:65
  3.4 0.7 %collective-permute-start = (f32[2,128,128]{2,1,0:T(8,128)S(1)}, f32[2,128,128]{2,1,0:T(8,128)S(1)}, u32[]{:S(2)}, u32[]{:S(2)}) collective-permute-start(f32[2,128,128]{2,1,0:T(8,128)S(1)} %get-tuple-element.94), channel_id=1, source_target_pairs={{0,1},{1,0},{2,3},{3,2},{4,5},{5,4},{6,7},{7,6},{8,9},{9,8},{10,11... | collective-permute-start | bytes 393224 | tf_op jit(solution)/shard_map/ppermute | solution.py:163
  5.1 2.1 %collective-permute-start.1 = (f32[2,128,128]{2,1,0:T(8,128)S(1)}, f32[2,128,128]{2,1,0:T(8,128)S(1)}, u32[]{:S(2)}, u32[]{:S(2)}) collective-permute-start(f32[2,128,128]{2,1,0:T(8,128)S(1)} %add.48), channel_id=1, source_target_pairs={{0,4},{13,9},{1,0},{4,5},{8,8},{12,12},{2,6},{15,11},{3,2},{6,7},{... | collective-permute-start | bytes 393224 | tf_op jit(solution)/shard_map/ppermute | solution.py:159
  7.3 1.3 %collective-permute-start.8 = (f32[2,128,128]{2,1,0:T(8,128)S(1)}, f32[2,128,128]{2,1,0:T(8,128)S(1)}, u32[]{:S(2)}, u32[]{:S(2)}) collective-permute-start(f32[2,128,128]{2,1,0:T(8,128)S(1)} %add.52), channel_id=1, source_target_pairs={{0,4},{13,9},{1,0},{4,5},{8,8},{12,12},{2,6},{15,11},{3,2},{6,7},{... | collective-permute-start | bytes 393224 | tf_op jit(solution)/shard_map/ppermute | solution.py:159
  8.6 1.3 %collective-permute-start.6 = (f32[2,128,128]{2,1,0:T(8,128)S(1)}, f32[2,128,128]{2,1,0:T(8,128)S(1)}, u32[]{:S(2)}, u32[]{:S(2)}) collective-permute-start(f32[2,128,128]{2,1,0:T(8,128)S(1)} %add.51), channel_id=1, source_target_pairs={{0,4},{13,9},{1,0},{4,5},{8,8},{12,12},{2,6},{15,11},{3,2},{6,7},{... | collective-permute-start | bytes 393224 | tf_op jit(solution)/shard_map/ppermute | solution.py:159
  9.9 1.3 %collective-permute-start.4 = (f32[2,128,128]{2,1,0:T(8,128)S(1)}, f32[2,128,128]{2,1,0:T(8,128)S(1)}, u32[]{:S(2)}, u32[]{:S(2)}) collective-permute-start(f32[2,128,128]{2,1,0:T(8,128)S(1)} %add.49), channel_id=1, source_target_pairs={{0,4},{13,9},{1,0},{4,5},{8,8},{12,12},{2,6},{15,11},{3,2},{6,7},{... | collective-permute-start | bytes 393224 | tf_op jit(solution)/shard_map/ppermute | solution.py:159
  11.3 0.7 %collective-permute-start.3 = (f32[2,128,128]{2,1,0:T(8,128)S(1)}, f32[2,128,128]{2,1,0:T(8,128)S(1)}, u32[]{:S(2)}, u32[]{:S(2)}) collective-permute-start(f32[2,128,128]{2,1,0:T(8,128)S(1)} %add.50), channel_id=1, source_target_pairs={{4,8},{9,5},{0,0},{1,1},{5,4},{8,9},{12,12},{13,13},{6,10},{11,7},... | collective-permute-start | bytes 393224 | tf_op jit(solution)/shard_map/ppermute | solution.py:159
  12.0 0.9 %intra.7 = (f32[512,128]{1,0:T(8,128)S(1)}, f32[512,128]{1,0:T(8,128)S(1)}, f32[512,128]{1,0:T(8,128)S(1)}) custom-call(bf16[512,1024]{1,0:T(8,128)(2,1)S(1)} %get-tuple-element.140.q, bf16[512,1024]{1,0:T(8,128)(2,1)S(1)} %get-tuple-element.141.k, bf16[512,1024]{1,0:T(8,128)(2,1)S(1)} %get-tuple-element.142.v, bf16[512,1024]{1,0:T(8,128)(2,1)S(1)} %get-tuple-element.143.g), custom_call_target="tpu_custom_call" | custom-call | tf_op jit(solution)/shard_map/intra/pallas_call | solution.py:92
  12.9 0.7 %collective-permute-start.12 = (f32[2,128,128]{2,1,0:T(8,128)S(1)}, f32[2,128,128]{2,1,0:T(8,128)S(1)}, u32[]{:S(2)}, u32[]{:S(2)}) collective-permute-start(f32[2,128,128]{2,1,0:T(8,128)S(1)} %add.53), channel_id=1, source_target_pairs={{4,8},{9,5},{0,0},{1,1},{5,4},{8,9},{12,12},{13,13},{6,10},{11,7},... | collective-permute-start | bytes 393224 | tf_op jit(solution)/shard_map/ppermute | solution.py:159
  13.6 0.9 %intra.8 = (f32[512,128]{1,0:T(8,128)S(1)}, f32[512,128]{1,0:T(8,128)S(1)}, f32[512,128]{1,0:T(8,128)S(1)}) custom-call(bf16[512,1024]{1,0:T(8,128)(2,1)S(1)} %get-tuple-element.140.q, bf16[512,1024]{1,0:T(8,128)(2,1)S(1)} %get-tuple-element.141.k, bf16[512,1024]{1,0:T(8,128)(2,1)S(1)} %get-tuple-element.142.v, bf16[512,1024]{1,0:T(8,128)(2,1)S(1)} %get-tuple-element.143.g), custom_call_target="tpu_custom_call" | custom-call | tf_op jit(solution)/shard_map/intra/pallas_call | solution.py:92
  14.6 0.7 %collective-permute-start.11 = (f32[2,128,128]{2,1,0:T(8,128)S(1)}, f32[2,128,128]{2,1,0:T(8,128)S(1)}, u32[]{:S(2)}, u32[]{:S(2)}) collective-permute-start(f32[2,128,128]{2,1,0:T(8,128)S(1)} %add.54), channel_id=1, source_target_pairs={{4,8},{9,5},{0,0},{1,1},{5,4},{8,9},{12,12},{13,13},{6,10},{11,7},... | collective-permute-start | bytes 393224 | tf_op jit(solution)/shard_map/ppermute | solution.py:159
  15.3 0.9 %intra.9 = (f32[512,128]{1,0:T(8,128)S(1)}, f32[512,128]{1,0:T(8,128)S(1)}, f32[512,128]{1,0:T(8,128)S(1)}) custom-call(bf16[512,1024]{1,0:T(8,128)(2,1)S(1)} %get-tuple-element.140.q, bf16[512,1024]{1,0:T(8,128)(2,1)S(1)} %get-tuple-element.141.k, bf16[512,1024]{1,0:T(8,128)(2,1)S(1)} %get-tuple-element.142.v, bf16[512,1024]{1,0:T(8,128)(2,1)S(1)} %get-tuple-element.143.g), custom_call_target="tpu_custom_call" | custom-call | tf_op jit(solution)/shard_map/intra/pallas_call | solution.py:92
  16.3 0.7 %collective-permute-start.10 = (f32[2,128,128]{2,1,0:T(8,128)S(1)}, f32[2,128,128]{2,1,0:T(8,128)S(1)}, u32[]{:S(2)}, u32[]{:S(2)}) collective-permute-start(f32[2,128,128]{2,1,0:T(8,128)S(1)} %add.55), channel_id=1, source_target_pairs={{4,8},{9,5},{0,0},{1,1},{5,4},{8,9},{12,12},{13,13},{6,10},{11,7},... | collective-permute-start | bytes 393224 | tf_op jit(solution)/shard_map/ppermute | solution.py:159
  17.0 1.3 %collective-permute-start.9 = (f32[2,128,128]{2,1,0:T(8,128)S(1)}, f32[2,128,128]{2,1,0:T(8,128)S(1)}, u32[]{:S(2)}, u32[]{:S(2)}) collective-permute-start(f32[2,128,128]{2,1,0:T(8,128)S(1)} %add.56), channel_id=1, source_target_pairs={{8,12},{5,1},{0,0},{4,4},{9,8},{12,13},{10,14},{7,3},{2,2},{6,6},{... | collective-permute-start | bytes 393224 | tf_op jit(solution)/shard_map/ppermute | solution.py:159
  18.3 0.9 %intra.10 = (f32[512,128]{1,0:T(8,128)S(1)}, f32[512,128]{1,0:T(8,128)S(1)}, f32[512,128]{1,0:T(8,128)S(1)}) custom-call(bf16[512,1024]{1,0:T(8,128)(2,1)S(1)} %get-tuple-element.140.q, bf16[512,1024]{1,0:T(8,128)(2,1)S(1)} %get-tuple-element.141.k, bf16[512,1024]{1,0:T(8,128)(2,1)S(1)} %get-tuple-element.142.v, bf16[512,1024]{1,0:T(8,128)(2,1)S(1)} %get-tuple-element.143.g), custom_call_target="tpu_custom_call" | custom-call | tf_op jit(solution)/shard_map/intra/pallas_call | solution.py:92
  19.3 1.3 %collective-permute-start.13 = (f32[2,128,128]{2,1,0:T(8,128)S(1)}, f32[2,128,128]{2,1,0:T(8,128)S(1)}, u32[]{:S(2)}, u32[]{:S(2)}) collective-permute-start(f32[2,128,128]{2,1,0:T(8,128)S(1)} %add.57), channel_id=1, source_target_pairs={{8,12},{5,1},{0,0},{4,4},{9,8},{12,13},{10,14},{7,3},{2,2},{6,6},{... | collective-permute-start | bytes 393224 | tf_op jit(solution)/shard_map/ppermute | solution.py:159
  20.6 0.9 %intra.11 = (f32[512,128]{1,0:T(8,128)S(1)}, f32[512,128]{1,0:T(8,128)S(1)}, f32[512,128]{1,0:T(8,128)S(1)}) custom-call(bf16[512,1024]{1,0:T(8,128)(2,1)S(1)} %get-tuple-element.140.q, bf16[512,1024]{1,0:T(8,128)(2,1)S(1)} %get-tuple-element.141.k, bf16[512,1024]{1,0:T(8,128)(2,1)S(1)} %get-tuple-element.142.v, bf16[512,1024]{1,0:T(8,128)(2,1)S(1)} %get-tuple-element.143.g), custom_call_target="tpu_custom_call" | custom-call | tf_op jit(solution)/shard_map/intra/pallas_call | solution.py:92
  21.5 1.3 %collective-permute-start.14 = (f32[2,128,128]{2,1,0:T(8,128)S(1)}, f32[2,128,128]{2,1,0:T(8,128)S(1)}, u32[]{:S(2)}, u32[]{:S(2)}) collective-permute-start(f32[2,128,128]{2,1,0:T(8,128)S(1)} %add.58), channel_id=1, source_target_pairs={{8,12},{5,1},{0,0},{4,4},{9,8},{12,13},{10,14},{7,3},{2,2},{6,6},{... | collective-permute-start | bytes 393224 | tf_op jit(solution)/shard_map/ppermute | solution.py:159
  22.8 0.9 %intra.12 = (f32[512,128]{1,0:T(8,128)S(1)}, f32[512,128]{1,0:T(8,128)S(1)}, f32[512,128]{1,0:T(8,128)S(1)}) custom-call(bf16[512,1024]{1,0:T(8,128)(2,1)S(1)} %get-tuple-element.140.q, bf16[512,1024]{1,0:T(8,128)(2,1)S(1)} %get-tuple-element.141.k, bf16[512,1024]{1,0:T(8,128)(2,1)S(1)} %get-tuple-element.142.v, bf16[512,1024]{1,0:T(8,128)(2,1)S(1)} %get-tuple-element.143.g), custom_call_target="tpu_custom_call" | custom-call | tf_op jit(solution)/shard_map/intra/pallas_call | solution.py:92
  23.8 1.3 %collective-permute-start.15 = (f32[2,128,128]{2,1,0:T(8,128)S(1)}, f32[2,128,128]{2,1,0:T(8,128)S(1)}, u32[]{:S(2)}, u32[]{:S(2)}) collective-permute-start(f32[2,128,128]{2,1,0:T(8,128)S(1)} %add.59), channel_id=1, source_target_pairs={{8,12},{5,1},{0,0},{4,4},{9,8},{12,13},{10,14},{7,3},{2,2},{6,6},{... | collective-permute-start | bytes 393224 | tf_op jit(solution)/shard_map/ppermute | solution.py:159
  25.1 1.6 %intra.13 = (f32[512,256]{1,0:T(8,128)S(1)}, f32[512,256]{1,0:T(8,128)S(1)}, f32[512,256]{1,0:T(8,128)S(1)}) custom-call(bf16[512,1024]{1,0:T(8,128)(2,1)S(1)} %get-tuple-element.140.q, bf16[512,1024]{1,0:T(8,128)(2,1)S(1)} %get-tuple-element.141.k, bf16[512,1024]{1,0:T(8,128)(2,1)S(1)} %get-tuple-element.142.v, bf16[512,1024]{1,0:T(8,128)(2,1)S(1)} %get-tuple-element.143.g), custom_call_target="tpu_custom_call" | custom-call | tf_op jit(solution)/shard_map/intra/pallas_call | solution.py:92
  26.9 2.0 %collective-permute-done.15 = f32[2,128,128]{2,1,0:T(8,128)S(1)} collective-permute-done((f32[2,128,128]{2,1,0:T(8,128)S(1)}, f32[2,128,128]{2,1,0:T(8,128)S(1)}, u32[]{:S(2)}, u32[]{:S(2)}) %collective-permute-start.15) | collective-permute-done | bytes 131104 | tf_op jit(solution)/shard_map/ppermute | solution.py:159
  29.0 10.0 %collective-permute-start.19 = (f32[2,128,128]{2,1,0:T(8,128)S(1)}, f32[2,128,128]{2,1,0:T(8,128)S(1)}, u32[]{:S(2)}, u32[]{:S(2)}) collective-permute-start(f32[2,128,128]{2,1,0:T(8,128)S(1)} %get-tuple-element.165), channel_id=1, source_target_pairs={{0,1},{1,0},{2,3},{3,2},{4,5},{5,4},{6,7},{7,6},{8,9},{9,8},{10,11... | collective-permute-start | bytes 393224 | tf_op jit(solution)/shard_map/ppermute | solution.py:163
  40.8 2.2 %final.1 = (bf16[512,1024]{1,0:T(8,128)(2,1)}, bf16[512,1024]{1,0:T(8,128)(2,1)}, bf16[512,1024]{1,0:T(8,128)(2,1)}) custom-call(s32[1]{0:T(128)} %bitcast.core, bf16[512,1024]{1,0:T(8,128)(2,1)S(1)} %get-tuple-element.141.k, bf16[512,1024]{1,0:T(8,128)(2,1)S(1)} %get-tuple-element.142.v, bf16[512,1024]{1,0:T(8,128)(2,1)S(1)} %get-tuple-element.143.g, ...), custom_call_target="tpu_custom_call" | custom-call | tf_op jit(solution)/shard_map/final/pallas_call | solution.py:135
  (41 shorter events, 3.3 us)
Async XLA Ops:
  3.4 1.7 %collective-permute-start = (f32[2,128,128]{2,1,0:T(8,128)S(1)}, f32[2,128,128]{2,1,0:T(8,128)S(1)}, u32[]{:S(2)}, u32[]{:S(2)}) collective-permute-start(f32[2,128,128]{2,1,0:T(8,128)S(1)} %get-tuple-element.94), channel_id=1, source_target_pairs={{0,1},{1,0},{2,3},{3,2},{4,5},{5,4},{6,7},{7,6},{8,9},{9,8},{10,11... | collective-permute-start | bytes 393224 | tf_op jit(solution)/shard_map/ppermute | solution.py:163
  4.1 3.1 %collective-permute-start.7 = (f32[2,128,128]{2,1,0:T(8,128)S(1)}, f32[2,128,128]{2,1,0:T(8,128)S(1)}, u32[]{:S(2)}, u32[]{:S(2)}) collective-permute-start(f32[2,128,128]{2,1,0:T(8,128)S(1)} %get-tuple-element.102), channel_id=1, source_target_pairs={{0,1},{1,0},{2,3},{3,2},{4,5},{5,4},{6,7},{7,6},{8,9},{9,8},{10,11... | collective-permute-start | bytes 393224 | tf_op jit(solution)/shard_map/ppermute | solution.py:163
  4.2 4.4 %collective-permute-start.5 = (f32[2,128,128]{2,1,0:T(8,128)S(1)}, f32[2,128,128]{2,1,0:T(8,128)S(1)}, u32[]{:S(2)}, u32[]{:S(2)}) collective-permute-start(f32[2,128,128]{2,1,0:T(8,128)S(1)} %get-tuple-element.100), channel_id=1, source_target_pairs={{0,1},{1,0},{2,3},{3,2},{4,5},{5,4},{6,7},{7,6},{8,9},{9,8},{10,11... | collective-permute-start | bytes 393224 | tf_op jit(solution)/shard_map/ppermute | solution.py:163
  4.6 5.3 %collective-permute-start.2 = (f32[2,128,128]{2,1,0:T(8,128)S(1)}, f32[2,128,128]{2,1,0:T(8,128)S(1)}, u32[]{:S(2)}, u32[]{:S(2)}) collective-permute-start(f32[2,128,128]{2,1,0:T(8,128)S(1)} %get-tuple-element.96), channel_id=1, source_target_pairs={{0,1},{1,0},{2,3},{3,2},{4,5},{5,4},{6,7},{7,6},{8,9},{9,8},{10,11... | collective-permute-start | bytes 393224 | tf_op jit(solution)/shard_map/ppermute | solution.py:163
  5.1 6.1 %collective-permute-start.1 = (f32[2,128,128]{2,1,0:T(8,128)S(1)}, f32[2,128,128]{2,1,0:T(8,128)S(1)}, u32[]{:S(2)}, u32[]{:S(2)}) collective-permute-start(f32[2,128,128]{2,1,0:T(8,128)S(1)} %add.48), channel_id=1, source_target_pairs={{0,4},{13,9},{1,0},{4,5},{8,8},{12,12},{2,6},{15,11},{3,2},{6,7},{... | collective-permute-start | bytes 393224 | tf_op jit(solution)/shard_map/ppermute | solution.py:159
  7.3 5.7 %collective-permute-start.8 = (f32[2,128,128]{2,1,0:T(8,128)S(1)}, f32[2,128,128]{2,1,0:T(8,128)S(1)}, u32[]{:S(2)}, u32[]{:S(2)}) collective-permute-start(f32[2,128,128]{2,1,0:T(8,128)S(1)} %add.52), channel_id=1, source_target_pairs={{0,4},{13,9},{1,0},{4,5},{8,8},{12,12},{2,6},{15,11},{3,2},{6,7},{... | collective-permute-start | bytes 393224 | tf_op jit(solution)/shard_map/ppermute | solution.py:159
  8.6 6.0 %collective-permute-start.6 = (f32[2,128,128]{2,1,0:T(8,128)S(1)}, f32[2,128,128]{2,1,0:T(8,128)S(1)}, u32[]{:S(2)}, u32[]{:S(2)}) collective-permute-start(f32[2,128,128]{2,1,0:T(8,128)S(1)} %add.51), channel_id=1, source_target_pairs={{0,4},{13,9},{1,0},{4,5},{8,8},{12,12},{2,6},{15,11},{3,2},{6,7},{... | collective-permute-start | bytes 393224 | tf_op jit(solution)/shard_map/ppermute | solution.py:159
  9.9 6.3 %collective-permute-start.4 = (f32[2,128,128]{2,1,0:T(8,128)S(1)}, f32[2,128,128]{2,1,0:T(8,128)S(1)}, u32[]{:S(2)}, u32[]{:S(2)}) collective-permute-start(f32[2,128,128]{2,1,0:T(8,128)S(1)} %add.49), channel_id=1, source_target_pairs={{0,4},{13,9},{1,0},{4,5},{8,8},{12,12},{2,6},{15,11},{3,2},{6,7},{... | collective-permute-start | bytes 393224 | tf_op jit(solution)/shard_map/ppermute | solution.py:159
  11.3 5.7 %collective-permute-start.3 = (f32[2,128,128]{2,1,0:T(8,128)S(1)}, f32[2,128,128]{2,1,0:T(8,128)S(1)}, u32[]{:S(2)}, u32[]{:S(2)}) collective-permute-start(f32[2,128,128]{2,1,0:T(8,128)S(1)} %add.50), channel_id=1, source_target_pairs={{4,8},{9,5},{0,0},{1,1},{5,4},{8,9},{12,12},{13,13},{6,10},{11,7},... | collective-permute-start | bytes 393224 | tf_op jit(solution)/shard_map/ppermute | solution.py:159
  12.9 6.3 %collective-permute-start.12 = (f32[2,128,128]{2,1,0:T(8,128)S(1)}, f32[2,128,128]{2,1,0:T(8,128)S(1)}, u32[]{:S(2)}, u32[]{:S(2)}) collective-permute-start(f32[2,128,128]{2,1,0:T(8,128)S(1)} %add.53), channel_id=1, source_target_pairs={{4,8},{9,5},{0,0},{1,1},{5,4},{8,9},{12,12},{13,13},{6,10},{11,7},... | collective-permute-start | bytes 393224 | tf_op jit(solution)/shard_map/ppermute | solution.py:159
  14.6 6.9 %collective-permute-start.11 = (f32[2,128,128]{2,1,0:T(8,128)S(1)}, f32[2,128,128]{2,1,0:T(8,128)S(1)}, u32[]{:S(2)}, u32[]{:S(2)}) collective-permute-start(f32[2,128,128]{2,1,0:T(8,128)S(1)} %add.54), channel_id=1, source_target_pairs={{4,8},{9,5},{0,0},{1,1},{5,4},{8,9},{12,12},{13,13},{6,10},{11,7},... | collective-permute-start | bytes 393224 | tf_op jit(solution)/shard_map/ppermute | solution.py:159
  16.3 7.5 %collective-permute-start.10 = (f32[2,128,128]{2,1,0:T(8,128)S(1)}, f32[2,128,128]{2,1,0:T(8,128)S(1)}, u32[]{:S(2)}, u32[]{:S(2)}) collective-permute-start(f32[2,128,128]{2,1,0:T(8,128)S(1)} %add.55), channel_id=1, source_target_pairs={{4,8},{9,5},{0,0},{1,1},{5,4},{8,9},{12,12},{13,13},{6,10},{11,7},... | collective-permute-start | bytes 393224 | tf_op jit(solution)/shard_map/ppermute | solution.py:159
  17.0 9.8 %collective-permute-start.9 = (f32[2,128,128]{2,1,0:T(8,128)S(1)}, f32[2,128,128]{2,1,0:T(8,128)S(1)}, u32[]{:S(2)}, u32[]{:S(2)}) collective-permute-start(f32[2,128,128]{2,1,0:T(8,128)S(1)} %add.56), channel_id=1, source_target_pairs={{8,12},{5,1},{0,0},{4,4},{9,8},{12,13},{10,14},{7,3},{2,2},{6,6},{... | collective-permute-start | bytes 393224 | tf_op jit(solution)/shard_map/ppermute | solution.py:159
  19.3 7.6 %collective-permute-start.13 = (f32[2,128,128]{2,1,0:T(8,128)S(1)}, f32[2,128,128]{2,1,0:T(8,128)S(1)}, u32[]{:S(2)}, u32[]{:S(2)}) collective-permute-start(f32[2,128,128]{2,1,0:T(8,128)S(1)} %add.57), channel_id=1, source_target_pairs={{8,12},{5,1},{0,0},{4,4},{9,8},{12,13},{10,14},{7,3},{2,2},{6,6},{... | collective-permute-start | bytes 393224 | tf_op jit(solution)/shard_map/ppermute | solution.py:159
  21.5 5.3 %collective-permute-start.14 = (f32[2,128,128]{2,1,0:T(8,128)S(1)}, f32[2,128,128]{2,1,0:T(8,128)S(1)}, u32[]{:S(2)}, u32[]{:S(2)}) collective-permute-start(f32[2,128,128]{2,1,0:T(8,128)S(1)} %add.58), channel_id=1, source_target_pairs={{8,12},{5,1},{0,0},{4,4},{9,8},{12,13},{10,14},{7,3},{2,2},{6,6},{... | collective-permute-start | bytes 393224 | tf_op jit(solution)/shard_map/ppermute | solution.py:159
  23.8 5.1 %collective-permute-start.15 = (f32[2,128,128]{2,1,0:T(8,128)S(1)}, f32[2,128,128]{2,1,0:T(8,128)S(1)}, u32[]{:S(2)}, u32[]{:S(2)}) collective-permute-start(f32[2,128,128]{2,1,0:T(8,128)S(1)} %add.59), channel_id=1, source_target_pairs={{8,12},{5,1},{0,0},{4,4},{9,8},{12,13},{10,14},{7,3},{2,2},{6,6},{... | collective-permute-start | bytes 393224 | tf_op jit(solution)/shard_map/ppermute | solution.py:159
  29.0 11.0 %collective-permute-start.19 = (f32[2,128,128]{2,1,0:T(8,128)S(1)}, f32[2,128,128]{2,1,0:T(8,128)S(1)}, u32[]{:S(2)}, u32[]{:S(2)}) collective-permute-start(f32[2,128,128]{2,1,0:T(8,128)S(1)} %get-tuple-element.165), channel_id=1, source_target_pairs={{0,1},{1,0},{2,3},{3,2},{4,5},{5,4},{6,7},{7,6},{8,9},{9,8},{10,11... | collective-permute-start | bytes 393224 | tf_op jit(solution)/shard_map/ppermute | solution.py:163
  39.0 1.3 %collective-permute-start.18 = (f32[2,128,128]{2,1,0:T(8,128)S(1)}, f32[2,128,128]{2,1,0:T(8,128)S(1)}, u32[]{:S(2)}, u32[]{:S(2)}) collective-permute-start(f32[2,128,128]{2,1,0:T(8,128)S(1)} %get-tuple-element.167), channel_id=1, source_target_pairs={{0,1},{1,0},{2,3},{3,2},{4,5},{5,4},{6,7},{7,6},{8,9},{9,8},{10,11... | collective-permute-start | bytes 393224 | tf_op jit(solution)/shard_map/ppermute | solution.py:163
  39.0 1.5 %collective-permute-start.17 = (f32[2,128,128]{2,1,0:T(8,128)S(1)}, f32[2,128,128]{2,1,0:T(8,128)S(1)}, u32[]{:S(2)}, u32[]{:S(2)}) collective-permute-start(f32[2,128,128]{2,1,0:T(8,128)S(1)} %get-tuple-element.169), channel_id=1, source_target_pairs={{0,1},{1,0},{2,3},{3,2},{4,5},{5,4},{6,7},{7,6},{8,9},{9,8},{10,11... | collective-permute-start | bytes 393224 | tf_op jit(solution)/shard_map/ppermute | solution.py:163
  39.5 1.3 %collective-permute-start.16 = (f32[2,128,128]{2,1,0:T(8,128)S(1)}, f32[2,128,128]{2,1,0:T(8,128)S(1)}, u32[]{:S(2)}, u32[]{:S(2)}) collective-permute-start(f32[2,128,128]{2,1,0:T(8,128)S(1)} %get-tuple-element.171), channel_id=1, source_target_pairs={{0,1},{1,0},{2,3},{3,2},{4,5},{5,4},{6,7},{7,6},{8,9},{9,8},{10,11... | collective-permute-start | bytes 393224 | tf_op jit(solution)/shard_map/ppermute | solution.py:163

commit v5 on v4

--- a/solution.py
+++ b/solution.py
@@ -8,8 +8,6 @@
 from jax.sharding import PartitionSpec as P
 
 DH = 128
-CHUNKS = 4
-PLAN = (1, 1, 1, 0, 1, 1, 1, 2)
 F32 = jnp.float32
 BF16 = jnp.bfloat16
 VMEM = pl.BlockSpec(memory_space=pltpu.VMEM)
@@ -149,14 +147,21 @@
     return lax.optimization_barrier(values + tuple(events))[: len(values)]
 
 
-def hop(value, chips, a, b):
-    sends = {2 * a: 2 * b, 2 * (chips - 1 - a) + 1: 2 * (chips - 1 - b) + 1}
+def move(value, chips, hops):
+    sends = {}
+    for a, b in hops:
+        sends[2 * a] = 2 * b
+        sends[2 * (chips - 1 - a) + 1] = 2 * (chips - 1 - b) + 1
     pairs = list(sends.items())
     for c in range(chips):
         free = [d for d in (2 * c, 2 * c + 1) if d not in sends]
         open_ = [d for d in (2 * c, 2 * c + 1) if d not in sends.values()]
-        pairs += zip(free, open_)
+        pairs += zip(free, open_, strict=True)
     return lax.ppermute(value, ("seq", "sub"), pairs)
+
+
+def step_hops(chips, step):
+    return [(step, step + 1), (chips - 2 - step, chips - 1 - step)]
 
 
 def swap(value):
@@ -165,43 +170,53 @@
 
 def body(*args):
     chips = lax.axis_size("seq")
+    last = chips - 1
     core, chip = lax.axis_index("sub").astype(jnp.int32), lax.axis_index("seq")
-    rank = jnp.where(core == 0, chip, chips - 1 - chip)
+    rank = jnp.where(core == 0, chip, last - chip)
     heads = args[0].shape[1] // DH
-    chunks = min(CHUNKS, heads)
-    parts = tuple(heads * (c + 1) // chunks - heads * c // chunks for c in range(chunks))
+    parts = (heads // 2, heads - heads // 2)
+    pieces = parts
     core = core.reshape(1)
-    arrives = [rank == step for step in range(chips)]
-    core, *rest = lax.optimization_barrier((core, *arrives, *args))
-    arrives, args = rest[:chips], rest[chips:]
+    at = [rank == r for r in range(chips)] + [(rank == 1) | (rank == 3)]
+    core, *rest = lax.optimization_barrier((core, *at, *args))
+    at, args = rest[: chips + 1], rest[chips + 1 :]
     args, give, keep = states(core, parts, *args)
-    total = [x + swap(y) for x, y in zip(keep, give)]
-    mine = [jnp.zeros_like(x) for x in total]
-    arrived = [hop(x, chips, 0, 1) for x in total]
-    slots = (chips - 2) * chunks
-    plan = PLAN if (heads, slots) == (sum(PLAN), len(PLAN)) else (0,) * (slots - 1) + (heads,)
-    local, pieces = [], []
-    event = total[-1]
-    for step in range(1, chips - 1):
-        for c in range(chunks):
-            (arrived[c],) = after(arrived[c : c + 1], event)
-            mine[c] = jnp.where(arrives[step], arrived[c], mine[c])
-            sent = total[c] + arrived[c]
-            arrived[c] = hop(sent, chips, step, step + 1)
-            event = sent
-            now = plan[(step - 1) * chunks + c]
-            if now:
-                local.append(intra(sum(pieces), now, *after(args, sent)))
-                pieces.append(now)
-                event = local[-1][0]
-    other = []
-    for c in range(chunks):
-        (arrived[c],) = after(arrived[c : c + 1], event)
-        mine[c] = jnp.where(arrives[chips - 1], arrived[c], mine[c])
-        event = mine[c] + keep[c]
-        other.append(swap(event))
+    total_a, total_b = (x + swap(y) for x, y in zip(keep, give))
+    zero_a, zero_b = jnp.zeros_like(total_a), jnp.zeros_like(total_b)
+    arrived_a, arrived_b = (move(x, chips, step_hops(chips, 0)) for x in (total_a, total_b))
+    local_a = intra(0, parts[0], *after(args, total_a, total_b))
+    (arrived_a,) = after((arrived_a,), local_a[0])
+    mine_a = jnp.where(at[1], arrived_a, zero_a)
+    direct = chips == 4
+    mine_b = jnp.where(at[-1] if direct else at[1], arrived_b, zero_b)
+    for step in range(1, last):
+        sent_a = total_a + arrived_a
+        arrived_a = move(sent_a, chips, step_hops(chips, step))
+        if not (direct and step == last - 1):
+            (arrived_b,) = after((arrived_b,), sent_a)
+            sent_b = total_b + arrived_b
+            arrived_b = move(sent_b, chips, step_hops(chips, step))
+            if direct:
+                far_b = move(sent_b, chips, [(1, 3), (0, 1)])
+        if step == last - 1:
+            local_b = intra(parts[0], parts[1], *after(args, sent_a))
+            if direct:
+                arrived_a, far_b = after((arrived_a, far_b), local_b[0])
+                mine_b = mine_b + jnp.where(at[3], far_b, zero_b)
+                mine_b = jnp.where(at[2], arrived_b, mine_b)
+            else:
+                (arrived_a,) = after((arrived_a,), local_b[0])
+        if not direct:
+            mine_b = jnp.where(at[step + 1], arrived_b, mine_b)
+        mine_a = jnp.where(at[step + 1], arrived_a, mine_a)
+    other_b = swap(mine_b + keep[1])
+    other_a = swap(mine_a + keep[0])
     q, k, v, g = args
-    return tuple(final(core, parts, tuple(pieces), k, v, g, mine, other, local))
+    return tuple(
+        final(
+            core, parts, pieces, k, v, g, (mine_a, mine_b), (other_a, other_b), (local_a, local_b)
+        )
+    )
 
 
 def solution(mesh):

time: 43.4 us -> 32.2 us (0.74)
  the two profiles are of different devices: /device:TPU:25 before, /device:TPU:19 now
where the time goes in v5:
time: 32.2 us; the launch traced here: 32 us
  starting transfers between devices  15.6 us (48%)
  Pallas kernels  11 us (34%)
  waiting for transfers between devices  4.32 us (13%)
  between operations  0.73 us (2%)
  other arithmetic  0.34 us (1%)
    ppermute x6, starting transfers between devices, move(): return lax.ppermute(value, ('seq', 'sub'), pairs)  11.6 us
    pallas_call x2, Pallas kernels, intra(): pl.pallas_call(functools.partial(intra_kernel, first), in_specs=[VMEM] *...  5.98 us
    ppermute x4, starting transfers between devices, swap(): return lax.ppermute(value, 'sub', [(0, 1), (1, 0)])  4.02 us
    pallas_call x1, Pallas kernels, states(): pl.pallas_call(states_kernel, in_specs=[SMEM] + [HBM] * 4, out_specs=[VME...  2.73 us
    ppermute x4, waiting for transfers between devices, swap(): return lax.ppermute(value, 'sub', [(0, 1), (1, 0)])  2.6 us
    pallas_call x1, Pallas kernels, final(): pl.pallas_call(functools.partial(final_kernel, parts, pieces), in_specs=[...  2.29 us
    ppermute x6, waiting for transfers between devices, move(): return lax.ppermute(value, ('seq', 'sub'), pairs)  1.72 us
  transfers between devices with their start and end apart: 10, of which 7 were waited for; matrix products, arithmetic and copies ran while one was open for 1% of the time, Pallas kernels for 19%

profile of v5, /device:TPU:19, one launch (start us, length us, event | category | flops | bytes accessed | tf_op | source)
XLA Modules:
  0.0 32.0 jit_solution(11918154829944225675)
XLA Ops:
  0.6 2.7 %states.1 = (bf16[512,1024]{1,0:T(8,128)(2,1)S(1)}, bf16[512,1024]{1,0:T(8,128)(2,1)S(1)}, bf16[512,1024]{1,0:T(8,128)(2,1)S(1)}, bf16[512,1024]{1,0:T(8,128)(2,...) custom-call(s32[1]{0:T(128)} %bitcast.core, ...), custom_call_target="tpu_custom_call" | custom-call | tf_op jit(solution)/shard_map/states/pallas_call | solution.py:63
  3.4 0.7 %collective-permute-start = (f32[4,128,128]{2,1,0:T(8,128)S(1)}, f32[4,128,128]{2,1,0:T(8,128)S(1)}, u32[]{:S(2)}, u32[]{:S(2)}) collective-permute-start(f32[4,128,128]{2,1,0:T(8,128)S(1)} %get-tuple-element.48), channel_id=1, source_target_pairs={{0,1},{1,0},{2,3},{3,2},{4,5},{5,4},{6,7},{7,6},{8,9},{9,8},{10,11... | collective-permute-start | bytes 786440 | tf_op jit(solution)/shard_map/ppermute | solution.py:168
  4.1 0.1 collective-permute-start.2
  4.2 1.1 %collective-permute-done = f32[4,128,128]{2,1,0:T(8,128)S(1)} collective-permute-done((f32[4,128,128]{2,1,0:T(8,128)S(1)}, f32[4,128,128]{2,1,0:T(8,128)S(1)}, u32[]{:S(2)}, u32[]{:S(2)}) %collective-permute-start) | collective-permute-done | bytes 262176 | tf_op jit(solution)/shard_map/ppermute | solution.py:168
  5.3 0.4 %collective-permute-start.1 = (f32[4,128,128]{2,1,0:T(8,128)S(1)}, f32[4,128,128]{2,1,0:T(8,128)S(1)}, u32[]{:S(2)}, u32[]{:S(2)}) collective-permute-start(f32[4,128,128]{2,1,0:T(8,128)S(1)} %add.24), channel_id=1, source_target_pairs={{0,4},{13,9},{8,12},{5,1},{1,0},{4,5},{9,8},{12,13},{2,6},{15,11},... | collective-permute-start | bytes 786440 | tf_op jit(solution)/shard_map/ppermute | solution.py:160
  5.8 1.6 %collective-permute-start.5 = (f32[4,128,128]{2,1,0:T(8,128)S(1)}, f32[4,128,128]{2,1,0:T(8,128)S(1)}, u32[]{:S(2)}, u32[]{:S(2)}) collective-permute-start(f32[4,128,128]{2,1,0:T(8,128)S(1)} %add.25), channel_id=1, source_target_pairs={{0,4},{13,9},{8,12},{5,1},{1,0},{4,5},{9,8},{12,13},{2,6},{15,11},... | collective-permute-start | bytes 786440 | tf_op jit(solution)/shard_map/ppermute | solution.py:160
  7.5 3.0 %intra.2 = (f32[512,512]{1,0:T(8,128)S(1)}, f32[512,512]{1,0:T(8,128)S(1)}, f32[512,512]{1,0:T(8,128)S(1)}) custom-call(bf16[512,1024]{1,0:T(8,128)(2,1)S(1)} %get-tuple-element.59.q, bf16[512,1024]{1,0:T(8,128)(2,1)S(1)} %get-tuple-element.60.k, bf16[512,1024]{1,0:T(8,128)(2,1)S(1)} %get-tuple-element.61.v, bf16[512,1024]{1,0:T(8,128)(2,1)S(1)} %get-tuple-element.62.g), custom_call_target="tpu_custom_call" | custom-call | tf_op jit(solution)/shard_map/intra/pallas_call | solution.py:90
  10.5 0.2 collective-permute-done.1
  10.7 1.9 %collective-permute-start.3 = (f32[4,128,128]{2,1,0:T(8,128)S(1)}, f32[4,128,128]{2,1,0:T(8,128)S(1)}, u32[]{:S(2)}, u32[]{:S(2)}) collective-permute-start(f32[4,128,128]{2,1,0:T(8,128)S(1)} %add.26), channel_id=1, source_target_pairs={{4,8},{9,5},{0,0},{1,1},{5,4},{8,9},{12,12},{13,13},{6,10},{11,7},... | collective-permute-start | bytes 786440 | tf_op jit(solution)/shard_map/ppermute | solution.py:160
  12.6 0.8 %collective-permute-done.5 = f32[4,128,128]{2,1,0:T(8,128)S(1)} collective-permute-done((f32[4,128,128]{2,1,0:T(8,128)S(1)}, f32[4,128,128]{2,1,0:T(8,128)S(1)}, u32[]{:S(2)}, u32[]{:S(2)}) %collective-permute-start.5) | collective-permute-done | bytes 262176 | tf_op jit(solution)/shard_map/ppermute | solution.py:160
  13.4 2.0 %collective-permute-start.6 = (f32[4,128,128]{2,1,0:T(8,128)S(1)}, f32[4,128,128]{2,1,0:T(8,128)S(1)}, u32[]{:S(2)}, u32[]{:S(2)}) collective-permute-start(f32[4,128,128]{2,1,0:T(8,128)S(1)} %add.28), channel_id=1, source_target_pairs={{4,12},{9,1},{0,4},{13,9},{1,0},{5,5},{8,8},{12,13},{6,14},{11,3},... | collective-permute-start | bytes 786440 | tf_op jit(solution)/shard_map/ppermute | solution.py:160
  15.4 0.5 %collective-permute-done.3 = f32[4,128,128]{2,1,0:T(8,128)S(1)} collective-permute-done((f32[4,128,128]{2,1,0:T(8,128)S(1)}, f32[4,128,128]{2,1,0:T(8,128)S(1)}, u32[]{:S(2)}, u32[]{:S(2)}) %collective-permute-start.3) | collective-permute-done | bytes 262176 | tf_op jit(solution)/shard_map/ppermute | solution.py:160
  15.9 3.7 %collective-permute-start.4 = (f32[4,128,128]{2,1,0:T(8,128)S(1)}, f32[4,128,128]{2,1,0:T(8,128)S(1)}, u32[]{:S(2)}, u32[]{:S(2)}) collective-permute-start(f32[4,128,128]{2,1,0:T(8,128)S(1)} %add.27), channel_id=1, source_target_pairs={{8,12},{5,1},{0,4},{13,9},{1,0},{4,5},{9,8},{12,13},{10,14},{7,3},... | collective-permute-start | bytes 786440 | tf_op jit(solution)/shard_map/ppermute | solution.py:160
  19.7 1.9 %collective-permute-start.7 = (f32[4,128,128]{2,1,0:T(8,128)S(1)}, f32[4,128,128]{2,1,0:T(8,128)S(1)}, u32[]{:S(2)}, u32[]{:S(2)}) collective-permute-start(f32[4,128,128]{2,1,0:T(8,128)S(1)} %add.28), channel_id=1, source_target_pairs={{4,8},{9,5},{0,0},{1,1},{5,4},{8,9},{12,12},{13,13},{6,10},{11,7},... | collective-permute-start | bytes 786440 | tf_op jit(solution)/shard_map/ppermute | solution.py:160
  21.6 3.0 %intra.3 = (f32[512,512]{1,0:T(8,128)S(1)}, f32[512,512]{1,0:T(8,128)S(1)}, f32[512,512]{1,0:T(8,128)S(1)}) custom-call(bf16[512,1024]{1,0:T(8,128)(2,1)S(1)} %get-tuple-element.59.q, bf16[512,1024]{1,0:T(8,128)(2,1)S(1)} %get-tuple-element.60.k, bf16[512,1024]{1,0:T(8,128)(2,1)S(1)} %get-tuple-element.61.v, bf16[512,1024]{1,0:T(8,128)(2,1)S(1)} %get-tuple-element.62.g), custom_call_target="tpu_custom_call" | custom-call | tf_op jit(solution)/shard_map/intra/pallas_call | solution.py:90
  24.6 0.0 collective-permute-done.6
  24.6 0.3 collective-permute-done.7
  24.9 0.1 fusion
  24.9 3.1 %collective-permute-start.9 = (f32[4,128,128]{2,1,0:T(8,128)S(1)}, f32[4,128,128]{2,1,0:T(8,128)S(1)}, u32[]{:S(2)}, u32[]{:S(2)}) collective-permute-start(f32[4,128,128]{2,1,0:T(8,128)S(1)} %get-tuple-element.73), channel_id=1, source_target_pairs={{0,1},{1,0},{2,3},{3,2},{4,5},{5,4},{6,7},{7,6},{8,9},{9,8},{10,11... | collective-permute-start | bytes 786440 | tf_op jit(solution)/shard_map/ppermute | solution.py:168
  28.1 0.1 fusion.1
  28.1 0.1 collective-permute-start.8
  28.2 1.0 %collective-permute-done.9.rest_3_ = f32[4,128,128]{2,1,0:T(8,128)S(1)} collective-permute-done((f32[4,128,128]{2,1,0:T(8,128)S(1)}, f32[4,128,128]{2,1,0:T(8,128)S(1)}, u32[]{:S(2)}, u32[]{:S(2)}) %collective-permute-start.9) | collective-permute-done | bytes 262176 | tf_op jit(solution)/shard_map/ppermute | solution.py:168
  29.2 0.5 %collective-permute-done.8.rest_2_ = f32[4,128,128]{2,1,0:T(8,128)S(1)} collective-permute-done((f32[4,128,128]{2,1,0:T(8,128)S(1)}, f32[4,128,128]{2,1,0:T(8,128)S(1)}, u32[]{:S(2)}, u32[]{:S(2)}) %collective-permute-start.8) | collective-permute-done | bytes 262176 | tf_op jit(solution)/shard_map/ppermute | solution.py:168
  29.7 2.3 %final.1 = (bf16[512,1024]{1,0:T(8,128)(2,1)}, bf16[512,1024]{1,0:T(8,128)(2,1)}, bf16[512,1024]{1,0:T(8,128)(2,1)}) custom-call(s32[1]{0:T(128)} %bitcast.core, bf16[512,1024]{1,0:T(8,128)(2,1)S(1)} %get-tuple-element.60.k, bf16[512,1024]{1,0:T(8,128)(2,1)S(1)} %get-tuple-element.61.v, bf16[512,1024]{1,0:T(8,128)(2,1)S(1)} %get-tuple-element.62.g, ...), custom_call_target="tpu_custom_call" | custom-call | tf_op jit(solution)/shard_map/final/pallas_call | solution.py:133
  (7 shorter events, 0.2 us)
Async XLA Ops:
  3.4 1.9 %collective-permute-start = (f32[4,128,128]{2,1,0:T(8,128)S(1)}, f32[4,128,128]{2,1,0:T(8,128)S(1)}, u32[]{:S(2)}, u32[]{:S(2)}) collective-permute-start(f32[4,128,128]{2,1,0:T(8,128)S(1)} %get-tuple-element.48), channel_id=1, source_target_pairs={{0,1},{1,0},{2,3},{3,2},{4,5},{5,4},{6,7},{7,6},{8,9},{9,8},{10,11... | collective-permute-start | bytes 786440 | tf_op jit(solution)/shard_map/ppermute | solution.py:168
  4.1 1.6 %collective-permute-start.2 = (f32[4,128,128]{2,1,0:T(8,128)S(1)}, f32[4,128,128]{2,1,0:T(8,128)S(1)}, u32[]{:S(2)}, u32[]{:S(2)}) collective-permute-start(f32[4,128,128]{2,1,0:T(8,128)S(1)} %get-tuple-element.51), channel_id=1, source_target_pairs={{0,1},{1,0},{2,3},{3,2},{4,5},{5,4},{6,7},{7,6},{8,9},{9,8},{10,11... | collective-permute-start | bytes 786440 | tf_op jit(solution)/shard_map/ppermute | solution.py:168
  5.3 5.3 %collective-permute-start.1 = (f32[4,128,128]{2,1,0:T(8,128)S(1)}, f32[4,128,128]{2,1,0:T(8,128)S(1)}, u32[]{:S(2)}, u32[]{:S(2)}) collective-permute-start(f32[4,128,128]{2,1,0:T(8,128)S(1)} %add.24), channel_id=1, source_target_pairs={{0,4},{13,9},{8,12},{5,1},{1,0},{4,5},{9,8},{12,13},{2,6},{15,11},... | collective-permute-start | bytes 786440 | tf_op jit(solution)/shard_map/ppermute | solution.py:160
  5.8 7.6 %collective-permute-start.5 = (f32[4,128,128]{2,1,0:T(8,128)S(1)}, f32[4,128,128]{2,1,0:T(8,128)S(1)}, u32[]{:S(2)}, u32[]{:S(2)}) collective-permute-start(f32[4,128,128]{2,1,0:T(8,128)S(1)} %add.25), channel_id=1, source_target_pairs={{0,4},{13,9},{8,12},{5,1},{1,0},{4,5},{9,8},{12,13},{2,6},{15,11},... | collective-permute-start | bytes 786440 | tf_op jit(solution)/shard_map/ppermute | solution.py:160
  10.7 5.2 %collective-permute-start.3 = (f32[4,128,128]{2,1,0:T(8,128)S(1)}, f32[4,128,128]{2,1,0:T(8,128)S(1)}, u32[]{:S(2)}, u32[]{:S(2)}) collective-permute-start(f32[4,128,128]{2,1,0:T(8,128)S(1)} %add.26), channel_id=1, source_target_pairs={{4,8},{9,5},{0,0},{1,1},{5,4},{8,9},{12,12},{13,13},{6,10},{11,7},... | collective-permute-start | bytes 786440 | tf_op jit(solution)/shard_map/ppermute | solution.py:160
  13.4 11.1 %collective-permute-start.6 = (f32[4,128,128]{2,1,0:T(8,128)S(1)}, f32[4,128,128]{2,1,0:T(8,128)S(1)}, u32[]{:S(2)}, u32[]{:S(2)}) collective-permute-start(f32[4,128,128]{2,1,0:T(8,128)S(1)} %add.28), channel_id=1, source_target_pairs={{4,12},{9,1},{0,4},{13,9},{1,0},{5,5},{8,8},{12,13},{6,14},{11,3},... | collective-permute-start | bytes 786440 | tf_op jit(solution)/shard_map/ppermute | solution.py:160
  15.9 8.7 %collective-permute-start.4 = (f32[4,128,128]{2,1,0:T(8,128)S(1)}, f32[4,128,128]{2,1,0:T(8,128)S(1)}, u32[]{:S(2)}, u32[]{:S(2)}) collective-permute-start(f32[4,128,128]{2,1,0:T(8,128)S(1)} %add.27), channel_id=1, source_target_pairs={{8,12},{5,1},{0,4},{13,9},{1,0},{4,5},{9,8},{12,13},{10,14},{7,3},... | collective-permute-start | bytes 786440 | tf_op jit(solution)/shard_map/ppermute | solution.py:160
  19.7 5.2 %collective-permute-start.7 = (f32[4,128,128]{2,1,0:T(8,128)S(1)}, f32[4,128,128]{2,1,0:T(8,128)S(1)}, u32[]{:S(2)}, u32[]{:S(2)}) collective-permute-start(f32[4,128,128]{2,1,0:T(8,128)S(1)} %add.28), channel_id=1, source_target_pairs={{4,8},{9,5},{0,0},{1,1},{5,4},{8,9},{12,12},{13,13},{6,10},{11,7},... | collective-permute-start | bytes 786440 | tf_op jit(solution)/shard_map/ppermute | solution.py:160
  24.9 4.3 %collective-permute-start.9 = (f32[4,128,128]{2,1,0:T(8,128)S(1)}, f32[4,128,128]{2,1,0:T(8,128)S(1)}, u32[]{:S(2)}, u32[]{:S(2)}) collective-permute-start(f32[4,128,128]{2,1,0:T(8,128)S(1)} %get-tuple-element.73), channel_id=1, source_target_pairs={{0,1},{1,0},{2,3},{3,2},{4,5},{5,4},{6,7},{7,6},{8,9},{9,8},{10,11... | collective-permute-start | bytes 786440 | tf_op jit(solution)/shard_map/ppermute | solution.py:168
  28.1 1.6 %collective-permute-start.8 = (f32[4,128,128]{2,1,0:T(8,128)S(1)}, f32[4,128,128]{2,1,0:T(8,128)S(1)}, u32[]{:S(2)}, u32[]{:S(2)}) collective-permute-start(f32[4,128,128]{2,1,0:T(8,128)S(1)} %get-tuple-element.75), channel_id=1, source_target_pairs={{0,1},{1,0},{2,3},{3,2},{4,5},{5,4},{6,7},{7,6},{8,9},{9,8},{10,11... | collective-permute-start | bytes 786440 | tf_op jit(solution)/shard_map/ppermute | solution.py:168

commit v6 on v3

--- a/solution.py
+++ b/solution.py
@@ -8,8 +8,8 @@
 from jax.sharding import PartitionSpec as P
 
 DH = 128
-LITTLE = pl.CostEstimate(flops=1, transcendentals=0, bytes_accessed=1)
-PIECES = (1, 2, 5)
+CHUNKS = 2
+PLAN = (2, 1, 3, 1, 1)
 F32 = jnp.float32
 BF16 = jnp.bfloat16
 VMEM = pl.BlockSpec(memory_space=pltpu.VMEM)
@@ -64,8 +64,7 @@
                 state(*pair, keep if give_first else give)
 
 
-def states(core, active, parts, args, filled=()):
-    place = jnp.stack([core, active.astype(jnp.int32)])
+def states(place, parts, args, filled=()):
     outs = [pltpu.VMEM((n, DH, DH), F32) for n in parts]
     result = pl.pallas_call(
         functools.partial(states_kernel, len(filled)),
@@ -76,7 +75,6 @@
         input_output_aliases={5 + i: i for i in range(len(filled))},
         compiler_params=pltpu.CompilerParams(vmem_limit_bytes=8 << 20),
         name="states",
-        cost_estimate=LITTLE,
     )(place, *[pltpu.with_memory_space_constraint(x, pltpu.HBM) for x in args], *filled)
     return result[: 4 + len(parts)], result[4 + len(parts) :]
 
@@ -103,7 +101,6 @@
         out_shape=[pltpu.VMEM((q.shape[0], heads * DH), F32)] * 3,
         compiler_params=pltpu.CompilerParams(vmem_limit_bytes=16 << 20),
         name="intra",
-        cost_estimate=LITTLE,
     )(q, k, v, g)
 
 
@@ -149,8 +146,7 @@
         + [pltpu.SemaphoreType.DMA((3, (sum(parts) + 1) // 2))],
         compiler_params=pltpu.CompilerParams(vmem_limit_bytes=16 << 20),
         name="final",
-        cost_estimate=LITTLE,
-    )(core.reshape(1), k, v, g, *mine, *other, *[x for piece in local for x in piece])
+    )(core, k, v, g, *mine, *other, *[x for piece in local for x in piece])
 
 
 def after(values, *events):
@@ -165,63 +161,69 @@
     return lax.ppermute(value, ("seq", "sub"), pairs)
 
 
-def swap(value, chips=None):
-    if chips is None:
-        return lax.ppermute(value, "sub", [(0, 1), (1, 0)])
-    pairs = [pair for c in chips for pair in ((2 * c, 2 * c + 1), (2 * c + 1, 2 * c))]
-    return lax.ppermute(value, ("seq", "sub"), pairs)
+def swap(value):
+    return lax.ppermute(value, "sub", [(0, 1), (1, 0)])
 
 
 def body(*args):
     chips = lax.axis_size("seq")
     last = chips - 1
-    ends, middle = (0, last), range(1, last)
-    core = lax.axis_index("sub").astype(jnp.int32)
-    chip = lax.axis_index("seq")
+    core, chip = lax.axis_index("sub").astype(jnp.int32), lax.axis_index("seq")
     at_end = jnp.logical_or(chip == 0, chip == last)
     heads = args[0].shape[1] // DH
-    parts = (heads // 2, heads - heads // 2)
-    pieces = PIECES if heads == 8 else (1, 1, heads - 2)
-
-    filled, give = states(core, at_end, parts, args)
-    got_a, got_b = (swap(x, ends) for x in give)
-    first_a, first_b = filled[4] + got_a, filled[5] + got_b
-    arrived_a, arrived_b = (move(x, chips, [(0, 1)]) for x in (first_a, first_b))
-    filled, give = states(
-        core, jnp.logical_not(at_end), parts, args, after(filled, first_a, first_b)
+    chunks = CHUNKS
+    parts = tuple(heads * (c + 1) // chunks - heads * c // chunks for c in range(chunks))
+    slots = 1 + (chips - 2) * chunks
+    plan = PLAN if (heads, slots) == (sum(PLAN), len(PLAN)) else (0,) * (slots - 1) + (heads,)
+    at_end_now = jnp.stack([core, at_end.astype(jnp.int32)])
+    elsewhere = jnp.stack([core, 1 - at_end.astype(jnp.int32)])
+    core = core.reshape(1)
+    at_end, at_end_now, elsewhere, core, *args = lax.optimization_barrier(
+        (at_end, at_end_now, elsewhere, core, *args)
     )
+
+    filled, give = states(at_end_now, parts, args)
+    early = [swap(x) for x in give]
+    first = [x + y for x, y in zip(filled[4:], early)]
+    arrived = [move(x, chips, [(0, 1)]) for x in first]
+    filled, give = states(elsewhere, parts, args, after(filled, *first))
     args, keep = filled[:4], filled[4:]
-    total_a, total_b = (x + y + swap(z, middle) for x, y, z in zip(keep, (got_a, got_b), give))
-    mine_a, mine_b = arrived_a, arrived_b
-    carried_b = move(total_b, chips, [(last - 1, last)])
-    local = [intra(0, pieces[0], *after(args, total_a, total_b))]
-    (arrived_a,) = after((arrived_a,), local[0][0])
-    (arrived_b,) = after((arrived_b,), carried_b)
-    mine_b = mine_b + carried_b
-    for hop in range(1, last):
-        sent_a = total_a + arrived_a
-        arrived_a = move(sent_a, chips, [(hop, hop + 1)])
-        if hop < last - 1:
-            mine_a = mine_a + arrived_a
-            if hop == last - 2:
-                local.append(intra(pieces[0], pieces[1], *after(args, sent_a)))
-                (arrived_b,) = after((arrived_b,), local[1][0])
+    late = [swap(x) for x in give]
+
+    local, pieces = [], []
+
+    def local_piece(count, event):
+        if count:
+            local.append(intra(sum(pieces), count, *after(args, event)))
+            pieces.append(count)
+            event = local[-1][0]
+        return event
+
+    event = local_piece(plan[0], give[-1])
+    mine = [None] * chunks
+    total = [None] * chunks
+    for step in range(1, last):
+        for c in range(chunks):
+            (arrived[c],) = after(arrived[c : c + 1], event)
+            mine[c] = arrived[c] if mine[c] is None else mine[c] + arrived[c]
+            if step == 1:
+                sent = keep[c] + arrived[c]
+                (late[c],) = after(late[c : c + 1], sent)
+                other = jnp.where(at_end, early[c], late[c])
+                total[c] = keep[c] + other
+                sent = sent + other
             else:
-                (arrived_b,) = after((arrived_b,), sent_a)
-            sent_b = total_b + arrived_b
-            if hop == last - 2:
-                mine_b = mine_b + move(sent_b, chips, [(hop, last)])
-            arrived_b = move(sent_b, chips, [(hop, hop + 1)])
-            if hop < last - 2:
-                mine_b = mine_b + arrived_b
-    local.append(intra(sum(pieces[:2]), pieces[2], *after(args, sent_a)))
-    arrived_a, arrived_b = after((arrived_a, arrived_b), local[2][0])
-    mine_a = mine_a + arrived_a
-    mine_b = mine_b + arrived_b
-    other_b = swap(mine_b + keep[1])
-    other_a = swap(mine_a + keep[0])
+                sent = total[c] + arrived[c]
+            arrived[c] = move(sent, chips, [(step, step + 1)])
+            event = local_piece(plan[1 + (step - 1) * chunks + c], sent)
+    other = []
+    for c in range(chunks):
+        (arrived[c],) = after(arrived[c : c + 1], event)
+        mine[c] = mine[c] + arrived[c]
+        event = mine[c] + keep[c]
+        other.append(swap(event))
     q, k, v, g = args
-    return tuple(final(core, parts, pieces, k, v, g, (mine_a, mine_b), (other_a, other_b), local))
+    return tuple(final(core, parts, tuple(pieces), k, v, g, mine, other, local))
 
 
 def solution(mesh):

time: 43.3 us -> 33.4 us (0.77); the launches traced: 42.5 us -> 33.2 us
  starting transfers between devices: 24.5 us -> 16.3 us
  waiting for transfers between devices: 4.17 us -> 2.67 us
  Pallas kernels: 12.3 us -> 12.9 us
    ppermute x4 -> x0, starting transfers between devices: 5.68 us -> none  [swap(): return lax.ppermute(value, ('seq', 'sub'), pairs)]
    ppermute x2 -> x6, starting transfers between devices: 10.4 us -> 7.38 us  [swap(): return lax.ppermute(value, 'sub', [(0, 1), (1, 0)])]
    ppermute x4 -> x0, waiting for transfers between devices: 1.42 us -> none  [swap(): return lax.ppermute(value, ('seq', 'sub'), pairs)]
    ppermute x7 -> x6, waiting for transfers between devices: 1.24 us -> 0.42 us  [move(): return lax.ppermute(value, ('seq', 'sub'), pairs)]
    ppermute x2 -> x6, waiting for transfers between devices: 1.52 us -> 2.25 us  [swap(): return lax.ppermute(value, 'sub', [(0, 1), (1, 0)])]
    pallas_call x3 -> x5, Pallas kernels: 6.24 us -> 6.76 us  [intra(): pl.pallas_call(functools.partial(intra_kernel, first), in_specs=[VMEM] *...]
    ppermute x7 -> x6, starting transfers between devices: 8.42 us -> 8.88 us  [move(): return lax.ppermute(value, ('seq', 'sub'), pairs)]
  transfers between devices with their start and end apart: 13 -> 12, of which waited for: 5 -> 3; matrix products, arithmetic and copies ran while one was open for 1% -> 2% of each run, Pallas kernels for 15% -> 22%
where the time goes in v6:
time: 33.4 us; the launch traced here: 33.2 us
  starting transfers between devices  16.3 us (49%)
  Pallas kernels  12.9 us (39%)
  waiting for transfers between devices  2.67 us (8%)
  between operations  0.86 us (3%)
  other arithmetic  0.58 us (2%)
    ppermute x6, starting transfers between devices, move(): return lax.ppermute(value, ('seq', 'sub'), pairs)  8.88 us
    ppermute x6, starting transfers between devices, swap(): return lax.ppermute(value, 'sub', [(0, 1), (1, 0)])  7.38 us
    pallas_call x5, Pallas kernels, intra(): pl.pallas_call(functools.partial(intra_kernel, first), in_specs=[VMEM] *...  6.76 us
    pallas_call x2, Pallas kernels, states(): pl.pallas_call(functools.partial(states_kernel, len(filled)), in_specs=[S...  3.87 us
    ppermute x6, waiting for transfers between devices, swap(): return lax.ppermute(value, 'sub', [(0, 1), (1, 0)])  2.25 us
    pallas_call x1, Pallas kernels, final(): pl.pallas_call(functools.partial(final_kernel, parts, pieces), in_specs=[...  2.22 us
  transfers between devices with their start and end apart: 12, of which 3 were waited for; matrix products, arithmetic and copies ran while one was open for 2% of the time, Pallas kernels for 22%

profile of v6, /device:TPU:0, one launch (start us, length us, event | category | flops | bytes accessed | tf_op | source)
XLA Modules:
  0.0 33.2 jit_solution(8202553095595734929)
XLA Ops:
  0.6 0.1 pad_add_fusion
  0.7 3.3 %states.2 = (bf16[512,1024]{1,0:T(8,128)(2,1)S(1)}, bf16[512,1024]{1,0:T(8,128)(2,1)S(1)}, bf16[512,1024]{1,0:T(8,128)(2,1)S(1)}, bf16[512,1024]{1,0:T(8,128)(2,...) custom-call(s32[2]{0:T(128)S(1)} %get-tuple-element.82.place, ...), custom_call_target="tpu_custom_call" | custom-call | tf_op jit(solution)/shard_map/states/pallas_call | solution.py:69
  4.0 0.5 %collective-permute-start = (f32[4,128,128]{2,1,0:T(8,128)S(1)}, f32[4,128,128]{2,1,0:T(8,128)S(1)}, u32[]{:S(2)}, u32[]{:S(2)}) collective-permute-start(f32[4,128,128]{2,1,0:T(8,128)S(1)} %get-tuple-element.89), channel_id=1, source_target_pairs={{0,1},{1,0},{2,3},{3,2},{4,5},{5,4},{6,7},{7,6},{8,9},{9,8},{10,11... | collective-permute-start | bytes 786440 | tf_op jit(solution)/shard_map/ppermute | solution.py:165
  4.5 0.1 collective-permute-start.1
  4.6 1.1 %collective-permute-done = f32[4,128,128]{2,1,0:T(8,128)S(1)} collective-permute-done((f32[4,128,128]{2,1,0:T(8,128)S(1)}, f32[4,128,128]{2,1,0:T(8,128)S(1)}, u32[]{:S(2)}, u32[]{:S(2)}) %collective-permute-start) | collective-permute-done | bytes 262176 | tf_op jit(solution)/shard_map/ppermute | solution.py:165
  5.7 2.2 %collective-permute-start.2 = (f32[4,128,128]{2,1,0:T(8,128)S(1)}, f32[4,128,128]{2,1,0:T(8,128)S(1)}, u32[]{:S(2)}, u32[]{:S(2)}) collective-permute-start(f32[4,128,128]{2,1,0:T(8,128)S(1)} %add.48), channel_id=1, source_target_pairs={{0,4},{13,9},{2,6},{15,11},{16,20},{29,25},{18,22},{31,27}} | collective-permute-start | bytes 786440 | tf_op jit(solution)/shard_map/ppermute | solution.py:161
  7.9 0.6 %states.3 = (bf16[512,1024]{1,0:T(8,128)(2,1)S(1)}, bf16[512,1024]{1,0:T(8,128)(2,1)S(1)}, bf16[512,1024]{1,0:T(8,128)(2,1)S(1)}, bf16[512,1024]{1,0:T(8,128)(2,...) custom-call(s32[2]{0:T(128)S(1)} %get-tuple-element.77.place, ...), custom_call_target="tpu_custom_call", output_to_operand_aliasing={{0}: (5, {}), {1}: (6, {}), {2}: (7, {}), {3}: (8, {}), {4}... | custom-call | tf_op jit(solution)/shard_map/states/pallas_call | solution.py:69
  8.6 4.0 %collective-permute-start.5 = (f32[4,128,128]{2,1,0:T(8,128)S(1)}, f32[4,128,128]{2,1,0:T(8,128)S(1)}, u32[]{:S(2)}, u32[]{:S(2)}) collective-permute-start(f32[4,128,128]{2,1,0:T(8,128)S(1)} %add.49), channel_id=1, source_target_pairs={{0,4},{13,9},{2,6},{15,11},{16,20},{29,25},{18,22},{31,27}} | collective-permute-start | bytes 786440 | tf_op jit(solution)/shard_map/ppermute | solution.py:161
  12.7 1.6 %intra.5 = (f32[512,256]{1,0:T(8,128)S(1)}, f32[512,256]{1,0:T(8,128)S(1)}, f32[512,256]{1,0:T(8,128)S(1)}) custom-call(bf16[512,1024]{1,0:T(8,128)(2,1)S(1)} %get-tuple-element.132.q, bf16[512,1024]{1,0:T(8,128)(2,1)S(1)} %get-tuple-element.133.k, bf16[512,1024]{1,0:T(8,128)(2,1)S(1)} %get-tuple-element.134.v, bf16[512,1024]{1,0:T(8,128)(2,1)S(1)} %get-tuple-element.135.g), custom_call_target="tpu_custom_call" | custom-call | tf_op jit(solution)/shard_map/intra/pallas_call | solution.py:97
  14.4 0.7 %collective-permute-start.4 = (f32[4,128,128]{2,1,0:T(8,128)S(1)}, f32[4,128,128]{2,1,0:T(8,128)S(1)}, u32[]{:S(2)}, u32[]{:S(2)}) collective-permute-start(f32[4,128,128]{2,1,0:T(8,128)S(1)} %fusion), channel_id=1, source_target_pairs={{4,8},{9,5},{6,10},{11,7},{20,24},{25,21},{22,26},{27,23}} | collective-permute-start | bytes 786440 | tf_op jit(solution)/shard_map/ppermute | solution.py:161
  15.1 0.9 %intra.6 = (f32[512,128]{1,0:T(8,128)S(1)}, f32[512,128]{1,0:T(8,128)S(1)}, f32[512,128]{1,0:T(8,128)S(1)}) custom-call(bf16[512,1024]{1,0:T(8,128)(2,1)S(1)} %get-tuple-element.132.q, bf16[512,1024]{1,0:T(8,128)(2,1)S(1)} %get-tuple-element.133.k, bf16[512,1024]{1,0:T(8,128)(2,1)S(1)} %get-tuple-element.134.v, bf16[512,1024]{1,0:T(8,128)(2,1)S(1)} %get-tuple-element.135.g), custom_call_target="tpu_custom_call" | custom-call | tf_op jit(solution)/shard_map/intra/pallas_call | solution.py:97
  16.1 0.4 %collective-permute-done.5 = f32[4,128,128]{2,1,0:T(8,128)S(1)} collective-permute-done((f32[4,128,128]{2,1,0:T(8,128)S(1)}, f32[4,128,128]{2,1,0:T(8,128)S(1)}, u32[]{:S(2)}, u32[]{:S(2)}) %collective-permute-start.5) | collective-permute-done | bytes 262176 | tf_op jit(solution)/shard_map/ppermute | solution.py:161
  16.6 0.7 %collective-permute-start.8 = (f32[4,128,128]{2,1,0:T(8,128)S(1)}, f32[4,128,128]{2,1,0:T(8,128)S(1)}, u32[]{:S(2)}, u32[]{:S(2)}) collective-permute-start(f32[4,128,128]{2,1,0:T(8,128)S(1)} %fusion.1), channel_id=1, source_target_pairs={{4,8},{9,5},{6,10},{11,7},{20,24},{25,21},{22,26},{27,23}} | collective-permute-start | bytes 786440 | tf_op jit(solution)/shard_map/ppermute | solution.py:161
  17.3 2.3 %intra.7 = (f32[512,384]{1,0:T(8,128)S(1)}, f32[512,384]{1,0:T(8,128)S(1)}, f32[512,384]{1,0:T(8,128)S(1)}) custom-call(bf16[512,1024]{1,0:T(8,128)(2,1)S(1)} %get-tuple-element.132.q, bf16[512,1024]{1,0:T(8,128)(2,1)S(1)} %get-tuple-element.133.k, bf16[512,1024]{1,0:T(8,128)(2,1)S(1)} %get-tuple-element.134.v, bf16[512,1024]{1,0:T(8,128)(2,1)S(1)} %get-tuple-element.135.g), custom_call_target="tpu_custom_call" | custom-call | tf_op jit(solution)/shard_map/intra/pallas_call | solution.py:97
  19.6 0.1 add_add_fusion.2
  19.7 0.7 %collective-permute-start.7 = (f32[4,128,128]{2,1,0:T(8,128)S(1)}, f32[4,128,128]{2,1,0:T(8,128)S(1)}, u32[]{:S(2)}, u32[]{:S(2)}) collective-permute-start(f32[4,128,128]{2,1,0:T(8,128)S(1)} %add_add_fusion.2), channel_id=1, source_target_pairs={{8,12},{5,1},{10,14},{7,3},{24,28},{21,17},{26,30},{23,19}} | collective-permute-start | bytes 786440 | tf_op jit(solution)/shard_map/ppermute | solution.py:161
  20.3 0.9 %intra.8 = (f32[512,128]{1,0:T(8,128)S(1)}, f32[512,128]{1,0:T(8,128)S(1)}, f32[512,128]{1,0:T(8,128)S(1)}) custom-call(bf16[512,1024]{1,0:T(8,128)(2,1)S(1)} %get-tuple-element.132.q, bf16[512,1024]{1,0:T(8,128)(2,1)S(1)} %get-tuple-element.133.k, bf16[512,1024]{1,0:T(8,128)(2,1)S(1)} %get-tuple-element.134.v, bf16[512,1024]{1,0:T(8,128)(2,1)S(1)} %get-tuple-element.135.g), custom_call_target="tpu_custom_call" | custom-call | tf_op jit(solution)/shard_map/intra/pallas_call | solution.py:97
  21.3 0.1 add_add_fusion.1
  21.4 0.7 %collective-permute-start.9 = (f32[4,128,128]{2,1,0:T(8,128)S(1)}, f32[4,128,128]{2,1,0:T(8,128)S(1)}, u32[]{:S(2)}, u32[]{:S(2)}) collective-permute-start(f32[4,128,128]{2,1,0:T(8,128)S(1)} %add_add_fusion.1), channel_id=1, source_target_pairs={{8,12},{5,1},{10,14},{7,3},{24,28},{21,17},{26,30},{23,19}} | collective-permute-start | bytes 786440 | tf_op jit(solution)/shard_map/ppermute | solution.py:161
  22.1 0.9 %intra.9 = (f32[512,128]{1,0:T(8,128)S(1)}, f32[512,128]{1,0:T(8,128)S(1)}, f32[512,128]{1,0:T(8,128)S(1)}) custom-call(bf16[512,1024]{1,0:T(8,128)(2,1)S(1)} %get-tuple-element.132.q, bf16[512,1024]{1,0:T(8,128)(2,1)S(1)} %get-tuple-element.133.k, bf16[512,1024]{1,0:T(8,128)(2,1)S(1)} %get-tuple-element.134.v, bf16[512,1024]{1,0:T(8,128)(2,1)S(1)} %get-tuple-element.135.g), custom_call_target="tpu_custom_call" | custom-call | tf_op jit(solution)/shard_map/intra/pallas_call | solution.py:97
  23.1 3.9 %collective-permute-start.10 = (f32[4,128,128]{2,1,0:T(8,128)S(1)}, f32[4,128,128]{2,1,0:T(8,128)S(1)}, u32[]{:S(2)}, u32[]{:S(2)}) collective-permute-start(f32[4,128,128]{2,1,0:T(8,128)S(1)} %get-tuple-element.151), channel_id=1, source_target_pairs={{0,1},{1,0},{2,3},{3,2},{4,5},{5,4},{6,7},{7,6},{8,9},{9,8},{10,11... | collective-permute-start | bytes 786440 | tf_op jit(solution)/shard_map/ppermute | solution.py:165
  27.1 2.7 %collective-permute-start.11 = (f32[4,128,128]{2,1,0:T(8,128)S(1)}, f32[4,128,128]{2,1,0:T(8,128)S(1)}, u32[]{:S(2)}, u32[]{:S(2)}) collective-permute-start(f32[4,128,128]{2,1,0:T(8,128)S(1)} %get-tuple-element.149), channel_id=1, source_target_pairs={{0,1},{1,0},{2,3},{3,2},{4,5},{5,4},{6,7},{7,6},{8,9},{9,8},{10,11... | collective-permute-start | bytes 786440 | tf_op jit(solution)/shard_map/ppermute | solution.py:165
  29.8 1.2 %collective-permute-done.11.rest_3_ = f32[4,128,128]{2,1,0:T(8,128)S(1)} collective-permute-done((f32[4,128,128]{2,1,0:T(8,128)S(1)}, f32[4,128,128]{2,1,0:T(8,128)S(1)}, u32[]{:S(2)}, u32[]{:S(2)}) %collective-permute-start.11) | collective-permute-done | bytes 262176 | tf_op jit(solution)/shard_map/ppermute | solution.py:165
  31.0 2.2 %final.1 = (bf16[512,1024]{1,0:T(8,128)(2,1)}, bf16[512,1024]{1,0:T(8,128)(2,1)}, bf16[512,1024]{1,0:T(8,128)(2,1)}) custom-call(s32[1]{0:T(128)} %bitcast.core, bf16[512,1024]{1,0:T(8,128)(2,1)S(1)} %get-tuple-element.133.k, bf16[512,1024]{1,0:T(8,128)(2,1)S(1)} %get-tuple-element.134.v, bf16[512,1024]{1,0:T(8,128)(2,1)S(1)} %get-tuple-element.135.g, ...), custom_call_target="tpu_custom_call" | custom-call | tf_op jit(solution)/shard_map/final/pallas_call | solution.py:140
  (19 shorter events, 0.5 us)
Async XLA Ops:
  4.0 1.7 %collective-permute-start = (f32[4,128,128]{2,1,0:T(8,128)S(1)}, f32[4,128,128]{2,1,0:T(8,128)S(1)}, u32[]{:S(2)}, u32[]{:S(2)}) collective-permute-start(f32[4,128,128]{2,1,0:T(8,128)S(1)} %get-tuple-element.89), channel_id=1, source_target_pairs={{0,1},{1,0},{2,3},{3,2},{4,5},{5,4},{6,7},{7,6},{8,9},{9,8},{10,11... | collective-permute-start | bytes 786440 | tf_op jit(solution)/shard_map/ppermute | solution.py:165
  4.5 3.4 %collective-permute-start.1 = (f32[4,128,128]{2,1,0:T(8,128)S(1)}, f32[4,128,128]{2,1,0:T(8,128)S(1)}, u32[]{:S(2)}, u32[]{:S(2)}) collective-permute-start(f32[4,128,128]{2,1,0:T(8,128)S(1)} %get-tuple-element.90), channel_id=1, source_target_pairs={{0,1},{1,0},{2,3},{3,2},{4,5},{5,4},{6,7},{7,6},{8,9},{9,8},{10,11... | collective-permute-start | bytes 786440 | tf_op jit(solution)/shard_map/ppermute | solution.py:165
  5.7 8.6 %collective-permute-start.2 = (f32[4,128,128]{2,1,0:T(8,128)S(1)}, f32[4,128,128]{2,1,0:T(8,128)S(1)}, u32[]{:S(2)}, u32[]{:S(2)}) collective-permute-start(f32[4,128,128]{2,1,0:T(8,128)S(1)} %add.48), channel_id=1, source_target_pairs={{0,4},{13,9},{2,6},{15,11},{16,20},{29,25},{18,22},{31,27}} | collective-permute-start | bytes 786440 | tf_op jit(solution)/shard_map/ppermute | solution.py:161
  8.6 5.8 %collective-permute-start.3 = (f32[4,128,128]{2,1,0:T(8,128)S(1)}, f32[4,128,128]{2,1,0:T(8,128)S(1)}, u32[]{:S(2)}, u32[]{:S(2)}) collective-permute-start(f32[4,128,128]{2,1,0:T(8,128)S(1)} %get-tuple-element.110), channel_id=1, source_target_pairs={{0,1},{1,0},{2,3},{3,2},{4,5},{5,4},{6,7},{7,6},{8,9},{9,8},{10,11... | collective-permute-start | bytes 786440 | tf_op jit(solution)/shard_map/ppermute | solution.py:165
  8.6 7.8 %collective-permute-start.5 = (f32[4,128,128]{2,1,0:T(8,128)S(1)}, f32[4,128,128]{2,1,0:T(8,128)S(1)}, u32[]{:S(2)}, u32[]{:S(2)}) collective-permute-start(f32[4,128,128]{2,1,0:T(8,128)S(1)} %add.49), channel_id=1, source_target_pairs={{0,4},{13,9},{2,6},{15,11},{16,20},{29,25},{18,22},{31,27}} | collective-permute-start | bytes 786440 | tf_op jit(solution)/shard_map/ppermute | solution.py:161
  12.6 3.9 %collective-permute-start.6 = (f32[4,128,128]{2,1,0:T(8,128)S(1)}, f32[4,128,128]{2,1,0:T(8,128)S(1)}, u32[]{:S(2)}, u32[]{:S(2)}) collective-permute-start(f32[4,128,128]{2,1,0:T(8,128)S(1)} %get-tuple-element.101), channel_id=1, source_target_pairs={{0,1},{1,0},{2,3},{3,2},{4,5},{5,4},{6,7},{7,6},{8,9},{9,8},{10,11... | collective-permute-start | bytes 786440 | tf_op jit(solution)/shard_map/ppermute | solution.py:165
  14.4 5.1 %collective-permute-start.4 = (f32[4,128,128]{2,1,0:T(8,128)S(1)}, f32[4,128,128]{2,1,0:T(8,128)S(1)}, u32[]{:S(2)}, u32[]{:S(2)}) collective-permute-start(f32[4,128,128]{2,1,0:T(8,128)S(1)} %fusion), channel_id=1, source_target_pairs={{4,8},{9,5},{6,10},{11,7},{20,24},{25,21},{22,26},{27,23}} | collective-permute-start | bytes 786440 | tf_op jit(solution)/shard_map/ppermute | solution.py:161
  16.6 4.7 %collective-permute-start.8 = (f32[4,128,128]{2,1,0:T(8,128)S(1)}, f32[4,128,128]{2,1,0:T(8,128)S(1)}, u32[]{:S(2)}, u32[]{:S(2)}) collective-permute-start(f32[4,128,128]{2,1,0:T(8,128)S(1)} %fusion.1), channel_id=1, source_target_pairs={{4,8},{9,5},{6,10},{11,7},{20,24},{25,21},{22,26},{27,23}} | collective-permute-start | bytes 786440 | tf_op jit(solution)/shard_map/ppermute | solution.py:161
  19.7 3.4 %collective-permute-start.7 = (f32[4,128,128]{2,1,0:T(8,128)S(1)}, f32[4,128,128]{2,1,0:T(8,128)S(1)}, u32[]{:S(2)}, u32[]{:S(2)}) collective-permute-start(f32[4,128,128]{2,1,0:T(8,128)S(1)} %add_add_fusion.2), channel_id=1, source_target_pairs={{8,12},{5,1},{10,14},{7,3},{24,28},{21,17},{26,30},{23,19}} | collective-permute-start | bytes 786440 | tf_op jit(solution)/shard_map/ppermute | solution.py:161
  21.4 5.6 %collective-permute-start.9 = (f32[4,128,128]{2,1,0:T(8,128)S(1)}, f32[4,128,128]{2,1,0:T(8,128)S(1)}, u32[]{:S(2)}, u32[]{:S(2)}) collective-permute-start(f32[4,128,128]{2,1,0:T(8,128)S(1)} %add_add_fusion.1), channel_id=1, source_target_pairs={{8,12},{5,1},{10,14},{7,3},{24,28},{21,17},{26,30},{23,19}} | collective-permute-start | bytes 786440 | tf_op jit(solution)/shard_map/ppermute | solution.py:161
  23.1 6.7 %collective-permute-start.10 = (f32[4,128,128]{2,1,0:T(8,128)S(1)}, f32[4,128,128]{2,1,0:T(8,128)S(1)}, u32[]{:S(2)}, u32[]{:S(2)}) collective-permute-start(f32[4,128,128]{2,1,0:T(8,128)S(1)} %get-tuple-element.151), channel_id=1, source_target_pairs={{0,1},{1,0},{2,3},{3,2},{4,5},{5,4},{6,7},{7,6},{8,9},{9,8},{10,11... | collective-permute-start | bytes 786440 | tf_op jit(solution)/shard_map/ppermute | solution.py:165
  27.1 3.9 %collective-permute-start.11 = (f32[4,128,128]{2,1,0:T(8,128)S(1)}, f32[4,128,128]{2,1,0:T(8,128)S(1)}, u32[]{:S(2)}, u32[]{:S(2)}) collective-permute-start(f32[4,128,128]{2,1,0:T(8,128)S(1)} %get-tuple-element.149), channel_id=1, source_target_pairs={{0,1},{1,0},{2,3},{3,2},{4,5},{5,4},{6,7},{7,6},{8,9},{9,8},{10,11... | collective-permute-start | bytes 786440 | tf_op jit(solution)/shard_map/ppermute | solution.py:165

commit v7 on v4

v7 whole, which is shorter than its diff:
```python
import functools

import jax
import jax.numpy as jnp
from jax import lax
from jax.experimental import pallas as pl
from jax.experimental.pallas import tpu as pltpu
from jax.sharding import PartitionSpec as P

DH = 128
CHUNKS = 4
PLAN = (3, 0, 0, 0, 0, 1, 1, 1, 2)
F32 = jnp.float32
BF16 = jnp.bfloat16
VMEM = pl.BlockSpec(memory_space=pltpu.VMEM)
HBM = pl.BlockSpec(memory_space=pltpu.HBM)
SMEM = pl.BlockSpec(memory_space=pltpu.SMEM)


def product(left, right, left_axis, right_axis):
    return lax.dot_general(
        left, right, (((left_axis,), (right_axis,)), ((), ())), preferred_element_type=F32
    )


def head_columns(head):
    return slice(head * DH, (head + 1) * DH)


def states_kernel(core, q_hbm, k_hbm, v_hbm, g_hbm, q, k, v, g, *rest):
    chunks = (len(rest) - 1) // 2
    keep, give, sems = rest[:chunks], rest[chunks : 2 * chunks], rest[-1]
    copies = [
        pltpu.make_async_copy(source, target, sems.at[i])
        for i, (source, target) in enumerate(zip((q_hbm, k_hbm, v_hbm, g_hbm), (q, k, v, g)))
    ]
    for c in (1, 2, 0, 3):
        copies[c].start()
    half = q.shape[1] // 2
    for left, right, place in ((1, 2, 0), (0, 3, 1)):
        copies[left].wait()
        copies[right].wait()
        x, y = (q, k, v, g)[left], (q, k, v, g)[right]
        for outs, start in ((give, (1 - core[0]) * half), (keep, core[0] * half)):
            h = 0
            for out in outs:
                count = out.shape[0] // 2
                for i in range(count):
                    c = pl.ds(pl.multiple_of(start + h * DH, DH), DH)
                    out[place * count + i] = product(x[:, c], y[:, c], 0, 0)
                    h += 1


def states(core, parts, q, k, v, g):
    outs = [pltpu.VMEM((2 * n, DH, DH), F32) for n in parts] * 2
    result = pl.pallas_call(
        states_kernel,
        in_specs=[SMEM] + [HBM] * 4,
        out_specs=[VMEM] * (4 + len(outs)),
        out_shape=[pltpu.VMEM(q.shape, BF16)] * 4 + outs,
        scratch_shapes=[pltpu.SemaphoreType.DMA((4,))],
        compiler_params=pltpu.CompilerParams(vmem_limit_bytes=8 << 20),
        name="states",
    )(core, *[pltpu.with_memory_space_constraint(x, pltpu.HBM) for x in (q, k, v, g)])
    return result[:4], result[4 : 4 + len(parts)], result[4 + len(parts) :]


def intra_kernel(first, q, k, v, g, dq, dk, dv):
    rows = q.shape[0]
    row = lax.broadcasted_iota(jnp.int32, (rows, rows), 0)
    col = lax.broadcasted_iota(jnp.int32, (rows, rows), 1)
    for h in range(dq.shape[1] // DH):
        c, o = head_columns(first + h), head_columns(h)
        qh, kh, vh, gh = q[:, c], k[:, c], v[:, c], g[:, c]
        grad_scores = jnp.where(row >= col, product(gh, vh, 1, 1), 0.0).astype(BF16)
        dq[:, o] = product(grad_scores, kh, 1, 0)
        dk[:, o] = product(grad_scores, qh, 0, 0)
        attn_scores = jnp.where(row <= col, product(kh, qh, 1, 1), 0.0).astype(BF16)
        dv[:, o] = product(attn_scores, gh, 1, 0)


def intra(first, heads, q, k, v, g):
    return pl.pallas_call(
        functools.partial(intra_kernel, first),
        in_specs=[VMEM] * 4,
        out_specs=[VMEM] * 3,
        out_shape=[pltpu.VMEM((q.shape[0], heads * DH), F32)] * 3,
        compiler_params=pltpu.CompilerParams(vmem_limit_bytes=16 << 20),
        name="intra",
    )(q, k, v, g)


def final_kernel(parts, pieces, core, k, v, g, *rest):
    count = len(parts)
    own, other, rest = rest[:count], rest[count : 2 * count], rest[2 * count :]
    local, rest = rest[: 3 * len(pieces)], rest[3 * len(pieces) :]
    (targets, outs, sems) = rest[:3], rest[3:6], rest[6]
    of_part = [(half, p, i) for half in (0, 1) for p, n in enumerate(parts) for i in range(n)]
    of_piece = [(p, i) for p, n in enumerate(pieces) for i in range(n)]
    heads = len(of_part)
    copies = []
    for h in range(heads):
        (half, part, i), (piece, j) = of_part[h], of_piece[h]
        c, o = head_columns(h), head_columns(j)
        mine = core[0] == half
        prefix, suffix = (
            jnp.where(mine, own[part][n], other[part][n]).astype(BF16)
            for n in (i, parts[part] + i)
        )
        local_q, local_k, local_v = (x[:, o] for x in local[3 * piece : 3 * piece + 3])
        outs[0][:, c] = (local_q + product(g[:, c], prefix, 1, 1)).astype(BF16)
        outs[1][:, c] = (local_k + product(v[:, c], suffix, 1, 1)).astype(BF16)
        outs[2][:, c] = (local_v + product(k[:, c], suffix, 1, 0)).astype(BF16)
        if h % 2 == 1 or h == heads - 1:
            cc = slice((h - h % 2) * DH, (h + 1) * DH)
            for n in range(3):
                copy = pltpu.make_async_copy(
                    outs[n].at[:, cc], targets[n].at[:, cc], sems.at[n, h // 2]
                )
                copy.start()
                copies.append(copy)
    for copy in copies:
        copy.wait()


def final(core, parts, pieces, k, v, g, own, other, local):
    shape = jax.ShapeDtypeStruct(k.shape, BF16)
    return pl.pallas_call(
        functools.partial(final_kernel, parts, pieces),
        in_specs=[SMEM] + [VMEM] * (3 + 2 * len(parts) + 3 * len(pieces)),
        out_specs=[HBM] * 3,
        out_shape=[shape] * 3,
        scratch_shapes=[pltpu.VMEM(k.shape, BF16)] * 3
        + [pltpu.SemaphoreType.DMA((3, (2 * sum(parts) + 1) // 2))],
        compiler_params=pltpu.CompilerParams(vmem_limit_bytes=16 << 20),
        name="final",
    )(core, k, v, g, *own, *other, *[x for piece in local for x in piece])


def after(values, *events):
    values = tuple(values)
    return lax.optimization_barrier(values + tuple(events))[: len(values)]


def swap(value):
    return lax.ppermute(value, "sub", [(0, 1), (1, 0)])


def exchange(value, chips, step):
    partner = {}
    for low in (step, chips - 2 - step):
        for core in (0, 1):
            a, b = 2 * low + core, 2 * low + 2 + core
            partner[a], partner[b] = b, a
    pairs = [(d, partner.get(d, d ^ 1)) for d in range(2 * chips)]
    return lax.ppermute(value, ("seq", "sub"), pairs)


def body(*args):
    chips = lax.axis_size("seq")
    core, chip = lax.axis_index("sub").astype(jnp.int32), lax.axis_index("seq")
    heads = args[0].shape[1] // DH
    chunks = min(CHUNKS, heads // 2)
    parts = tuple(
        heads // 2 * (c + 1) // chunks - heads // 2 * c // chunks for c in range(chunks)
    )
    slots = 1 + (chips - 2) * chunks
    plan = PLAN if (heads, slots) == (sum(PLAN), len(PLAN)) else (0,) * (slots - 1) + (heads,)
    at = [chip == c for c in range(chips)]
    core, first_core, *rest = lax.optimization_barrier((core.reshape(1), core == 0, *at, *args))
    at, args = rest[:chips], rest[chips:]
    args, keep, give = states(core, parts, *args)
    got = [swap(x) for x in give]
    total = [None] * chunks
    local, pieces = [], []

    def local_piece(count, event):
        if count:
            local.append(intra(sum(pieces), count, *after(args, event)))
            pieces.append(count)
            event = local[-1][0]
        return event

    prefix = [jnp.zeros_like(x[:n]) for x, n in zip(keep, parts)]
    suffix = list(prefix)
    arrived = [None] * chunks
    event = None
    for step in range(chips):
        if step == 1:
            event = local_piece(plan[0], event)
        for c, n in enumerate(parts):
            if step == 0:
                if c:
                    (got[c],) = after(got[c : c + 1], event)
                total[c] = keep[c] + got[c]
            else:
                (arrived[c],) = after(arrived[c : c + 1], event)
                prefix[c] = jnp.where(at[step], arrived[c], prefix[c])
                suffix[c] = jnp.where(at[chips - 1 - step], arrived[c], suffix[c])
            if step == chips - 1:
                event = prefix[c]
                continue
            sent = jnp.where(at[step], total[c][:n], total[c][n:])
            if step:
                sent = sent + arrived[c]
            arrived[c] = exchange(sent, chips, step)
            event = sent
            if step:
                event = local_piece(plan[1 + (step - 1) * chunks + c], sent)
    own, other = [], []
    for c, n in enumerate(parts):
        zero = jnp.zeros_like(prefix[c])
        own.append(
            jnp.concatenate(
                [
                    prefix[c] + jnp.where(first_core, zero, got[c][:n]),
                    suffix[c] + jnp.where(first_core, got[c][n:], zero),
                ]
            )
        )
        other.append(
            swap(
                jnp.concatenate(
                    [
                        prefix[c] + jnp.where(first_core, keep[c][:n], zero),
                        suffix[c] + jnp.where(first_core, zero, keep[c][n:]),
                    ]
                )
            )
        )
    q, k, v, g = args
    return tuple(final(core, parts, tuple(pieces), k, v, g, own, other, local))


def solution(mesh):
    placed = P(("rep", "seq", "sub"), "head")
    return jax.shard_map(
        body, mesh=mesh, in_specs=(placed,) * 4, out_specs=(placed,) * 3, check_vma=False
    )
```

time: 43.4 us -> 34.4 us (0.79)
  the two profiles are of different devices: /device:TPU:25 before, /device:TPU:0 now
where the time goes in v7:
time: 34.4 us; the launch traced here: 34.2 us
  starting transfers between devices  16.7 us (49%)
  Pallas kernels  12.2 us (35%)
  waiting for transfers between devices  3.79 us (11%)
  between operations  0.95 us (3%)
  other arithmetic  0.53 us (2%)
    ppermute x12, starting transfers between devices, exchange(): return lax.ppermute(value, ('seq', 'sub'), pairs)  14.4 us
    pallas_call x5, Pallas kernels, intra(): pl.pallas_call(functools.partial(intra_kernel, first), in_specs=[VMEM] *...  6.74 us
    pallas_call x1, Pallas kernels, states(): pl.pallas_call(states_kernel, in_specs=[SMEM] + [HBM] * 4, out_specs=[VME...  3.24 us
    ppermute x12, waiting for transfers between devices, exchange(): return lax.ppermute(value, ('seq', 'sub'), pairs)  2.51 us
    ppermute x8, starting transfers between devices, swap(): return lax.ppermute(value, 'sub', [(0, 1), (1, 0)])  2.37 us
    pallas_call x1, Pallas kernels, final(): pl.pallas_call(functools.partial(final_kernel, parts, pieces), in_specs=[...  2.24 us
    ppermute x8, waiting for transfers between devices, swap(): return lax.ppermute(value, 'sub', [(0, 1), (1, 0)])  1.28 us
  transfers between devices with their start and end apart: 20, of which 7 were waited for; matrix products, arithmetic and copies ran while one was open for 1% of the time, Pallas kernels for 20%

profile of v7, /device:TPU:0, one launch (start us, length us, event | category | flops | bytes accessed | tf_op | source)
XLA Modules:
  0.0 34.2 jit_solution(9005366425038918586)
XLA Ops:
  0.6 3.2 %states.1 = (bf16[512,1024]{1,0:T(8,128)(2,1)S(1)}, bf16[512,1024]{1,0:T(8,128)(2,1)S(1)}, bf16[512,1024]{1,0:T(8,128)(2,1)S(1)}, bf16[512,1024]{1,0:T(8,128)(2,...) custom-call(s32[1]{0:T(128)} %bitcast.core, ...), custom_call_target="tpu_custom_call" | custom-call | tf_op jit(solution)/shard_map/states/pallas_call | solution.py:56
  3.9 0.5 %collective-permute-start = (f32[2,128,128]{2,1,0:T(8,128)S(1)}, f32[2,128,128]{2,1,0:T(8,128)S(1)}, u32[]{:S(2)}, u32[]{:S(2)}) collective-permute-start(f32[2,128,128]{2,1,0:T(8,128)S(1)} %get-tuple-element.86), channel_id=1, source_target_pairs={{0,1},{1,0},{2,3},{3,2},{4,5},{5,4},{6,7},{7,6},{8,9},{9,8},{10,11... | collective-permute-start | bytes 393224 | tf_op jit(solution)/shard_map/ppermute | solution.py:146
  4.5 0.4 %collective-permute-start.3 = (f32[2,128,128]{2,1,0:T(8,128)S(1)}, f32[2,128,128]{2,1,0:T(8,128)S(1)}, u32[]{:S(2)}, u32[]{:S(2)}) collective-permute-start(f32[2,128,128]{2,1,0:T(8,128)S(1)} %get-tuple-element.93), channel_id=1, source_target_pairs={{0,1},{1,0},{2,3},{3,2},{4,5},{5,4},{6,7},{7,6},{8,9},{9,8},{10,11... | collective-permute-start | bytes 393224 | tf_op jit(solution)/shard_map/ppermute | solution.py:146
  5.0 0.4 %collective-permute-done = f32[2,128,128]{2,1,0:T(8,128)S(1)} collective-permute-done((f32[2,128,128]{2,1,0:T(8,128)S(1)}, f32[2,128,128]{2,1,0:T(8,128)S(1)}, u32[]{:S(2)}, u32[]{:S(2)}) %collective-permute-start) | collective-permute-done | bytes 131104 | tf_op jit(solution)/shard_map/ppermute | solution.py:146
  5.4 3.0 %collective-permute-start.1 = (f32[1,128,128]{2,1,0:T(8,128)S(1)}, f32[1,128,128]{2,1,0:T(8,128)S(1)}, u32[]{:S(2)}, u32[]{:S(2)}) collective-permute-start(f32[1,128,128]{2,1,0:T(8,128)S(1)} %slice_select_fusion.5), channel_id=1, source_target_pairs={{0,4},{1,5},{4,0},{5,1},{8,12},{9,13},{12,8},{13,9},{2,6},{3,7},{6... | collective-permute-start | bytes 196616 | tf_op jit(solution)/shard_map/ppermute | solution.py:156
  8.5 0.7 %collective-permute-start.8 = (f32[1,128,128]{2,1,0:T(8,128)S(1)}, f32[1,128,128]{2,1,0:T(8,128)S(1)}, u32[]{:S(2)}, u32[]{:S(2)}) collective-permute-start(f32[1,128,128]{2,1,0:T(8,128)S(1)} %slice_select_fusion.4), channel_id=1, source_target_pairs={{0,4},{1,5},{4,0},{5,1},{8,12},{9,13},{12,8},{13,9},{2,6},{3,7},{6... | collective-permute-start | bytes 196616 | tf_op jit(solution)/shard_map/ppermute | solution.py:156
  9.2 1.5 %collective-permute-start.7 = (f32[1,128,128]{2,1,0:T(8,128)S(1)}, f32[1,128,128]{2,1,0:T(8,128)S(1)}, u32[]{:S(2)}, u32[]{:S(2)}) collective-permute-start(f32[1,128,128]{2,1,0:T(8,128)S(1)} %slice_select_fusion.3), channel_id=1, source_target_pairs={{0,4},{1,5},{4,0},{5,1},{8,12},{9,13},{12,8},{13,9},{2,6},{3,7},{6... | collective-permute-start | bytes 196616 | tf_op jit(solution)/shard_map/ppermute | solution.py:156
  10.7 0.7 %collective-permute-start.6 = (f32[1,128,128]{2,1,0:T(8,128)S(1)}, f32[1,128,128]{2,1,0:T(8,128)S(1)}, u32[]{:S(2)}, u32[]{:S(2)}) collective-permute-start(f32[1,128,128]{2,1,0:T(8,128)S(1)} %slice_select_fusion.2), channel_id=1, source_target_pairs={{0,4},{1,5},{4,0},{5,1},{8,12},{9,13},{12,8},{13,9},{2,6},{3,7},{6... | collective-permute-start | bytes 196616 | tf_op jit(solution)/shard_map/ppermute | solution.py:156
  11.4 2.3 %intra.5 = (f32[512,384]{1,0:T(8,128)S(1)}, f32[512,384]{1,0:T(8,128)S(1)}, f32[512,384]{1,0:T(8,128)S(1)}) custom-call(bf16[512,1024]{1,0:T(8,128)(2,1)S(1)} %get-tuple-element.127.q, bf16[512,1024]{1,0:T(8,128)(2,1)S(1)} %get-tuple-element.128.k, bf16[512,1024]{1,0:T(8,128)(2,1)S(1)} %get-tuple-element.129.v, bf16[512,1024]{1,0:T(8,128)(2,1)S(1)} %get-tuple-element.130.g), custom_call_target="tpu_custom_call" | custom-call | tf_op jit(solution)/shard_map/intra/pallas_call | solution.py:83
  13.8 0.5 %collective-permute-start.12 = (f32[1,128,128]{2,1,0:T(8,128)S(1)}, f32[1,128,128]{2,1,0:T(8,128)S(1)}, u32[]{:S(2)}, u32[]{:S(2)}) collective-permute-start(f32[1,128,128]{2,1,0:T(8,128)S(1)} %select_add_fusion.17), channel_id=1, source_target_pairs={{0,1},{1,0},{4,8},{5,9},{8,4},{9,5},{12,13},{13,12},{2,3},{3,2},{6... | collective-permute-start | bytes 196616 | tf_op jit(solution)/shard_map/ppermute | solution.py:156
  14.8 0.6 %collective-permute-done.6 = f32[1,128,128]{2,1,0:T(8,128)S(1)} collective-permute-done((f32[1,128,128]{2,1,0:T(8,128)S(1)}, f32[1,128,128]{2,1,0:T(8,128)S(1)}, u32[]{:S(2)}, u32[]{:S(2)}) %collective-permute-start.6) | collective-permute-done | bytes 65568 | tf_op jit(solution)/shard_map/ppermute | solution.py:156
  15.5 4.7 %collective-permute-start.9 = (f32[1,128,128]{2,1,0:T(8,128)S(1)}, f32[1,128,128]{2,1,0:T(8,128)S(1)}, u32[]{:S(2)}, u32[]{:S(2)}) collective-permute-start(f32[1,128,128]{2,1,0:T(8,128)S(1)} %select_add_fusion.21), channel_id=1, source_target_pairs={{0,4},{1,5},{4,0},{5,1},{8,12},{9,13},{12,8},{13,9},{2,6},{3,7},{6... | collective-permute-start | bytes 196616 | tf_op jit(solution)/shard_map/ppermute | solution.py:156
  20.2 0.9 %intra.6 = (f32[512,128]{1,0:T(8,128)S(1)}, f32[512,128]{1,0:T(8,128)S(1)}, f32[512,128]{1,0:T(8,128)S(1)}) custom-call(bf16[512,1024]{1,0:T(8,128)(2,1)S(1)} %get-tuple-element.127.q, bf16[512,1024]{1,0:T(8,128)(2,1)S(1)} %get-tuple-element.128.k, bf16[512,1024]{1,0:T(8,128)(2,1)S(1)} %get-tuple-element.129.v, bf16[512,1024]{1,0:T(8,128)(2,1)S(1)} %get-tuple-element.130.g), custom_call_target="tpu_custom_call" | custom-call | tf_op jit(solution)/shard_map/intra/pallas_call | solution.py:83
  21.2 0.9 %collective-permute-start.13 = (f32[1,128,128]{2,1,0:T(8,128)S(1)}, f32[1,128,128]{2,1,0:T(8,128)S(1)}, u32[]{:S(2)}, u32[]{:S(2)}) collective-permute-start(f32[1,128,128]{2,1,0:T(8,128)S(1)} %select_add_fusion.14), channel_id=1, source_target_pairs={{0,4},{1,5},{4,0},{5,1},{8,12},{9,13},{12,8},{13,9},{2,6},{3,7},{6... | collective-permute-start | bytes 196616 | tf_op jit(solution)/shard_map/ppermute | solution.py:156
  22.1 0.9 %intra.7 = (f32[512,128]{1,0:T(8,128)S(1)}, f32[512,128]{1,0:T(8,128)S(1)}, f32[512,128]{1,0:T(8,128)S(1)}) custom-call(bf16[512,1024]{1,0:T(8,128)(2,1)S(1)} %get-tuple-element.127.q, bf16[512,1024]{1,0:T(8,128)(2,1)S(1)} %get-tuple-element.128.k, bf16[512,1024]{1,0:T(8,128)(2,1)S(1)} %get-tuple-element.129.v, bf16[512,1024]{1,0:T(8,128)(2,1)S(1)} %get-tuple-element.130.g), custom_call_target="tpu_custom_call" | custom-call | tf_op jit(solution)/shard_map/intra/pallas_call | solution.py:83
  23.1 1.2 %collective-permute-start.14 = (f32[1,128,128]{2,1,0:T(8,128)S(1)}, f32[1,128,128]{2,1,0:T(8,128)S(1)}, u32[]{:S(2)}, u32[]{:S(2)}) collective-permute-start(f32[1,128,128]{2,1,0:T(8,128)S(1)} %select_add_fusion.15), channel_id=1, source_target_pairs={{0,4},{1,5},{4,0},{5,1},{8,12},{9,13},{12,8},{13,9},{2,6},{3,7},{6... | collective-permute-start | bytes 196616 | tf_op jit(solution)/shard_map/ppermute | solution.py:156
  24.3 0.9 %intra.8 = (f32[512,128]{1,0:T(8,128)S(1)}, f32[512,128]{1,0:T(8,128)S(1)}, f32[512,128]{1,0:T(8,128)S(1)}) custom-call(bf16[512,1024]{1,0:T(8,128)(2,1)S(1)} %get-tuple-element.127.q, bf16[512,1024]{1,0:T(8,128)(2,1)S(1)} %get-tuple-element.128.k, bf16[512,1024]{1,0:T(8,128)(2,1)S(1)} %get-tuple-element.129.v, bf16[512,1024]{1,0:T(8,128)(2,1)S(1)} %get-tuple-element.130.g), custom_call_target="tpu_custom_call" | custom-call | tf_op jit(solution)/shard_map/intra/pallas_call | solution.py:83
  25.3 0.9 %collective-permute-start.15 = (f32[1,128,128]{2,1,0:T(8,128)S(1)}, f32[1,128,128]{2,1,0:T(8,128)S(1)}, u32[]{:S(2)}, u32[]{:S(2)}) collective-permute-start(f32[1,128,128]{2,1,0:T(8,128)S(1)} %select_add_fusion.16), channel_id=1, source_target_pairs={{0,4},{1,5},{4,0},{5,1},{8,12},{9,13},{12,8},{13,9},{2,6},{3,7},{6... | collective-permute-start | bytes 196616 | tf_op jit(solution)/shard_map/ppermute | solution.py:156
  26.2 1.6 %intra.9 = (f32[512,256]{1,0:T(8,128)S(1)}, f32[512,256]{1,0:T(8,128)S(1)}, f32[512,256]{1,0:T(8,128)S(1)}) custom-call(bf16[512,1024]{1,0:T(8,128)(2,1)S(1)} %get-tuple-element.127.q, bf16[512,1024]{1,0:T(8,128)(2,1)S(1)} %get-tuple-element.128.k, bf16[512,1024]{1,0:T(8,128)(2,1)S(1)} %get-tuple-element.129.v, bf16[512,1024]{1,0:T(8,128)(2,1)S(1)} %get-tuple-element.130.g), custom_call_target="tpu_custom_call" | custom-call | tf_op jit(solution)/shard_map/intra/pallas_call | solution.py:83
  28.1 1.6 %collective-permute-done.15 = f32[1,128,128]{2,1,0:T(8,128)S(1)} collective-permute-done((f32[1,128,128]{2,1,0:T(8,128)S(1)}, f32[1,128,128]{2,1,0:T(8,128)S(1)}, u32[]{:S(2)}, u32[]{:S(2)}) %collective-permute-start.15) | collective-permute-done | bytes 65568 | tf_op jit(solution)/shard_map/ppermute | solution.py:156
  29.8 0.6 %collective-permute-start.18 = (f32[2,128,128]{2,1,0:T(8,128)S(1)}, f32[2,128,128]{2,1,0:T(8,128)S(1)}, u32[]{:S(2)}, u32[]{:S(2)}) collective-permute-start(f32[2,128,128]{2,1,0:T(8,128)S(1)} %pad_maximum_fusion.6), channel_id=1, source_target_pairs={{0,1},{1,0},{2,3},{3,2},{4,5},{5,4},{6,7},{7,6},{8,9},{9,8},{10,11... | collective-permute-start | bytes 393224 | tf_op jit(solution)/shard_map/ppermute | solution.py:146
  30.5 0.6 %collective-permute-start.16 = (f32[2,128,128]{2,1,0:T(8,128)S(1)}, f32[2,128,128]{2,1,0:T(8,128)S(1)}, u32[]{:S(2)}, u32[]{:S(2)}) collective-permute-start(f32[2,128,128]{2,1,0:T(8,128)S(1)} %pad_maximum_fusion.4), channel_id=1, source_target_pairs={{0,1},{1,0},{2,3},{3,2},{4,5},{5,4},{6,7},{7,6},{8,9},{9,8},{10,11... | collective-permute-start | bytes 393224 | tf_op jit(solution)/shard_map/ppermute | solution.py:146
  31.3 0.4 %collective-permute-done.17.rest_5_ = f32[2,128,128]{2,1,0:T(8,128)S(1)} collective-permute-done((f32[2,128,128]{2,1,0:T(8,128)S(1)}, f32[2,128,128]{2,1,0:T(8,128)S(1)}, u32[]{:S(2)}, u32[]{:S(2)}) %collective-permute-start.17) | collective-permute-done | bytes 131104 | tf_op jit(solution)/shard_map/ppermute | solution.py:146
  32.0 2.2 %final.1 = (bf16[512,1024]{1,0:T(8,128)(2,1)}, bf16[512,1024]{1,0:T(8,128)(2,1)}, bf16[512,1024]{1,0:T(8,128)(2,1)}) custom-call(s32[1]{0:T(128)} %bitcast.core, bf16[512,1024]{1,0:T(8,128)(2,1)S(1)} %get-tuple-element.128.k, bf16[512,1024]{1,0:T(8,128)(2,1)S(1)} %get-tuple-element.129.v, bf16[512,1024]{1,0:T(8,128)(2,1)S(1)} %get-tuple-element.130.g, ...), custom_call_target="tpu_custom_call" | custom-call | tf_op jit(solution)/shard_map/final/pallas_call | solution.py:128
  (53 shorter events, 1.8 us)
Async XLA Ops:
  3.9 1.5 %collective-permute-start = (f32[2,128,128]{2,1,0:T(8,128)S(1)}, f32[2,128,128]{2,1,0:T(8,128)S(1)}, u32[]{:S(2)}, u32[]{:S(2)}) collective-permute-start(f32[2,128,128]{2,1,0:T(8,128)S(1)} %get-tuple-element.86), channel_id=1, source_target_pairs={{0,1},{1,0},{2,3},{3,2},{4,5},{5,4},{6,7},{7,6},{8,9},{9,8},{10,11... | collective-permute-start | bytes 393224 | tf_op jit(solution)/shard_map/ppermute | solution.py:146
  4.4 6.3 %collective-permute-start.2 = (f32[2,128,128]{2,1,0:T(8,128)S(1)}, f32[2,128,128]{2,1,0:T(8,128)S(1)}, u32[]{:S(2)}, u32[]{:S(2)}) collective-permute-start(f32[2,128,128]{2,1,0:T(8,128)S(1)} %get-tuple-element.91), channel_id=1, source_target_pairs={{0,1},{1,0},{2,3},{3,2},{4,5},{5,4},{6,7},{7,6},{8,9},{9,8},{10,11... | collective-permute-start | bytes 393224 | tf_op jit(solution)/shard_map/ppermute | solution.py:146
  4.5 4.6 %collective-permute-start.3 = (f32[2,128,128]{2,1,0:T(8,128)S(1)}, f32[2,128,128]{2,1,0:T(8,128)S(1)}, u32[]{:S(2)}, u32[]{:S(2)}) collective-permute-start(f32[2,128,128]{2,1,0:T(8,128)S(1)} %get-tuple-element.93), channel_id=1, source_target_pairs={{0,1},{1,0},{2,3},{3,2},{4,5},{5,4},{6,7},{7,6},{8,9},{9,8},{10,11... | collective-permute-start | bytes 393224 | tf_op jit(solution)/shard_map/ppermute | solution.py:146
  4.9 3.5 %collective-permute-start.4 = (f32[2,128,128]{2,1,0:T(8,128)S(1)}, f32[2,128,128]{2,1,0:T(8,128)S(1)}, u32[]{:S(2)}, u32[]{:S(2)}) collective-permute-start(f32[2,128,128]{2,1,0:T(8,128)S(1)} %get-tuple-element.95), channel_id=1, source_target_pairs={{0,1},{1,0},{2,3},{3,2},{4,5},{5,4},{6,7},{7,6},{8,9},{9,8},{10,11... | collective-permute-start | bytes 393224 | tf_op jit(solution)/shard_map/ppermute | solution.py:146
  5.4 8.3 %collective-permute-start.1 = (f32[1,128,128]{2,1,0:T(8,128)S(1)}, f32[1,128,128]{2,1,0:T(8,128)S(1)}, u32[]{:S(2)}, u32[]{:S(2)}) collective-permute-start(f32[1,128,128]{2,1,0:T(8,128)S(1)} %slice_select_fusion.5), channel_id=1, source_target_pairs={{0,4},{1,5},{4,0},{5,1},{8,12},{9,13},{12,8},{13,9},{2,6},{3,7},{6... | collective-permute-start | bytes 196616 | tf_op jit(solution)/shard_map/ppermute | solution.py:156
  8.5 5.3 %collective-permute-start.8 = (f32[1,128,128]{2,1,0:T(8,128)S(1)}, f32[1,128,128]{2,1,0:T(8,128)S(1)}, u32[]{:S(2)}, u32[]{:S(2)}) collective-permute-start(f32[1,128,128]{2,1,0:T(8,128)S(1)} %slice_select_fusion.4), channel_id=1, source_target_pairs={{0,4},{1,5},{4,0},{5,1},{8,12},{9,13},{12,8},{13,9},{2,6},{3,7},{6... | collective-permute-start | bytes 196616 | tf_op jit(solution)/shard_map/ppermute | solution.py:156
  9.2 5.5 %collective-permute-start.7 = (f32[1,128,128]{2,1,0:T(8,128)S(1)}, f32[1,128,128]{2,1,0:T(8,128)S(1)}, u32[]{:S(2)}, u32[]{:S(2)}) collective-permute-start(f32[1,128,128]{2,1,0:T(8,128)S(1)} %slice_select_fusion.3), channel_id=1, source_target_pairs={{0,4},{1,5},{4,0},{5,1},{8,12},{9,13},{12,8},{13,9},{2,6},{3,7},{6... | collective-permute-start | bytes 196616 | tf_op jit(solution)/shard_map/ppermute | solution.py:156
  10.7 4.7 %collective-permute-start.6 = (f32[1,128,128]{2,1,0:T(8,128)S(1)}, f32[1,128,128]{2,1,0:T(8,128)S(1)}, u32[]{:S(2)}, u32[]{:S(2)}) collective-permute-start(f32[1,128,128]{2,1,0:T(8,128)S(1)} %slice_select_fusion.2), channel_id=1, source_target_pairs={{0,4},{1,5},{4,0},{5,1},{8,12},{9,13},{12,8},{13,9},{2,6},{3,7},{6... | collective-permute-start | bytes 196616 | tf_op jit(solution)/shard_map/ppermute | solution.py:156
  13.7 1.8 %collective-permute-start.5 = (f32[1,128,128]{2,1,0:T(8,128)S(1)}, f32[1,128,128]{2,1,0:T(8,128)S(1)}, u32[]{:S(2)}, u32[]{:S(2)}) collective-permute-start(f32[1,128,128]{2,1,0:T(8,128)S(1)} %select_add_fusion.20), channel_id=1, source_target_pairs={{0,1},{1,0},{4,8},{5,9},{8,4},{9,5},{12,13},{13,12},{2,3},{3,2},{6... | collective-permute-start | bytes 196616 | tf_op jit(solution)/shard_map/ppermute | solution.py:156
  13.8 7.3 %collective-permute-start.12 = (f32[1,128,128]{2,1,0:T(8,128)S(1)}, f32[1,128,128]{2,1,0:T(8,128)S(1)}, u32[]{:S(2)}, u32[]{:S(2)}) collective-permute-start(f32[1,128,128]{2,1,0:T(8,128)S(1)} %select_add_fusion.17), channel_id=1, source_target_pairs={{0,1},{1,0},{4,8},{5,9},{8,4},{9,5},{12,13},{13,12},{2,3},{3,2},{6... | collective-permute-start | bytes 196616 | tf_op jit(solution)/shard_map/ppermute | solution.py:156
  14.7 8.4 %collective-permute-start.11 = (f32[1,128,128]{2,1,0:T(8,128)S(1)}, f32[1,128,128]{2,1,0:T(8,128)S(1)}, u32[]{:S(2)}, u32[]{:S(2)}) collective-permute-start(f32[1,128,128]{2,1,0:T(8,128)S(1)} %select_add_fusion.18), channel_id=1, source_target_pairs={{0,1},{1,0},{4,8},{5,9},{8,4},{9,5},{12,13},{13,12},{2,3},{3,2},{6... | collective-permute-start | bytes 196616 | tf_op jit(solution)/shard_map/ppermute | solution.py:156
  15.4 9.9 %collective-permute-start.10 = (f32[1,128,128]{2,1,0:T(8,128)S(1)}, f32[1,128,128]{2,1,0:T(8,128)S(1)}, u32[]{:S(2)}, u32[]{:S(2)}) collective-permute-start(f32[1,128,128]{2,1,0:T(8,128)S(1)} %select_add_fusion.19), channel_id=1, source_target_pairs={{0,1},{1,0},{4,8},{5,9},{8,4},{9,5},{12,13},{13,12},{2,3},{3,2},{6... | collective-permute-start | bytes 196616 | tf_op jit(solution)/shard_map/ppermute | solution.py:156
  15.5 12.4 %collective-permute-start.9 = (f32[1,128,128]{2,1,0:T(8,128)S(1)}, f32[1,128,128]{2,1,0:T(8,128)S(1)}, u32[]{:S(2)}, u32[]{:S(2)}) collective-permute-start(f32[1,128,128]{2,1,0:T(8,128)S(1)} %select_add_fusion.21), channel_id=1, source_target_pairs={{0,4},{1,5},{4,0},{5,1},{8,12},{9,13},{12,8},{13,9},{2,6},{3,7},{6... | collective-permute-start | bytes 196616 | tf_op jit(solution)/shard_map/ppermute | solution.py:156
  21.2 6.7 %collective-permute-start.13 = (f32[1,128,128]{2,1,0:T(8,128)S(1)}, f32[1,128,128]{2,1,0:T(8,128)S(1)}, u32[]{:S(2)}, u32[]{:S(2)}) collective-permute-start(f32[1,128,128]{2,1,0:T(8,128)S(1)} %select_add_fusion.14), channel_id=1, source_target_pairs={{0,4},{1,5},{4,0},{5,1},{8,12},{9,13},{12,8},{13,9},{2,6},{3,7},{6... | collective-permute-start | bytes 196616 | tf_op jit(solution)/shard_map/ppermute | solution.py:156
  23.1 4.9 %collective-permute-start.14 = (f32[1,128,128]{2,1,0:T(8,128)S(1)}, f32[1,128,128]{2,1,0:T(8,128)S(1)}, u32[]{:S(2)}, u32[]{:S(2)}) collective-permute-start(f32[1,128,128]{2,1,0:T(8,128)S(1)} %select_add_fusion.15), channel_id=1, source_target_pairs={{0,4},{1,5},{4,0},{5,1},{8,12},{9,13},{12,8},{13,9},{2,6},{3,7},{6... | collective-permute-start | bytes 196616 | tf_op jit(solution)/shard_map/ppermute | solution.py:156
  25.3 4.3 %collective-permute-start.15 = (f32[1,128,128]{2,1,0:T(8,128)S(1)}, f32[1,128,128]{2,1,0:T(8,128)S(1)}, u32[]{:S(2)}, u32[]{:S(2)}) collective-permute-start(f32[1,128,128]{2,1,0:T(8,128)S(1)} %select_add_fusion.16), channel_id=1, source_target_pairs={{0,4},{1,5},{4,0},{5,1},{8,12},{9,13},{12,8},{13,9},{2,6},{3,7},{6... | collective-permute-start | bytes 196616 | tf_op jit(solution)/shard_map/ppermute | solution.py:156
  29.7 1.4 %collective-permute-start.19 = (f32[2,128,128]{2,1,0:T(8,128)S(1)}, f32[2,128,128]{2,1,0:T(8,128)S(1)}, u32[]{:S(2)}, u32[]{:S(2)}) collective-permute-start(f32[2,128,128]{2,1,0:T(8,128)S(1)} %pad_maximum_fusion.7), channel_id=1, source_target_pairs={{0,1},{1,0},{2,3},{3,2},{4,5},{5,4},{6,7},{7,6},{8,9},{9,8},{10,11... | collective-permute-start | bytes 393224 | tf_op jit(solution)/shard_map/ppermute | solution.py:146
  29.8 1.5 %collective-permute-start.18 = (f32[2,128,128]{2,1,0:T(8,128)S(1)}, f32[2,128,128]{2,1,0:T(8,128)S(1)}, u32[]{:S(2)}, u32[]{:S(2)}) collective-permute-start(f32[2,128,128]{2,1,0:T(8,128)S(1)} %pad_maximum_fusion.6), channel_id=1, source_target_pairs={{0,1},{1,0},{2,3},{3,2},{4,5},{5,4},{6,7},{7,6},{8,9},{9,8},{10,11... | collective-permute-start | bytes 393224 | tf_op jit(solution)/shard_map/ppermute | solution.py:146
  30.4 1.4 %collective-permute-start.17 = (f32[2,128,128]{2,1,0:T(8,128)S(1)}, f32[2,128,128]{2,1,0:T(8,128)S(1)}, u32[]{:S(2)}, u32[]{:S(2)}) collective-permute-start(f32[2,128,128]{2,1,0:T(8,128)S(1)} %pad_maximum_fusion.5), channel_id=1, source_target_pairs={{0,1},{1,0},{2,3},{3,2},{4,5},{5,4},{6,7},{7,6},{8,9},{9,8},{10,11... | collective-permute-start | bytes 393224 | tf_op jit(solution)/shard_map/ppermute | solution.py:146
  30.5 1.5 %collective-permute-start.16 = (f32[2,128,128]{2,1,0:T(8,128)S(1)}, f32[2,128,128]{2,1,0:T(8,128)S(1)}, u32[]{:S(2)}, u32[]{:S(2)}) collective-permute-start(f32[2,128,128]{2,1,0:T(8,128)S(1)} %pad_maximum_fusion.4), channel_id=1, source_target_pairs={{0,1},{1,0},{2,3},{3,2},{4,5},{5,4},{6,7},{7,6},{8,9},{9,8},{10,11... | collective-permute-start | bytes 393224 | tf_op jit(solution)/shard_map/ppermute | solution.py:146

commit v8 on v7

v8 whole, which is shorter than its diff:
```python
import functools

import jax
import jax.numpy as jnp
from jax import lax
from jax.experimental import pallas as pl
from jax.experimental.pallas import tpu as pltpu
from jax.sharding import PartitionSpec as P

DH = 128
CHUNKS = 2
PLAN = (5, 1, 2, 0, 0)
F32 = jnp.float32
BF16 = jnp.bfloat16
VMEM = pl.BlockSpec(memory_space=pltpu.VMEM)
HBM = pl.BlockSpec(memory_space=pltpu.HBM)
SMEM = pl.BlockSpec(memory_space=pltpu.SMEM)


def product(left, right, left_axis, right_axis):
    return lax.dot_general(
        left, right, (((left_axis,), (right_axis,)), ((), ())), preferred_element_type=F32
    )


def head_columns(head):
    return slice(head * DH, (head + 1) * DH)


def states_kernel(core, q_hbm, k_hbm, v_hbm, g_hbm, q, k, v, g, *rest):
    chunks = (len(rest) - 1) // 2
    keep, give, sems = rest[:chunks], rest[chunks : 2 * chunks], rest[-1]
    copies = [
        pltpu.make_async_copy(source, target, sems.at[i])
        for i, (source, target) in enumerate(zip((q_hbm, k_hbm, v_hbm, g_hbm), (q, k, v, g)))
    ]
    for c in (1, 2, 0, 3):
        copies[c].start()
    half = q.shape[1] // 2
    for left, right, place in ((1, 2, 0), (0, 3, 1)):
        copies[left].wait()
        copies[right].wait()
        x, y = (q, k, v, g)[left], (q, k, v, g)[right]
        for outs, start in ((give, (1 - core[0]) * half), (keep, core[0] * half)):
            h = 0
            for out in outs:
                count = out.shape[0] // 2
                for i in range(count):
                    c = pl.ds(pl.multiple_of(start + h * DH, DH), DH)
                    out[place * count + i] = product(x[:, c], y[:, c], 0, 0)
                    h += 1


def states(core, parts, q, k, v, g):
    outs = [pltpu.VMEM((2 * n, DH, DH), F32) for n in parts] * 2
    result = pl.pallas_call(
        states_kernel,
        in_specs=[SMEM] + [HBM] * 4,
        out_specs=[VMEM] * (4 + len(outs)),
        out_shape=[pltpu.VMEM(q.shape, BF16)] * 4 + outs,
        scratch_shapes=[pltpu.SemaphoreType.DMA((4,))],
        compiler_params=pltpu.CompilerParams(vmem_limit_bytes=8 << 20),
        name="states",
    )(core, *[pltpu.with_memory_space_constraint(x, pltpu.HBM) for x in (q, k, v, g)])
    return result[:4], result[4 : 4 + len(parts)], result[4 + len(parts) :]


def intra_kernel(first, heads, q, k, v, g, *rest):
    dq, dk, dv = rest[-3:]
    rows = q.shape[0]
    row = lax.broadcasted_iota(jnp.int32, (rows, rows), 0)
    col = lax.broadcasted_iota(jnp.int32, (rows, rows), 1)
    for h in range(first, first + heads):
        c = head_columns(h)
        qh, kh, vh, gh = q[:, c], k[:, c], v[:, c], g[:, c]
        grad_scores = jnp.where(row >= col, product(gh, vh, 1, 1), 0.0).astype(BF16)
        dq[:, c] = product(grad_scores, kh, 1, 0)
        dk[:, c] = product(grad_scores, qh, 0, 0)
        attn_scores = jnp.where(row <= col, product(kh, qh, 1, 1), 0.0).astype(BF16)
        dv[:, c] = product(attn_scores, gh, 1, 0)


def intra(first, heads, q, k, v, g, filled):
    return pl.pallas_call(
        functools.partial(intra_kernel, first, heads),
        in_specs=[VMEM] * (4 + len(filled)),
        out_specs=[VMEM] * 3,
        out_shape=[pltpu.VMEM(q.shape, F32)] * 3,
        input_output_aliases={4 + i: i for i in range(len(filled))},
        compiler_params=pltpu.CompilerParams(vmem_limit_bytes=16 << 20),
        name="intra",
    )(q, k, v, g, *filled)


def final_kernel(groups, heads, aliased, core, k, v, g, dqi, dki, dvi, *rest):
    states, rest = rest[: len(groups)], rest[len(groups) + aliased :]
    (targets, outs, sems) = rest[:3], rest[3:6], rest[6]
    copies, done = [], 0
    for n, ((other, first, count), both) in enumerate(zip(groups, states)):
        half = 1 - core[0] if other else core[0]
        start = half * (heads // 2) + first
        for i in range(count):
            c, w = pl.ds(pl.multiple_of((start + i) * DH, DH), DH), head_columns(done + i)
            before, behind = both[i].astype(BF16), both[count + i].astype(BF16)
            outs[0][:, w] = (dqi[:, c] + product(g[:, c], before, 1, 1)).astype(BF16)
            outs[1][:, w] = (dki[:, c] + product(v[:, c], behind, 1, 1)).astype(BF16)
            outs[2][:, w] = (dvi[:, c] + product(k[:, c], behind, 1, 0)).astype(BF16)
        here = slice(done * DH, (done + count) * DH)
        there = pl.ds(pl.multiple_of(start * DH, DH), count * DH)
        for m in range(3):
            copy = pltpu.make_async_copy(
                outs[m].at[:, here], targets[m].at[:, there], sems.at[n, m]
            )
            copy.start()
            copies.append(copy)
        done += count
    for copy in copies:
        copy.wait()


def final(groups, core, args, local, states, filled):
    _, k, v, g = args
    shape = jax.ShapeDtypeStruct(k.shape, BF16)
    inputs = (core, k, v, g, *local, *states)
    width = sum(count for _, _, count in groups) * DH
    return pl.pallas_call(
        functools.partial(final_kernel, groups, k.shape[1] // DH, len(filled)),
        in_specs=[SMEM] + [VMEM] * (len(inputs) - 1) + [HBM] * len(filled),
        out_specs=[HBM] * 3,
        out_shape=[shape] * 3,
        scratch_shapes=[pltpu.VMEM((k.shape[0], width), BF16)] * 3
        + [pltpu.SemaphoreType.DMA((len(groups), 3))],
        input_output_aliases={len(inputs) + i: i for i in range(len(filled))},
        compiler_params=pltpu.CompilerParams(vmem_limit_bytes=8 << 20),
        name="final",
    )(*inputs, *filled)


def after(values, *events):
    values = tuple(values)
    return lax.optimization_barrier(values + tuple(events))[: len(values)]


def swap(value):
    return lax.ppermute(value, "sub", [(0, 1), (1, 0)])


def exchange(value, chips, step):
    partner = {}
    for low in (step, chips - 2 - step):
        for core in (0, 1):
            a, b = 2 * low + core, 2 * low + 2 + core
            partner[a], partner[b] = b, a
    pairs = [(d, partner.get(d, d ^ 1)) for d in range(2 * chips)]
    return lax.ppermute(value, ("seq", "sub"), pairs)


def body(*args):
    chips = lax.axis_size("seq")
    core, chip = lax.axis_index("sub").astype(jnp.int32), lax.axis_index("seq")
    heads = args[0].shape[1] // DH
    chunks = min(CHUNKS, heads // 2)
    parts = tuple(
        heads // 2 * (c + 1) // chunks - heads // 2 * c // chunks for c in range(chunks)
    )
    slots = 1 + (chips - 2) * chunks
    plan = PLAN if (heads, slots) == (sum(PLAN), len(PLAN)) else (0,) * (slots - 1) + (heads,)
    at = [chip == c for c in range(chips)]
    core, first_core, *rest = lax.optimization_barrier((core.reshape(1), core == 0, *at, *args))
    at, args = rest[:chips], rest[chips:]
    args, keep, give = states(core, parts, *args)
    got = [swap(x) for x in give]
    total = [None] * chunks
    local, done = (), 0

    def local_piece(count, event):
        nonlocal local, done
        if count:
            local = intra(done, count, *after(args, event), local)
            done += count
            event = local[0]
        return event

    prefix = [jnp.zeros_like(x[:n]) for x, n in zip(keep, parts)]
    suffix = list(prefix)
    arrived = [None] * chunks
    event, outs, own, other = None, (), [], []
    for step in range(chips):
        if step == 1:
            event = local_piece(plan[0], event)
        for c, n in enumerate(parts):
            if step == 0:
                if c:
                    (got[c],) = after(got[c : c + 1], event)
                total[c] = keep[c] + got[c]
            else:
                (arrived[c],) = after(arrived[c : c + 1], event)
                prefix[c] = jnp.where(at[step], arrived[c], prefix[c])
                suffix[c] = jnp.where(at[chips - 1 - step], arrived[c], suffix[c])
            if step == chips - 1:
                zero = jnp.zeros_like(prefix[c])
                own.append(
                    jnp.concatenate(
                        [
                            prefix[c] + jnp.where(first_core, zero, got[c][:n]),
                            suffix[c] + jnp.where(first_core, got[c][n:], zero),
                        ]
                    )
                )
                lend = jnp.concatenate(
                    [
                        prefix[c] + jnp.where(first_core, keep[c][:n], zero),
                        suffix[c] + jnp.where(first_core, zero, keep[c][n:]),
                    ]
                )
                other.append(swap(lend))
                groups, use = [(False, sum(parts[:c]), n)], [own[c]]
                if c:
                    groups.append((True, sum(parts[: c - 1]), parts[c - 1]))
                    use.append(other[c - 1])
                outs = final(tuple(groups), core, args, local, use, outs)
                event = outs[0]
                continue
            sent = jnp.where(at[step], total[c][:n], total[c][n:])
            if step:
                sent = sent + arrived[c]
            arrived[c] = exchange(sent, chips, step)
            event = sent
            if step:
                event = local_piece(plan[1 + (step - 1) * chunks + c], sent)
    last_group = (True, sum(parts[:-1]), parts[-1])
    return tuple(final((last_group,), core, args, local, other[-1:], outs))


def solution(mesh):
    placed = P(("rep", "seq", "sub"), "head")
    return jax.shard_map(
        body, mesh=mesh, in_specs=(placed,) * 4, out_specs=(placed,) * 3, check_vma=False
    )
```

time: 34.4 us -> 30.8 us (0.90)
  starting transfers between devices: 16.7 us -> 10.6 us
  Pallas kernels: 12.2 us -> 13.8 us
  waiting for transfers between devices: 3.79 us -> 5.02 us
    ppermute x12 -> x6, starting transfers between devices: 14.4 us -> 9.34 us  [exchange(): return lax.ppermute(value, ('seq', 'sub'), pairs)]
    pallas_call x6, Pallas kernels: 8.99 us -> 10.6 us  [the longest x3 6.24 us: intra(): pl.pallas_call(functools.partial(intra_kernel, first, heads), in_specs=[V...]
    ppermute x12 -> x6, waiting for transfers between devices: 2.51 us -> 3.93 us  [exchange(): return lax.ppermute(value, ('seq', 'sub'), pairs)]
    ppermute x8 -> x4, starting transfers between devices: 2.37 us -> 1.22 us  [swap(): return lax.ppermute(value, 'sub', [(0, 1), (1, 0)])]
    ppermute x8 -> x4, waiting for transfers between devices: 1.28 us -> 1.09 us  [swap(): return lax.ppermute(value, 'sub', [(0, 1), (1, 0)])]
  transfers between devices with their start and end apart: 20 -> 10, of which waited for: 7 -> 4; matrix products, arithmetic and copies ran while one was open for 1% -> 2% of each run, Pallas kernels for 20% -> 30%
where the time goes in v8:
time: 30.8 us; the launch traced here: 30.7 us
  Pallas kernels  13.8 us (45%)
  starting transfers between devices  10.6 us (34%)
  waiting for transfers between devices  5.02 us (16%)
  between operations  0.81 us (3%)
  other arithmetic  0.48 us (2%)
    ppermute x6, starting transfers between devices, exchange(): return lax.ppermute(value, ('seq', 'sub'), pairs)  9.34 us
    pallas_call x3, Pallas kernels, intra(): pl.pallas_call(functools.partial(intra_kernel, first, heads), in_specs=[V...  6.24 us
    pallas_call x3, Pallas kernels, final(): pl.pallas_call(functools.partial(final_kernel, groups, k.shape[1] // DH,...  4.33 us
    ppermute x6, waiting for transfers between devices, exchange(): return lax.ppermute(value, ('seq', 'sub'), pairs)  3.93 us
    pallas_call x1, Pallas kernels, states(): pl.pallas_call(states_kernel, in_specs=[SMEM] + [HBM] * 4, out_specs=[VME...  3.23 us
    ppermute x4, starting transfers between devices, swap(): return lax.ppermute(value, 'sub', [(0, 1), (1, 0)])  1.22 us
    ppermute x4, waiting for transfers between devices, swap(): return lax.ppermute(value, 'sub', [(0, 1), (1, 0)])  1.09 us
  transfers between devices with their start and end apart: 10, of which 4 were waited for; matrix products, arithmetic and copies ran while one was open for 2% of the time, Pallas kernels for 30%

profile of v8, /device:TPU:0, one launch (start us, length us, event | category | flops | bytes accessed | tf_op | source)
XLA Modules:
  0.0 30.7 jit_solution(13641859563119943403)
XLA Ops:
  0.6 3.2 %states.1 = (bf16[512,1024]{1,0:T(8,128)(2,1)S(1)}, bf16[512,1024]{1,0:T(8,128)(2,1)S(1)}, bf16[512,1024]{1,0:T(8,128)(2,1)S(1)}, bf16[512,1024]{1,0:T(8,128)(2,...) custom-call(s32[1]{0:T(128)} %bitcast.core, ...), custom_call_target="tpu_custom_call" | custom-call | tf_op jit(solution)/shard_map/states/pallas_call | solution.py:56
  3.9 0.5 %collective-permute-start.1 = (f32[4,128,128]{2,1,0:T(8,128)S(1)}, f32[4,128,128]{2,1,0:T(8,128)S(1)}, u32[]{:S(2)}, u32[]{:S(2)}) collective-permute-start(f32[4,128,128]{2,1,0:T(8,128)S(1)} %get-tuple-element.69), channel_id=1, source_target_pairs={{0,1},{1,0},{2,3},{3,2},{4,5},{5,4},{6,7},{7,6},{8,9},{9,8},{10,11... | collective-permute-start | bytes 786440 | tf_op jit(solution)/shard_map/ppermute | solution.py:145
  4.4 0.1 collective-permute-start
  4.5 1.1 %collective-permute-done.1 = f32[4,128,128]{2,1,0:T(8,128)S(1)} collective-permute-done((f32[4,128,128]{2,1,0:T(8,128)S(1)}, f32[4,128,128]{2,1,0:T(8,128)S(1)}, u32[]{:S(2)}, u32[]{:S(2)}) %collective-permute-start.1) | collective-permute-done | bytes 262176 | tf_op jit(solution)/shard_map/ppermute | solution.py:145
  5.6 3.0 %collective-permute-start.3 = (f32[2,128,128]{2,1,0:T(8,128)S(1)}, f32[2,128,128]{2,1,0:T(8,128)S(1)}, u32[]{:S(2)}, u32[]{:S(2)}) collective-permute-start(f32[2,128,128]{2,1,0:T(8,128)S(1)} %slice_select_fusion.3), channel_id=1, source_target_pairs={{0,4},{1,5},{4,0},{5,1},{8,12},{9,13},{12,8},{13,9},{2,6},{3,7},{6... | collective-permute-start | bytes 393224 | tf_op jit(solution)/shard_map/ppermute | solution.py:155
  8.6 0.0 collective-permute-done
  8.7 0.3 %collective-permute-start.2 = (f32[2,128,128]{2,1,0:T(8,128)S(1)}, f32[2,128,128]{2,1,0:T(8,128)S(1)}, u32[]{:S(2)}, u32[]{:S(2)}) collective-permute-start(f32[2,128,128]{2,1,0:T(8,128)S(1)} %slice_select_fusion.2), channel_id=1, source_target_pairs={{0,4},{1,5},{4,0},{5,1},{8,12},{9,13},{12,8},{13,9},{2,6},{3,7},{6... | collective-permute-start | bytes 393224 | tf_op jit(solution)/shard_map/ppermute | solution.py:155
  9.0 3.7 %intra.3 = (f32[512,1024]{1,0:T(8,128)S(1)}, f32[512,1024]{1,0:T(8,128)S(1)}, f32[512,1024]{1,0:T(8,128)S(1)}) custom-call(bf16[512,1024]{1,0:T(8,128)(2,1)S(1)} %get-tuple-element.85.q, bf16[512,1024]{1,0:T(8,128)(2,1)S(1)} %get-tuple-element.86.k, bf16[512,1024]{1,0:T(8,128)(2,1)S(1)} %get-tuple-element.87.v, bf16[512,1024]{1,0:T(8,128)(2,1)S(1)} %get-tuple-element.88.g), custom_call_target="tpu_custom_call" | custom-call | tf_op jit(solution)/shard_map/intra/pallas_call | solution.py:84
  12.7 0.2 collective-permute-done.3
  12.9 0.1 collective-permute-start.5
  13.0 0.9 %intra.4 = (f32[512,1024]{1,0:T(8,128)S(1)}, f32[512,1024]{1,0:T(8,128)S(1)}, f32[512,1024]{1,0:T(8,128)S(1)}) custom-call(bf16[512,1024]{1,0:T(8,128)(2,1)S(1)} %get-tuple-element.85.q, bf16[512,1024]{1,0:T(8,128)(2,1)S(1)} %get-tuple-element.86.k, ...), custom_call_target="tpu_custom_call", output_to_operand_aliasing={{0}: (4, {}), {1}: (5, {}), {2}: (6, {})} | custom-call | tf_op jit(solution)/shard_map/intra/pallas_call | solution.py:84
  14.0 1.3 %collective-permute-done.2 = f32[2,128,128]{2,1,0:T(8,128)S(1)} collective-permute-done((f32[2,128,128]{2,1,0:T(8,128)S(1)}, f32[2,128,128]{2,1,0:T(8,128)S(1)}, u32[]{:S(2)}, u32[]{:S(2)}) %collective-permute-start.2) | collective-permute-done | bytes 131104 | tf_op jit(solution)/shard_map/ppermute | solution.py:155
  15.3 0.1 collective-permute-start.4
  15.3 1.6 %intra.5 = (f32[512,1024]{1,0:T(8,128)S(1)}, f32[512,1024]{1,0:T(8,128)S(1)}, f32[512,1024]{1,0:T(8,128)S(1)}) custom-call(bf16[512,1024]{1,0:T(8,128)(2,1)S(1)} %get-tuple-element.85.q, bf16[512,1024]{1,0:T(8,128)(2,1)S(1)} %get-tuple-element.86.k, ...), custom_call_target="tpu_custom_call", output_to_operand_aliasing={{0}: (4, {}), {1}: (5, {}), {2}: (6, {})} | custom-call | tf_op jit(solution)/shard_map/intra/pallas_call | solution.py:84
  17.0 4.0 %collective-permute-start.7 = (f32[2,128,128]{2,1,0:T(8,128)S(1)}, f32[2,128,128]{2,1,0:T(8,128)S(1)}, u32[]{:S(2)}, u32[]{:S(2)}) collective-permute-start(f32[2,128,128]{2,1,0:T(8,128)S(1)} %select_add_fusion.6), channel_id=1, source_target_pairs={{0,4},{1,5},{4,0},{5,1},{8,12},{9,13},{12,8},{13,9},{2,6},{3,7},{6... | collective-permute-start | bytes 393224 | tf_op jit(solution)/shard_map/ppermute | solution.py:155
  21.1 1.9 %collective-permute-start.6 = (f32[2,128,128]{2,1,0:T(8,128)S(1)}, f32[2,128,128]{2,1,0:T(8,128)S(1)}, u32[]{:S(2)}, u32[]{:S(2)}) collective-permute-start(f32[2,128,128]{2,1,0:T(8,128)S(1)} %select_add_fusion.7), channel_id=1, source_target_pairs={{0,4},{1,5},{4,0},{5,1},{8,12},{9,13},{12,8},{13,9},{2,6},{3,7},{6... | collective-permute-start | bytes 393224 | tf_op jit(solution)/shard_map/ppermute | solution.py:155
  22.9 2.4 %collective-permute-done.7 = f32[2,128,128]{2,1,0:T(8,128)S(1)} collective-permute-done((f32[2,128,128]{2,1,0:T(8,128)S(1)}, f32[2,128,128]{2,1,0:T(8,128)S(1)}, u32[]{:S(2)}, u32[]{:S(2)}) %collective-permute-start.7) | collective-permute-done | bytes 131104 | tf_op jit(solution)/shard_map/ppermute | solution.py:155
  25.4 0.1 select_add_fusion.1
  25.5 0.1 collective-permute-start.9
  25.6 1.3 %final.3 = (bf16[512,1024]{1,0:T(8,128)(2,1)}, bf16[512,1024]{1,0:T(8,128)(2,1)}, bf16[512,1024]{1,0:T(8,128)(2,1)}) custom-call(s32[1]{0:T(128)} %bitcast.core, bf16[512,1024]{1,0:T(8,128)(2,1)S(1)} %get-tuple-element.86.k, bf16[512,1024]{1,0:T(8,128)(2,1)S(1)} %get-tuple-element.87.v, bf16[512,1024]{1,0:T(8,128)(2,1)S(1)} %get-tuple-element.88.g, ...), custom_call_target="tpu_custom_call" | custom-call | tf_op jit(solution)/shard_map/final/pallas_call | solution.py:126
  26.9 0.1 select_add_fusion.3
  27.0 0.6 %collective-permute-start.8 = (f32[4,128,128]{2,1,0:T(8,128)S(1)}, f32[4,128,128]{2,1,0:T(8,128)S(1)}, u32[]{:S(2)}, u32[]{:S(2)}) collective-permute-start(f32[4,128,128]{2,1,0:T(8,128)S(1)} %pad_maximum_fusion.1), channel_id=1, source_target_pairs={{0,1},{1,0},{2,3},{3,2},{4,5},{5,4},{6,7},{7,6},{8,9},{9,8},{10,11... | collective-permute-start | bytes 786440 | tf_op jit(solution)/shard_map/ppermute | solution.py:145
  27.6 1.7 %final.4 = (bf16[512,1024]{1,0:T(8,128)(2,1)}, bf16[512,1024]{1,0:T(8,128)(2,1)}, bf16[512,1024]{1,0:T(8,128)(2,1)}) custom-call(s32[1]{0:T(128)} %bitcast.core, bf16[512,1024]{1,0:T(8,128)(2,1)S(1)} %get-tuple-element.86.k, bf16[512,1024]{1,0:T(8,128)(2,1)S(1)} %get-tuple-element.87.v, ...), custom_call_target="tpu_custom_call", output_to_operand_aliasing={{0}: (9, {}), {1}: (10, {}), {2}: (11, {})} | custom-call | tf_op jit(solution)/shard_map/final/pallas_call | solution.py:126
  29.4 1.3 %final.5 = (bf16[512,1024]{1,0:T(8,128)(2,1)}, bf16[512,1024]{1,0:T(8,128)(2,1)}, bf16[512,1024]{1,0:T(8,128)(2,1)}) custom-call(s32[1]{0:T(128)} %bitcast.core, bf16[512,1024]{1,0:T(8,128)(2,1)S(1)} %get-tuple-element.86.k, bf16[512,1024]{1,0:T(8,128)(2,1)S(1)} %get-tuple-element.87.v, ...), custom_call_target="tpu_custom_call", output_to_operand_aliasing={{0}: (8, {}), {1}: (9, {}), {2}: (10, {})} | custom-call | tf_op jit(solution)/shard_map/final/pallas_call | solution.py:126
  (19 shorter events, 0.4 us)
Async XLA Ops:
  3.9 1.7 %collective-permute-start.1 = (f32[4,128,128]{2,1,0:T(8,128)S(1)}, f32[4,128,128]{2,1,0:T(8,128)S(1)}, u32[]{:S(2)}, u32[]{:S(2)}) collective-permute-start(f32[4,128,128]{2,1,0:T(8,128)S(1)} %get-tuple-element.69), channel_id=1, source_target_pairs={{0,1},{1,0},{2,3},{3,2},{4,5},{5,4},{6,7},{7,6},{8,9},{9,8},{10,11... | collective-permute-start | bytes 786440 | tf_op jit(solution)/shard_map/ppermute | solution.py:145
  4.4 4.2 %collective-permute-start = (f32[4,128,128]{2,1,0:T(8,128)S(1)}, f32[4,128,128]{2,1,0:T(8,128)S(1)}, u32[]{:S(2)}, u32[]{:S(2)}) collective-permute-start(f32[4,128,128]{2,1,0:T(8,128)S(1)} %get-tuple-element.66), channel_id=1, source_target_pairs={{0,1},{1,0},{2,3},{3,2},{4,5},{5,4},{6,7},{7,6},{8,9},{9,8},{10,11... | collective-permute-start | bytes 786440 | tf_op jit(solution)/shard_map/ppermute | solution.py:145
  5.6 7.3 %collective-permute-start.3 = (f32[2,128,128]{2,1,0:T(8,128)S(1)}, f32[2,128,128]{2,1,0:T(8,128)S(1)}, u32[]{:S(2)}, u32[]{:S(2)}) collective-permute-start(f32[2,128,128]{2,1,0:T(8,128)S(1)} %slice_select_fusion.3), channel_id=1, source_target_pairs={{0,4},{1,5},{4,0},{5,1},{8,12},{9,13},{12,8},{13,9},{2,6},{3,7},{6... | collective-permute-start | bytes 393224 | tf_op jit(solution)/shard_map/ppermute | solution.py:155
  8.7 6.5 %collective-permute-start.2 = (f32[2,128,128]{2,1,0:T(8,128)S(1)}, f32[2,128,128]{2,1,0:T(8,128)S(1)}, u32[]{:S(2)}, u32[]{:S(2)}) collective-permute-start(f32[2,128,128]{2,1,0:T(8,128)S(1)} %slice_select_fusion.2), channel_id=1, source_target_pairs={{0,4},{1,5},{4,0},{5,1},{8,12},{9,13},{12,8},{13,9},{2,6},{3,7},{6... | collective-permute-start | bytes 393224 | tf_op jit(solution)/shard_map/ppermute | solution.py:155
  12.9 4.0 %collective-permute-start.5 = (f32[2,128,128]{2,1,0:T(8,128)S(1)}, f32[2,128,128]{2,1,0:T(8,128)S(1)}, u32[]{:S(2)}, u32[]{:S(2)}) collective-permute-start(f32[2,128,128]{2,1,0:T(8,128)S(1)} %select_add_fusion.8), channel_id=1, source_target_pairs={{0,1},{1,0},{4,8},{5,9},{8,4},{9,5},{12,13},{13,12},{2,3},{3,2},{6... | collective-permute-start | bytes 393224 | tf_op jit(solution)/shard_map/ppermute | solution.py:155
  15.3 5.8 %collective-permute-start.4 = (f32[2,128,128]{2,1,0:T(8,128)S(1)}, f32[2,128,128]{2,1,0:T(8,128)S(1)}, u32[]{:S(2)}, u32[]{:S(2)}) collective-permute-start(f32[2,128,128]{2,1,0:T(8,128)S(1)} %select_add_fusion.9), channel_id=1, source_target_pairs={{0,1},{1,0},{4,8},{5,9},{8,4},{9,5},{12,13},{13,12},{2,3},{3,2},{6... | collective-permute-start | bytes 393224 | tf_op jit(solution)/shard_map/ppermute | solution.py:155
  17.0 8.3 %collective-permute-start.7 = (f32[2,128,128]{2,1,0:T(8,128)S(1)}, f32[2,128,128]{2,1,0:T(8,128)S(1)}, u32[]{:S(2)}, u32[]{:S(2)}) collective-permute-start(f32[2,128,128]{2,1,0:T(8,128)S(1)} %select_add_fusion.6), channel_id=1, source_target_pairs={{0,4},{1,5},{4,0},{5,1},{8,12},{9,13},{12,8},{13,9},{2,6},{3,7},{6... | collective-permute-start | bytes 393224 | tf_op jit(solution)/shard_map/ppermute | solution.py:155
  21.1 5.8 %collective-permute-start.6 = (f32[2,128,128]{2,1,0:T(8,128)S(1)}, f32[2,128,128]{2,1,0:T(8,128)S(1)}, u32[]{:S(2)}, u32[]{:S(2)}) collective-permute-start(f32[2,128,128]{2,1,0:T(8,128)S(1)} %select_add_fusion.7), channel_id=1, source_target_pairs={{0,4},{1,5},{4,0},{5,1},{8,12},{9,13},{12,8},{13,9},{2,6},{3,7},{6... | collective-permute-start | bytes 393224 | tf_op jit(solution)/shard_map/ppermute | solution.py:155
  25.5 2.2 %collective-permute-start.9 = (f32[4,128,128]{2,1,0:T(8,128)S(1)}, f32[4,128,128]{2,1,0:T(8,128)S(1)}, u32[]{:S(2)}, u32[]{:S(2)}) collective-permute-start(f32[4,128,128]{2,1,0:T(8,128)S(1)} %pad_maximum_fusion.3), channel_id=1, source_target_pairs={{0,1},{1,0},{2,3},{3,2},{4,5},{5,4},{6,7},{7,6},{8,9},{9,8},{10,11... | collective-permute-start | bytes 786440 | tf_op jit(solution)/shard_map/ppermute | solution.py:145
  27.0 2.3 %collective-permute-start.8 = (f32[4,128,128]{2,1,0:T(8,128)S(1)}, f32[4,128,128]{2,1,0:T(8,128)S(1)}, u32[]{:S(2)}, u32[]{:S(2)}) collective-permute-start(f32[4,128,128]{2,1,0:T(8,128)S(1)} %pad_maximum_fusion.1), channel_id=1, source_target_pairs={{0,1},{1,0},{2,3},{3,2},{4,5},{5,4},{6,7},{7,6},{8,9},{9,8},{10,11... | collective-permute-start | bytes 786440 | tf_op jit(solution)/shard_map/ppermute | solution.py:145

commit v9 on v8

--- a/solution.py
+++ b/solution.py
@@ -27,42 +27,38 @@
     return slice(head * DH, (head + 1) * DH)
 
 
-def states_kernel(core, q_hbm, k_hbm, v_hbm, g_hbm, q, k, v, g, *rest):
-    chunks = (len(rest) - 1) // 2
-    keep, give, sems = rest[:chunks], rest[chunks : 2 * chunks], rest[-1]
-    copies = [
-        pltpu.make_async_copy(source, target, sems.at[i])
-        for i, (source, target) in enumerate(zip((q_hbm, k_hbm, v_hbm, g_hbm), (q, k, v, g)))
-    ]
-    for c in (1, 2, 0, 3):
-        copies[c].start()
-    half = q.shape[1] // 2
-    for left, right, place in ((1, 2, 0), (0, 3, 1)):
-        copies[left].wait()
-        copies[right].wait()
-        x, y = (q, k, v, g)[left], (q, k, v, g)[right]
-        for outs, start in ((give, (1 - core[0]) * half), (keep, core[0] * half)):
-            h = 0
-            for out in outs:
-                count = out.shape[0] // 2
-                for i in range(count):
-                    c = pl.ds(pl.multiple_of(start + h * DH, DH), DH)
-                    out[place * count + i] = product(x[:, c], y[:, c], 0, 0)
-                    h += 1
-
-
-def states(core, parts, q, k, v, g):
-    outs = [pltpu.VMEM((2 * n, DH, DH), F32) for n in parts] * 2
+def states_kernel(first, count, aliased, core, q_hbm, k_hbm, v_hbm, g_hbm, *rest):
+    q, k, v, g, keep, give, sems = rest[aliased:]
+    width = q.shape[1] // 2
+    copies = []
+    for source, target in ((k_hbm, k), (v_hbm, v), (q_hbm, q), (g_hbm, g)):
+        for half in (0, 1):
+            c = pl.ds(half * width + first * DH, count * DH)
+            copy = pltpu.make_async_copy(source.at[:, c], target.at[:, c], sems.at[len(copies)])
+            copy.start()
+            copies.append(copy)
+    for n, (x, y) in enumerate(((k, v), (q, g))):
+        for copy in copies[4 * n : 4 * n + 4]:
+            copy.wait()
+        for out, half in ((give, 1 - core[0]), (keep, core[0])):
+            for i in range(count):
+                c = pl.ds(pl.multiple_of(half * width + (first + i) * DH, DH), DH)
+                out[n * count + i] = product(x[:, c], y[:, c], 0, 0)
+
+
+def states(core, first, count, args, filled):
     result = pl.pallas_call(
-        states_kernel,
-        in_specs=[SMEM] + [HBM] * 4,
-        out_specs=[VMEM] * (4 + len(outs)),
-        out_shape=[pltpu.VMEM(q.shape, BF16)] * 4 + outs,
-        scratch_shapes=[pltpu.SemaphoreType.DMA((4,))],
+        functools.partial(states_kernel, first, count, len(filled)),
+        in_specs=[SMEM] + [HBM] * 4 + [VMEM] * len(filled),
+        out_specs=[VMEM] * 6,
+        out_shape=[pltpu.VMEM(args[0].shape, BF16)] * 4
+        + [pltpu.VMEM((2 * count, DH, DH), F32)] * 2,
+        scratch_shapes=[pltpu.SemaphoreType.DMA((8,))],
+        input_output_aliases={5 + i: i for i in range(len(filled))},
         compiler_params=pltpu.CompilerParams(vmem_limit_bytes=8 << 20),
         name="states",
-    )(core, *[pltpu.with_memory_space_constraint(x, pltpu.HBM) for x in (q, k, v, g)])
-    return result[:4], result[4 : 4 + len(parts)], result[4 + len(parts) :]
+    )(core, *[pltpu.with_memory_space_constraint(x, pltpu.HBM) for x in args], *filled)
+    return result[:4], *result[4:]
 
 
 def intra_kernel(first, heads, q, k, v, g, *rest):
@@ -92,48 +88,65 @@
     )(q, k, v, g, *filled)
 
 
-def final_kernel(groups, heads, aliased, core, k, v, g, dqi, dki, dvi, *rest):
-    states, rest = rest[: len(groups)], rest[len(groups) + aliased :]
-    (targets, outs, sems) = rest[:3], rest[3:6], rest[6]
-    copies, done = [], 0
-    for n, ((other, first, count), both) in enumerate(zip(groups, states)):
+def final_kernel(groups, send, core, k, v, g, dqi, dki, dvi, *rest):
+    count_new = len(groups)
+    states, rest = rest[:count_new], rest[count_new:]
+    half_heads = k.shape[1] // DH // 2
+    hbm = 3 if send else 0
+    targets, staged, sems = rest[-4 - hbm : -4], rest[-4:-1], rest[-1]
+    copies = []
+
+    def place(other, first, count):
         half = 1 - core[0] if other else core[0]
-        start = half * (heads // 2) + first
-        for i in range(count):
-            c, w = pl.ds(pl.multiple_of((start + i) * DH, DH), DH), head_columns(done + i)
-            before, behind = both[i].astype(BF16), both[count + i].astype(BF16)
-            outs[0][:, w] = (dqi[:, c] + product(g[:, c], before, 1, 1)).astype(BF16)
-            outs[1][:, w] = (dki[:, c] + product(v[:, c], behind, 1, 1)).astype(BF16)
-            outs[2][:, w] = (dvi[:, c] + product(k[:, c], behind, 1, 0)).astype(BF16)
-        here = slice(done * DH, (done + count) * DH)
-        there = pl.ds(pl.multiple_of(start * DH, DH), count * DH)
+        return pl.multiple_of((half * half_heads + first) * DH, DH)
+
+    def write(other, first, count):
+        c = pl.ds(place(other, first, count), count * DH)
         for m in range(3):
             copy = pltpu.make_async_copy(
-                outs[m].at[:, here], targets[m].at[:, there], sems.at[n, m]
+                staged[m].at[:, c], targets[m].at[:, c], sems.at[len(copies)]
             )
             copy.start()
             copies.append(copy)
-        done += count
+
+    for group in send:
+        if group not in groups:
+            write(*group)
+    for group, both in zip(groups, states):
+        start, count = place(*group), group[2]
+        for i in range(count):
+            c = pl.ds(pl.multiple_of(start + i * DH, DH), DH)
+            before, behind = both[i].astype(BF16), both[count + i].astype(BF16)
+            staged[0][:, c] = (dqi[:, c] + product(g[:, c], before, 1, 1)).astype(BF16)
+            staged[1][:, c] = (dki[:, c] + product(v[:, c], behind, 1, 1)).astype(BF16)
+            staged[2][:, c] = (dvi[:, c] + product(k[:, c], behind, 1, 0)).astype(BF16)
+        if group in send:
+            write(*group)
     for copy in copies:
         copy.wait()
 
 
-def final(groups, core, args, local, states, filled):
+def final(groups, send, core, args, local, states, outs, staged):
     _, k, v, g = args
-    shape = jax.ShapeDtypeStruct(k.shape, BF16)
     inputs = (core, k, v, g, *local, *states)
-    width = sum(count for _, _, count in groups) * DH
-    return pl.pallas_call(
-        functools.partial(final_kernel, groups, k.shape[1] // DH, len(filled)),
-        in_specs=[SMEM] + [VMEM] * (len(inputs) - 1) + [HBM] * len(filled),
-        out_specs=[HBM] * 3,
-        out_shape=[shape] * 3,
-        scratch_shapes=[pltpu.VMEM((k.shape[0], width), BF16)] * 3
-        + [pltpu.SemaphoreType.DMA((len(groups), 3))],
-        input_output_aliases={len(inputs) + i: i for i in range(len(filled))},
+    filled = (*outs, *staged)
+    shapes = [jax.ShapeDtypeStruct(k.shape, BF16)] * 3 if send else []
+    shapes += [pltpu.VMEM(k.shape, BF16)] * 3
+    behind = len(shapes) - len(filled)
+    result = pl.pallas_call(
+        functools.partial(final_kernel, groups, send),
+        in_specs=[SMEM]
+        + [VMEM] * (len(inputs) - 1)
+        + [HBM] * len(outs)
+        + [VMEM] * len(staged),
+        out_specs=([HBM] * 3 if send else []) + [VMEM] * 3,
+        out_shape=shapes,
+        scratch_shapes=[pltpu.SemaphoreType.DMA((3 * max(len(send), 1),))],
+        input_output_aliases={len(inputs) + i: behind + i for i in range(len(filled))},
         compiler_params=pltpu.CompilerParams(vmem_limit_bytes=8 << 20),
         name="final",
     )(*inputs, *filled)
+    return result[:-3], result[-3:]
 
 
 def after(values, *events):
@@ -168,7 +181,11 @@
     at = [chip == c for c in range(chips)]
     core, first_core, *rest = lax.optimization_barrier((core.reshape(1), core == 0, *at, *args))
     at, args = rest[:chips], rest[chips:]
-    args, keep, give = states(core, parts, *args)
+    given, args, keep, give = args, (), [], []
+    for c, n in enumerate(parts):
+        args, kept, gave = states(core, sum(parts[:c]), n, given, args)
+        keep.append(kept)
+        give.append(gave)
     got = [swap(x) for x in give]
     total = [None] * chunks
     local, done = (), 0
@@ -184,7 +201,7 @@
     prefix = [jnp.zeros_like(x[:n]) for x, n in zip(keep, parts)]
     suffix = list(prefix)
     arrived = [None] * chunks
-    event, outs, own, other = None, (), [], []
+    event, outs, staged, waiting, own, other = None, (), (), [], [], []
     for step in range(chips):
         if step == 1:
             event = local_piece(plan[0], event)
@@ -218,8 +235,11 @@
                 if c:
                     groups.append((True, sum(parts[: c - 1]), parts[c - 1]))
                     use.append(other[c - 1])
-                outs = final(tuple(groups), core, args, local, use, outs)
-                event = outs[0]
+                send, waiting = (waiting, groups) if c else ([], groups)
+                outs, staged = final(
+                    tuple(groups), tuple(send), core, args, local, use, outs, staged
+                )
+                event = staged[0]
                 continue
             sent = jnp.where(at[step], total[c][:n], total[c][n:])
             if step:
@@ -229,7 +249,9 @@
             if step:
                 event = local_piece(plan[1 + (step - 1) * chunks + c], sent)
     last_group = (True, sum(parts[:-1]), parts[-1])
-    return tuple(final((last_group,), core, args, local, other[-1:], outs))
+    send = (*waiting, last_group)
+    outs, _ = final((last_group,), send, core, args, local, other[-1:], outs, staged)
+    return tuple(outs)
 
 
 def solution(mesh):

time: 30.8 us -> 30.4 us (0.987)
  waiting for transfers between devices: 5.02 us -> 3.46 us
  starting transfers between devices: 10.6 us -> 11.6 us
    ppermute x6, starting transfers between devices: 9.34 us -> 10.8 us  [exchange(): return lax.ppermute(value, ('seq', 'sub'), pairs)]
    ppermute x6, waiting for transfers between devices: 3.93 us -> 2.96 us  [exchange(): return lax.ppermute(value, ('seq', 'sub'), pairs)]
    ppermute x4, waiting for transfers between devices: 1.09 us -> 0.5 us  [swap(): return lax.ppermute(value, 'sub', [(0, 1), (1, 0)])]
    ppermute x4, starting transfers between devices: 1.22 us -> 0.78 us  [swap(): return lax.ppermute(value, 'sub', [(0, 1), (1, 0)])]
    pallas_call x4 -> x5, Pallas kernels: 7.56 us -> 7.53 us  [the longest x2 4.49 us: states(): pl.pallas_call(functools.partial(states_kernel, first, count, len(filled)...]
  transfers between devices with their start and end apart: 10 -> 10, of which waited for: 4 -> 4; matrix products, arithmetic and copies ran while one was open for 2% -> 2% of each run, Pallas kernels for 30% -> 33%
where the time goes in v9:
time: 30.4 us; the launch traced here: 30.2 us
  Pallas kernels  13.8 us (45%)
  starting transfers between devices  11.6 us (38%)
  waiting for transfers between devices  3.46 us (11%)
  between operations  0.82 us (3%)
  other arithmetic  0.47 us (2%)
    ppermute x6, starting transfers between devices, exchange(): return lax.ppermute(value, ('seq', 'sub'), pairs)  10.8 us
    pallas_call x3, Pallas kernels, intra(): pl.pallas_call(functools.partial(intra_kernel, first, heads), in_specs=[V...  6.24 us
    pallas_call x2, Pallas kernels, states(): pl.pallas_call(functools.partial(states_kernel, first, count, len(filled)...  4.49 us
    pallas_call x3, Pallas kernels, final(): pl.pallas_call(functools.partial(final_kernel, groups, send), in_specs=[S...  3.04 us
    ppermute x6, waiting for transfers between devices, exchange(): return lax.ppermute(value, ('seq', 'sub'), pairs)  2.96 us
    ppermute x4, starting transfers between devices, swap(): return lax.ppermute(value, 'sub', [(0, 1), (1, 0)])  0.78 us
  transfers between devices with their start and end apart: 10, of which 4 were waited for; matrix products, arithmetic and copies ran while one was open for 2% of the time, Pallas kernels for 33%

profile of v9, /device:TPU:0, one launch (start us, length us, event | category | flops | bytes accessed | tf_op | source)
XLA Modules:
  0.0 30.2 jit_solution(4962266303867295095)
XLA Ops:
  0.6 2.2 %states.2 = (bf16[512,1024]{1,0:T(8,128)(2,1)S(1)}, bf16[512,1024]{1,0:T(8,128)(2,1)S(1)}, bf16[512,1024]{1,0:T(8,128)(2,1)S(1)}, bf16[512,1024]{1,0:T(8,128)(2,...) custom-call(s32[1]{0:T(128)} %bitcast.core, bf16[512,1024]{1,0:T(8,128)(2,1)} %q_hbm.1, ...), custom_call_target="tpu_custom_call" | custom-call | tf_op jit(solution)/shard_map/states/pallas_call | solution.py:50
  2.9 0.5 %collective-permute-start.1 = (f32[4,128,128]{2,1,0:T(8,128)S(1)}, f32[4,128,128]{2,1,0:T(8,128)S(1)}, u32[]{:S(2)}, u32[]{:S(2)}) collective-permute-start(f32[4,128,128]{2,1,0:T(8,128)S(1)} %get-tuple-element.83), channel_id=1, source_target_pairs={{0,1},{1,0},{2,3},{3,2},{4,5},{5,4},{6,7},{7,6},{8,9},{9,8},{10,11... | collective-permute-start | bytes 786440 | tf_op jit(solution)/shard_map/ppermute | solution.py:158
  3.4 2.2 %states.3 = (bf16[512,1024]{1,0:T(8,128)(2,1)S(1)}, bf16[512,1024]{1,0:T(8,128)(2,1)S(1)}, bf16[512,1024]{1,0:T(8,128)(2,1)S(1)}, bf16[512,1024]{1,0:T(8,128)(2,...) custom-call(s32[1]{0:T(128)} %bitcast.core, ...), custom_call_target="tpu_custom_call", output_to_operand_aliasing={{0}: (5, {}), {1}: (6, {}), {2}: (7, {}), {3}: (8, {})} | custom-call | tf_op jit(solution)/shard_map/states/pallas_call | solution.py:50
  5.7 0.1 collective-permute-start
  5.8 0.0 collective-permute-done.1
  5.9 3.1 %collective-permute-start.3 = (f32[2,128,128]{2,1,0:T(8,128)S(1)}, f32[2,128,128]{2,1,0:T(8,128)S(1)}, u32[]{:S(2)}, u32[]{:S(2)}) collective-permute-start(f32[2,128,128]{2,1,0:T(8,128)S(1)} %slice_select_fusion.3), channel_id=1, source_target_pairs={{0,4},{1,5},{4,0},{5,1},{8,12},{9,13},{12,8},{13,9},{2,6},{3,7},{6... | collective-permute-start | bytes 393224 | tf_op jit(solution)/shard_map/ppermute | solution.py:168
  9.0 1.1 %collective-permute-start.2 = (f32[2,128,128]{2,1,0:T(8,128)S(1)}, f32[2,128,128]{2,1,0:T(8,128)S(1)}, u32[]{:S(2)}, u32[]{:S(2)}) collective-permute-start(f32[2,128,128]{2,1,0:T(8,128)S(1)} %slice_select_fusion.2), channel_id=1, source_target_pairs={{0,4},{1,5},{4,0},{5,1},{8,12},{9,13},{12,8},{13,9},{2,6},{3,7},{6... | collective-permute-start | bytes 393224 | tf_op jit(solution)/shard_map/ppermute | solution.py:168
  10.1 3.7 %intra.3 = (f32[512,1024]{1,0:T(8,128)S(1)}, f32[512,1024]{1,0:T(8,128)S(1)}, f32[512,1024]{1,0:T(8,128)S(1)}) custom-call(bf16[512,1024]{1,0:T(8,128)(2,1)S(1)} %get-tuple-element.99.q, bf16[512,1024]{1,0:T(8,128)(2,1)S(1)} %get-tuple-element.100.k, bf16[512,1024]{1,0:T(8,128)(2,1)S(1)} %get-tuple-element.101.v, bf16[512,1024]{1,0:T(8,128)(2,1)S(1)} %get-tuple-element.102.g), custom_call_target="tpu_custom_call" | custom-call | tf_op jit(solution)/shard_map/intra/pallas_call | solution.py:80
  13.8 0.1 collective-permute-start.5
  14.0 0.9 %intra.4 = (f32[512,1024]{1,0:T(8,128)S(1)}, f32[512,1024]{1,0:T(8,128)S(1)}, f32[512,1024]{1,0:T(8,128)S(1)}) custom-call(bf16[512,1024]{1,0:T(8,128)(2,1)S(1)} %get-tuple-element.99.q, bf16[512,1024]{1,0:T(8,128)(2,1)S(1)} %get-tuple-element.100.k, ...), custom_call_target="tpu_custom_call", output_to_operand_aliasing={{0}: (4, {}), {1}: (5, {}), {2}: (6, {})} | custom-call | tf_op jit(solution)/shard_map/intra/pallas_call | solution.py:80
  14.9 0.5 %collective-permute-done.2 = f32[2,128,128]{2,1,0:T(8,128)S(1)} collective-permute-done((f32[2,128,128]{2,1,0:T(8,128)S(1)}, f32[2,128,128]{2,1,0:T(8,128)S(1)}, u32[]{:S(2)}, u32[]{:S(2)}) %collective-permute-start.2) | collective-permute-done | bytes 131104 | tf_op jit(solution)/shard_map/ppermute | solution.py:168
  15.5 0.1 collective-permute-start.4
  15.6 1.6 %intra.5 = (f32[512,1024]{1,0:T(8,128)S(1)}, f32[512,1024]{1,0:T(8,128)S(1)}, f32[512,1024]{1,0:T(8,128)S(1)}) custom-call(bf16[512,1024]{1,0:T(8,128)(2,1)S(1)} %get-tuple-element.99.q, bf16[512,1024]{1,0:T(8,128)(2,1)S(1)} %get-tuple-element.100.k, ...), custom_call_target="tpu_custom_call", output_to_operand_aliasing={{0}: (4, {}), {1}: (5, {}), {2}: (6, {})} | custom-call | tf_op jit(solution)/shard_map/intra/pallas_call | solution.py:80
  17.2 3.9 %collective-permute-start.7 = (f32[2,128,128]{2,1,0:T(8,128)S(1)}, f32[2,128,128]{2,1,0:T(8,128)S(1)}, u32[]{:S(2)}, u32[]{:S(2)}) collective-permute-start(f32[2,128,128]{2,1,0:T(8,128)S(1)} %select_add_fusion.6), channel_id=1, source_target_pairs={{0,4},{1,5},{4,0},{5,1},{8,12},{9,13},{12,8},{13,9},{2,6},{3,7},{6... | collective-permute-start | bytes 393224 | tf_op jit(solution)/shard_map/ppermute | solution.py:168
  21.2 2.5 %collective-permute-start.6 = (f32[2,128,128]{2,1,0:T(8,128)S(1)}, f32[2,128,128]{2,1,0:T(8,128)S(1)}, u32[]{:S(2)}, u32[]{:S(2)}) collective-permute-start(f32[2,128,128]{2,1,0:T(8,128)S(1)} %select_add_fusion.7), channel_id=1, source_target_pairs={{0,4},{1,5},{4,0},{5,1},{8,12},{9,13},{12,8},{13,9},{2,6},{3,7},{6... | collective-permute-start | bytes 393224 | tf_op jit(solution)/shard_map/ppermute | solution.py:168
  23.7 0.7 %collective-permute-done.7 = f32[2,128,128]{2,1,0:T(8,128)S(1)} collective-permute-done((f32[2,128,128]{2,1,0:T(8,128)S(1)}, f32[2,128,128]{2,1,0:T(8,128)S(1)}, u32[]{:S(2)}, u32[]{:S(2)}) %collective-permute-start.7) | collective-permute-done | bytes 131104 | tf_op jit(solution)/shard_map/ppermute | solution.py:168
  24.4 0.1 collective-permute-start.9
  24.6 0.5 %final.3 = (bf16[512,1024]{1,0:T(8,128)(2,1)S(1)}, bf16[512,1024]{1,0:T(8,128)(2,1)S(1)}, bf16[512,1024]{1,0:T(8,128)(2,1)S(1)}) custom-call(s32[1]{0:T(128)} %bitcast.core, bf16[512,1024]{1,0:T(8,128)(2,1)S(1)} %get-tuple-element.100.k, bf16[512,1024]{1,0:T(8,128)(2,1)S(1)} %get-tuple-element.101.v, bf16[512,1024]{1,0:T(8,128)(2,1)S(1)} %get-tuple-element.102.g, ...), custom_call_target="tpu_custom_call" | custom-call | tf_op jit(solution)/shard_map/final/pallas_call | solution.py:136
  25.1 1.8 %collective-permute-done.6 = f32[2,128,128]{2,1,0:T(8,128)S(1)} collective-permute-done((f32[2,128,128]{2,1,0:T(8,128)S(1)}, f32[2,128,128]{2,1,0:T(8,128)S(1)}, u32[]{:S(2)}, u32[]{:S(2)}) %collective-permute-start.6) | collective-permute-done | bytes 131104 | tf_op jit(solution)/shard_map/ppermute | solution.py:168
  26.9 0.1 select_add_fusion.3
  27.0 0.1 collective-permute-start.8
  27.1 1.0 %final.4 = (bf16[512,1024]{1,0:T(8,128)(2,1)}, bf16[512,1024]{1,0:T(8,128)(2,1)}, bf16[512,1024]{1,0:T(8,128)(2,1)}, bf16[512,1024]{1,0:T(8,128)(2,1)S(1)}, bf16...) custom-call(s32[1]{0:T(128)} %bitcast.core, ...), custom_call_target="tpu_custom_call", output_to_operand_aliasing={{3}: (9, {}), {4}: (10, {}), {5}: (11, {})} | custom-call | tf_op jit(solution)/shard_map/final/pallas_call | solution.py:136
  28.1 0.5 %collective-permute-done.8.rest_0_ = f32[4,128,128]{2,1,0:T(8,128)S(1)} collective-permute-done((f32[4,128,128]{2,1,0:T(8,128)S(1)}, f32[4,128,128]{2,1,0:T(8,128)S(1)}, u32[]{:S(2)}, u32[]{:S(2)}) %collective-permute-start.8) | collective-permute-done | bytes 262176 | tf_op jit(solution)/shard_map/ppermute | solution.py:158
  28.6 1.5 %final.5 = (bf16[512,1024]{1,0:T(8,128)(2,1)}, bf16[512,1024]{1,0:T(8,128)(2,1)}, bf16[512,1024]{1,0:T(8,128)(2,1)}, bf16[512,1024]{1,0:T(8,128)(2,1)S(1)}, bf16...) custom-call(s32[1]{0:T(128)} %bitcast.core, ...), custom_call_target="tpu_custom_call", output_to_operand_aliasing={{0}: (8, {}), {1}: (9, {}), {2}: (10, {}), {3}: (11, {}), {... | custom-call | tf_op jit(solution)/shard_map/final/pallas_call | solution.py:136
  (20 shorter events, 0.4 us)
Async XLA Ops:
  2.9 2.9 %collective-permute-start.1 = (f32[4,128,128]{2,1,0:T(8,128)S(1)}, f32[4,128,128]{2,1,0:T(8,128)S(1)}, u32[]{:S(2)}, u32[]{:S(2)}) collective-permute-start(f32[4,128,128]{2,1,0:T(8,128)S(1)} %get-tuple-element.83), channel_id=1, source_target_pairs={{0,1},{1,0},{2,3},{3,2},{4,5},{5,4},{6,7},{7,6},{8,9},{9,8},{10,11... | collective-permute-start | bytes 786440 | tf_op jit(solution)/shard_map/ppermute | solution.py:158
  5.7 3.3 %collective-permute-start = (f32[4,128,128]{2,1,0:T(8,128)S(1)}, f32[4,128,128]{2,1,0:T(8,128)S(1)}, u32[]{:S(2)}, u32[]{:S(2)}) collective-permute-start(f32[4,128,128]{2,1,0:T(8,128)S(1)} %get-tuple-element.80), channel_id=1, source_target_pairs={{0,1},{1,0},{2,3},{3,2},{4,5},{5,4},{6,7},{7,6},{8,9},{9,8},{10,11... | collective-permute-start | bytes 786440 | tf_op jit(solution)/shard_map/ppermute | solution.py:158
  5.9 7.9 %collective-permute-start.3 = (f32[2,128,128]{2,1,0:T(8,128)S(1)}, f32[2,128,128]{2,1,0:T(8,128)S(1)}, u32[]{:S(2)}, u32[]{:S(2)}) collective-permute-start(f32[2,128,128]{2,1,0:T(8,128)S(1)} %slice_select_fusion.3), channel_id=1, source_target_pairs={{0,4},{1,5},{4,0},{5,1},{8,12},{9,13},{12,8},{13,9},{2,6},{3,7},{6... | collective-permute-start | bytes 393224 | tf_op jit(solution)/shard_map/ppermute | solution.py:168
  9.0 6.4 %collective-permute-start.2 = (f32[2,128,128]{2,1,0:T(8,128)S(1)}, f32[2,128,128]{2,1,0:T(8,128)S(1)}, u32[]{:S(2)}, u32[]{:S(2)}) collective-permute-start(f32[2,128,128]{2,1,0:T(8,128)S(1)} %slice_select_fusion.2), channel_id=1, source_target_pairs={{0,4},{1,5},{4,0},{5,1},{8,12},{9,13},{12,8},{13,9},{2,6},{3,7},{6... | collective-permute-start | bytes 393224 | tf_op jit(solution)/shard_map/ppermute | solution.py:168
  13.8 3.3 %collective-permute-start.5 = (f32[2,128,128]{2,1,0:T(8,128)S(1)}, f32[2,128,128]{2,1,0:T(8,128)S(1)}, u32[]{:S(2)}, u32[]{:S(2)}) collective-permute-start(f32[2,128,128]{2,1,0:T(8,128)S(1)} %select_add_fusion.8), channel_id=1, source_target_pairs={{0,1},{1,0},{4,8},{5,9},{8,4},{9,5},{12,13},{13,12},{2,3},{3,2},{6... | collective-permute-start | bytes 393224 | tf_op jit(solution)/shard_map/ppermute | solution.py:168
  15.5 5.6 %collective-permute-start.4 = (f32[2,128,128]{2,1,0:T(8,128)S(1)}, f32[2,128,128]{2,1,0:T(8,128)S(1)}, u32[]{:S(2)}, u32[]{:S(2)}) collective-permute-start(f32[2,128,128]{2,1,0:T(8,128)S(1)} %select_add_fusion.9), channel_id=1, source_target_pairs={{0,1},{1,0},{4,8},{5,9},{8,4},{9,5},{12,13},{13,12},{2,3},{3,2},{6... | collective-permute-start | bytes 393224 | tf_op jit(solution)/shard_map/ppermute | solution.py:168
  17.2 7.1 %collective-permute-start.7 = (f32[2,128,128]{2,1,0:T(8,128)S(1)}, f32[2,128,128]{2,1,0:T(8,128)S(1)}, u32[]{:S(2)}, u32[]{:S(2)}) collective-permute-start(f32[2,128,128]{2,1,0:T(8,128)S(1)} %select_add_fusion.6), channel_id=1, source_target_pairs={{0,4},{1,5},{4,0},{5,1},{8,12},{9,13},{12,8},{13,9},{2,6},{3,7},{6... | collective-permute-start | bytes 393224 | tf_op jit(solution)/shard_map/ppermute | solution.py:168
  21.2 5.7 %collective-permute-start.6 = (f32[2,128,128]{2,1,0:T(8,128)S(1)}, f32[2,128,128]{2,1,0:T(8,128)S(1)}, u32[]{:S(2)}, u32[]{:S(2)}) collective-permute-start(f32[2,128,128]{2,1,0:T(8,128)S(1)} %select_add_fusion.7), channel_id=1, source_target_pairs={{0,4},{1,5},{4,0},{5,1},{8,12},{9,13},{12,8},{13,9},{2,6},{3,7},{6... | collective-permute-start | bytes 393224 | tf_op jit(solution)/shard_map/ppermute | solution.py:168
  24.4 2.7 %collective-permute-start.9 = (f32[4,128,128]{2,1,0:T(8,128)S(1)}, f32[4,128,128]{2,1,0:T(8,128)S(1)}, u32[]{:S(2)}, u32[]{:S(2)}) collective-permute-start(f32[4,128,128]{2,1,0:T(8,128)S(1)} %pad_maximum_fusion.3), channel_id=1, source_target_pairs={{0,1},{1,0},{2,3},{3,2},{4,5},{5,4},{6,7},{7,6},{8,9},{9,8},{10,11... | collective-permute-start | bytes 786440 | tf_op jit(solution)/shard_map/ppermute | solution.py:158
  27.0 1.6 %collective-permute-start.8 = (f32[4,128,128]{2,1,0:T(8,128)S(1)}, f32[4,128,128]{2,1,0:T(8,128)S(1)}, u32[]{:S(2)}, u32[]{:S(2)}) collective-permute-start(f32[4,128,128]{2,1,0:T(8,128)S(1)} %pad_maximum_fusion.1), channel_id=1, source_target_pairs={{0,1},{1,0},{2,3},{3,2},{4,5},{5,4},{6,7},{7,6},{8,9},{9,8},{10,11... | collective-permute-start | bytes 786440 | tf_op jit(solution)/shard_map/ppermute | solution.py:158

commit v10 on v9

--- a/solution.py
+++ b/solution.py
@@ -9,7 +9,7 @@
 
 DH = 128
 CHUNKS = 2
-PLAN = (5, 1, 2, 0, 0)
+PLAN = (4, 1, 3, 0, 0)
 F32 = jnp.float32
 BF16 = jnp.bfloat16
 VMEM = pl.BlockSpec(memory_space=pltpu.VMEM)
@@ -27,38 +27,58 @@
     return slice(head * DH, (head + 1) * DH)
 
 
-def states_kernel(first, count, aliased, core, q_hbm, k_hbm, v_hbm, g_hbm, *rest):
-    q, k, v, g, keep, give, sems = rest[aliased:]
+def states_kernel(parts, core, q_hbm, k_hbm, v_hbm, g_hbm, q, k, v, g, *rest):
+    keep, give, sems = rest[: len(parts)], rest[len(parts) : 2 * len(parts)], rest[-1]
     width = q.shape[1] // 2
-    copies = []
-    for source, target in ((k_hbm, k), (v_hbm, v), (q_hbm, q), (g_hbm, g)):
+    loads = []
+    for pair in (((k_hbm, k), (v_hbm, v)), ((q_hbm, q), (g_hbm, g))):
         for half in (0, 1):
-            c = pl.ds(half * width + first * DH, count * DH)
-            copy = pltpu.make_async_copy(source.at[:, c], target.at[:, c], sems.at[len(copies)])
-            copy.start()
-            copies.append(copy)
-    for n, (x, y) in enumerate(((k, v), (q, g))):
-        for copy in copies[4 * n : 4 * n + 4]:
+            c = slice(half * width, (half + 1) * width)
+            copies = [
+                pltpu.make_async_copy(
+                    source.at[:, c], target.at[:, c], sems.at[2 * len(loads) + i]
+                )
+                for i, (source, target) in enumerate(pair)
+            ]
+            loads.append(copies)
+            for copy in copies:
+                copy.start()
+
+    def fill(outs, x, y, place, half):
+        h = 0
+        for out, count in zip(outs, parts):
+            for i in range(count):
+                c = slice(half * width + h * DH, half * width + (h + 1) * DH)
+                out[place * count + i] = product(x[:, c], y[:, c], 0, 0)
+                h += 1
+
+    for n, copies in enumerate(loads):
+        place, half = divmod(n, 2)
+        x, y = ((k, v), (q, g))[place]
+        for copy in copies:
             copy.wait()
-        for out, half in ((give, 1 - core[0]), (keep, core[0])):
-            for i in range(count):
-                c = pl.ds(pl.multiple_of(half * width + (first + i) * DH, DH), DH)
-                out[n * count + i] = product(x[:, c], y[:, c], 0, 0)
-
-
-def states(core, first, count, args, filled):
+
+        @pl.when(core[0] == half)
+        def _():
+            fill(keep, x, y, place, half)
+
+        @pl.when(core[0] != half)
+        def _():
+            fill(give, x, y, place, half)
+
+
+def states(core, parts, args):
+    outs = [pltpu.VMEM((2 * n, DH, DH), F32) for n in parts] * 2
     result = pl.pallas_call(
-        functools.partial(states_kernel, first, count, len(filled)),
-        in_specs=[SMEM] + [HBM] * 4 + [VMEM] * len(filled),
-        out_specs=[VMEM] * 6,
-        out_shape=[pltpu.VMEM(args[0].shape, BF16)] * 4
-        + [pltpu.VMEM((2 * count, DH, DH), F32)] * 2,
+        functools.partial(states_kernel, parts),
+        in_specs=[SMEM] + [HBM] * 4,
+        out_specs=[VMEM] * (4 + len(outs)),
+        out_shape=[pltpu.VMEM(args[0].shape, BF16)] * 4 + outs,
         scratch_shapes=[pltpu.SemaphoreType.DMA((8,))],
-        input_output_aliases={5 + i: i for i in range(len(filled))},
         compiler_params=pltpu.CompilerParams(vmem_limit_bytes=8 << 20),
         name="states",
-    )(core, *[pltpu.with_memory_space_constraint(x, pltpu.HBM) for x in args], *filled)
-    return result[:4], *result[4:]
+    )(core, *[pltpu.with_memory_space_constraint(x, pltpu.HBM) for x in args])
+    return result[:4], list(result[4 : 4 + len(parts)]), list(result[4 + len(parts) :])
 
 
 def intra_kernel(first, heads, q, k, v, g, *rest):
@@ -181,11 +201,7 @@
     at = [chip == c for c in range(chips)]
     core, first_core, *rest = lax.optimization_barrier((core.reshape(1), core == 0, *at, *args))
     at, args = rest[:chips], rest[chips:]
-    given, args, keep, give = args, (), [], []
-    for c, n in enumerate(parts):
-        args, kept, gave = states(core, sum(parts[:c]), n, given, args)
-        keep.append(kept)
-        give.append(gave)
+    args, keep, give = states(core, parts, args)
     got = [swap(x) for x in give]
     total = [None] * chunks
     local, done = (), 0
@@ -233,9 +249,9 @@
                 other.append(swap(lend))
                 groups, use = [(False, sum(parts[:c]), n)], [own[c]]
                 if c:
-                    groups.append((True, sum(parts[: c - 1]), parts[c - 1]))
-                    use.append(other[c - 1])
-                send, waiting = (waiting, groups) if c else ([], groups)
+                    groups.insert(0, (True, sum(parts[: c - 1]), parts[c - 1]))
+                    use.insert(0, other[c - 1])
+                send, waiting = ([*waiting, *groups[:-1]], groups[-1:]) if c else ([], groups)
                 outs, staged = final(
                     tuple(groups), tuple(send), core, args, local, use, outs, staged
                 )

time: 30.4 us -> 29.6 us (0.974)
  waiting for transfers between devices: 3.46 us -> 6.45 us
  starting transfers between devices: 11.6 us -> 9.38 us
  Pallas kernels: 13.8 us -> 12.4 us
    ppermute x6, waiting for transfers between devices: 2.96 us -> 5.31 us  [exchange(): return lax.ppermute(value, ('seq', 'sub'), pairs)]
    ppermute x6, starting transfers between devices: 10.8 us -> 8.65 us  [exchange(): return lax.ppermute(value, ('seq', 'sub'), pairs)]
    pallas_call x2 -> x1, Pallas kernels: 4.49 us -> 2.82 us  [states(): pl.pallas_call(functools.partial(states_kernel, parts), in_specs=[SMEM] +...]
    ppermute x4, waiting for transfers between devices: 0.5 us -> 1.14 us  [swap(): return lax.ppermute(value, 'sub', [(0, 1), (1, 0)])]
  transfers between devices with their start and end apart: 10 -> 10, of which waited for: 4 -> 5; matrix products, arithmetic and copies ran while one was open for 2% -> 2% of each run, Pallas kernels for 33% -> 28%
where the time goes in v10:
time: 29.6 us; the launch traced here: 29.5 us
  Pallas kernels  12.4 us (42%)
  starting transfers between devices  9.38 us (32%)
  waiting for transfers between devices  6.45 us (22%)
  between operations  0.82 us (3%)
  other arithmetic  0.48 us (2%)
    ppermute x6, starting transfers between devices, exchange(): return lax.ppermute(value, ('seq', 'sub'), pairs)  8.65 us
    pallas_call x3, Pallas kernels, intra(): pl.pallas_call(functools.partial(intra_kernel, first, heads), in_specs=[V...  6.25 us
    ppermute x6, waiting for transfers between devices, exchange(): return lax.ppermute(value, ('seq', 'sub'), pairs)  5.31 us
    pallas_call x3, Pallas kernels, final(): pl.pallas_call(functools.partial(final_kernel, groups, send), in_specs=[S...  3.3 us
    pallas_call x1, Pallas kernels, states(): pl.pallas_call(functools.partial(states_kernel, parts), in_specs=[SMEM] +...  2.82 us
    ppermute x4, waiting for transfers between devices, swap(): return lax.ppermute(value, 'sub', [(0, 1), (1, 0)])  1.14 us
    ppermute x4, starting transfers between devices, swap(): return lax.ppermute(value, 'sub', [(0, 1), (1, 0)])  0.73 us
  transfers between devices with their start and end apart: 10, of which 5 were waited for; matrix products, arithmetic and copies ran while one was open for 2% of the time, Pallas kernels for 28%

profile of v10, /device:TPU:0, one launch (start us, length us, event | category | flops | bytes accessed | tf_op | source)
XLA Modules:
  0.0 29.5 jit_solution(17728616095498438012)
XLA Ops:
  0.6 2.8 %states.1 = (bf16[512,1024]{1,0:T(8,128)(2,1)S(1)}, bf16[512,1024]{1,0:T(8,128)(2,1)S(1)}, bf16[512,1024]{1,0:T(8,128)(2,1)S(1)}, bf16[512,1024]{1,0:T(8,128)(2,...) custom-call(s32[1]{0:T(128)} %bitcast.core, ...), custom_call_target="tpu_custom_call" | custom-call | tf_op jit(solution)/shard_map/states/pallas_call | solution.py:72
  3.5 0.5 %collective-permute-start.1 = (f32[4,128,128]{2,1,0:T(8,128)S(1)}, f32[4,128,128]{2,1,0:T(8,128)S(1)}, u32[]{:S(2)}, u32[]{:S(2)}) collective-permute-start(f32[4,128,128]{2,1,0:T(8,128)S(1)} %get-tuple-element.75), channel_id=1, source_target_pairs={{0,1},{1,0},{2,3},{3,2},{4,5},{5,4},{6,7},{7,6},{8,9},{9,8},{10,11... | collective-permute-start | bytes 786440 | tf_op jit(solution)/shard_map/ppermute | solution.py:178
  4.0 0.1 collective-permute-start
  4.1 1.1 %collective-permute-done.1 = f32[4,128,128]{2,1,0:T(8,128)S(1)} collective-permute-done((f32[4,128,128]{2,1,0:T(8,128)S(1)}, f32[4,128,128]{2,1,0:T(8,128)S(1)}, u32[]{:S(2)}, u32[]{:S(2)}) %collective-permute-start.1) | collective-permute-done | bytes 262176 | tf_op jit(solution)/shard_map/ppermute | solution.py:178
  5.2 3.0 %collective-permute-start.3 = (f32[2,128,128]{2,1,0:T(8,128)S(1)}, f32[2,128,128]{2,1,0:T(8,128)S(1)}, u32[]{:S(2)}, u32[]{:S(2)}) collective-permute-start(f32[2,128,128]{2,1,0:T(8,128)S(1)} %slice_select_fusion.3), channel_id=1, source_target_pairs={{0,4},{1,5},{4,0},{5,1},{8,12},{9,13},{12,8},{13,9},{2,6},{3,7},{6... | collective-permute-start | bytes 393224 | tf_op jit(solution)/shard_map/ppermute | solution.py:188
  8.3 0.3 %collective-permute-start.2 = (f32[2,128,128]{2,1,0:T(8,128)S(1)}, f32[2,128,128]{2,1,0:T(8,128)S(1)}, u32[]{:S(2)}, u32[]{:S(2)}) collective-permute-start(f32[2,128,128]{2,1,0:T(8,128)S(1)} %slice_select_fusion.2), channel_id=1, source_target_pairs={{0,4},{1,5},{4,0},{5,1},{8,12},{9,13},{12,8},{13,9},{2,6},{3,7},{6... | collective-permute-start | bytes 393224 | tf_op jit(solution)/shard_map/ppermute | solution.py:188
  8.6 3.0 %intra.3 = (f32[512,1024]{1,0:T(8,128)S(1)}, f32[512,1024]{1,0:T(8,128)S(1)}, f32[512,1024]{1,0:T(8,128)S(1)}) custom-call(bf16[512,1024]{1,0:T(8,128)(2,1)S(1)} %get-tuple-element.91.q, bf16[512,1024]{1,0:T(8,128)(2,1)S(1)} %get-tuple-element.92.k, bf16[512,1024]{1,0:T(8,128)(2,1)S(1)} %get-tuple-element.93.v, bf16[512,1024]{1,0:T(8,128)(2,1)S(1)} %get-tuple-element.94.g), custom_call_target="tpu_custom_call" | custom-call | tf_op jit(solution)/shard_map/intra/pallas_call | solution.py:100
  11.6 0.9 %collective-permute-done.3 = f32[2,128,128]{2,1,0:T(8,128)S(1)} collective-permute-done((f32[2,128,128]{2,1,0:T(8,128)S(1)}, f32[2,128,128]{2,1,0:T(8,128)S(1)}, u32[]{:S(2)}, u32[]{:S(2)}) %collective-permute-start.3) | collective-permute-done | bytes 131104 | tf_op jit(solution)/shard_map/ppermute | solution.py:188
  12.5 0.1 collective-permute-start.5
  12.6 0.9 %intra.4 = (f32[512,1024]{1,0:T(8,128)S(1)}, f32[512,1024]{1,0:T(8,128)S(1)}, f32[512,1024]{1,0:T(8,128)S(1)}) custom-call(bf16[512,1024]{1,0:T(8,128)(2,1)S(1)} %get-tuple-element.91.q, bf16[512,1024]{1,0:T(8,128)(2,1)S(1)} %get-tuple-element.92.k, ...), custom_call_target="tpu_custom_call", output_to_operand_aliasing={{0}: (4, {}), {1}: (5, {}), {2}: (6, {})} | custom-call | tf_op jit(solution)/shard_map/intra/pallas_call | solution.py:100
  13.6 1.3 %collective-permute-done.2 = f32[2,128,128]{2,1,0:T(8,128)S(1)} collective-permute-done((f32[2,128,128]{2,1,0:T(8,128)S(1)}, f32[2,128,128]{2,1,0:T(8,128)S(1)}, u32[]{:S(2)}, u32[]{:S(2)}) %collective-permute-start.2) | collective-permute-done | bytes 131104 | tf_op jit(solution)/shard_map/ppermute | solution.py:188
  14.9 0.1 collective-permute-start.4
  14.9 2.3 %intra.5 = (f32[512,1024]{1,0:T(8,128)S(1)}, f32[512,1024]{1,0:T(8,128)S(1)}, f32[512,1024]{1,0:T(8,128)S(1)}) custom-call(bf16[512,1024]{1,0:T(8,128)(2,1)S(1)} %get-tuple-element.91.q, bf16[512,1024]{1,0:T(8,128)(2,1)S(1)} %get-tuple-element.92.k, ...), custom_call_target="tpu_custom_call", output_to_operand_aliasing={{0}: (4, {}), {1}: (5, {}), {2}: (6, {})} | custom-call | tf_op jit(solution)/shard_map/intra/pallas_call | solution.py:100
  17.3 3.6 %collective-permute-start.7 = (f32[2,128,128]{2,1,0:T(8,128)S(1)}, f32[2,128,128]{2,1,0:T(8,128)S(1)}, u32[]{:S(2)}, u32[]{:S(2)}) collective-permute-start(f32[2,128,128]{2,1,0:T(8,128)S(1)} %select_add_fusion.6), channel_id=1, source_target_pairs={{0,4},{1,5},{4,0},{5,1},{8,12},{9,13},{12,8},{13,9},{2,6},{3,7},{6... | collective-permute-start | bytes 393224 | tf_op jit(solution)/shard_map/ppermute | solution.py:188
  20.9 1.6 %collective-permute-start.6 = (f32[2,128,128]{2,1,0:T(8,128)S(1)}, f32[2,128,128]{2,1,0:T(8,128)S(1)}, u32[]{:S(2)}, u32[]{:S(2)}) collective-permute-start(f32[2,128,128]{2,1,0:T(8,128)S(1)} %select_add_fusion.7), channel_id=1, source_target_pairs={{0,4},{1,5},{4,0},{5,1},{8,12},{9,13},{12,8},{13,9},{2,6},{3,7},{6... | collective-permute-start | bytes 393224 | tf_op jit(solution)/shard_map/ppermute | solution.py:188
  22.5 2.5 %collective-permute-done.7 = f32[2,128,128]{2,1,0:T(8,128)S(1)} collective-permute-done((f32[2,128,128]{2,1,0:T(8,128)S(1)}, f32[2,128,128]{2,1,0:T(8,128)S(1)}, u32[]{:S(2)}, u32[]{:S(2)}) %collective-permute-start.7) | collective-permute-done | bytes 131104 | tf_op jit(solution)/shard_map/ppermute | solution.py:188
  25.0 0.1 select_add_fusion.3
  25.1 0.1 collective-permute-start.9
  25.2 0.5 %final.3 = (bf16[512,1024]{1,0:T(8,128)(2,1)S(1)}, bf16[512,1024]{1,0:T(8,128)(2,1)S(1)}, bf16[512,1024]{1,0:T(8,128)(2,1)S(1)}) custom-call(s32[1]{0:T(128)} %bitcast.core, bf16[512,1024]{1,0:T(8,128)(2,1)S(1)} %get-tuple-element.92.k, bf16[512,1024]{1,0:T(8,128)(2,1)S(1)} %get-tuple-element.93.v, bf16[512,1024]{1,0:T(8,128)(2,1)S(1)} %get-tuple-element.94.g, ...), custom_call_target="tpu_custom_call" | custom-call | tf_op jit(solution)/shard_map/final/pallas_call | solution.py:156
  25.8 0.7 %collective-permute-done.6 = f32[2,128,128]{2,1,0:T(8,128)S(1)} collective-permute-done((f32[2,128,128]{2,1,0:T(8,128)S(1)}, f32[2,128,128]{2,1,0:T(8,128)S(1)}, u32[]{:S(2)}, u32[]{:S(2)}) %collective-permute-start.6) | collective-permute-done | bytes 131104 | tf_op jit(solution)/shard_map/ppermute | solution.py:188
  26.4 0.1 select_add_fusion.1
  26.5 0.1 collective-permute-start.8
  26.7 1.4 %final.4 = (bf16[512,1024]{1,0:T(8,128)(2,1)}, bf16[512,1024]{1,0:T(8,128)(2,1)}, bf16[512,1024]{1,0:T(8,128)(2,1)}, bf16[512,1024]{1,0:T(8,128)(2,1)S(1)}, bf16...) custom-call(s32[1]{0:T(128)} %bitcast.core, ...), custom_call_target="tpu_custom_call", output_to_operand_aliasing={{3}: (9, {}), {4}: (10, {}), {5}: (11, {})} | custom-call | tf_op jit(solution)/shard_map/final/pallas_call | solution.py:156
  28.1 1.3 %final.5 = (bf16[512,1024]{1,0:T(8,128)(2,1)}, bf16[512,1024]{1,0:T(8,128)(2,1)}, bf16[512,1024]{1,0:T(8,128)(2,1)}, bf16[512,1024]{1,0:T(8,128)(2,1)S(1)}, bf16...) custom-call(s32[1]{0:T(128)} %bitcast.core, ...), custom_call_target="tpu_custom_call", output_to_operand_aliasing={{0}: (8, {}), {1}: (9, {}), {2}: (10, {}), {3}: (11, {}), {... | custom-call | tf_op jit(solution)/shard_map/final/pallas_call | solution.py:156
  (19 shorter events, 0.4 us)
Async XLA Ops:
  3.5 1.7 %collective-permute-start.1 = (f32[4,128,128]{2,1,0:T(8,128)S(1)}, f32[4,128,128]{2,1,0:T(8,128)S(1)}, u32[]{:S(2)}, u32[]{:S(2)}) collective-permute-start(f32[4,128,128]{2,1,0:T(8,128)S(1)} %get-tuple-element.75), channel_id=1, source_target_pairs={{0,1},{1,0},{2,3},{3,2},{4,5},{5,4},{6,7},{7,6},{8,9},{9,8},{10,11... | collective-permute-start | bytes 786440 | tf_op jit(solution)/shard_map/ppermute | solution.py:178
  4.0 4.2 %collective-permute-start = (f32[4,128,128]{2,1,0:T(8,128)S(1)}, f32[4,128,128]{2,1,0:T(8,128)S(1)}, u32[]{:S(2)}, u32[]{:S(2)}) collective-permute-start(f32[4,128,128]{2,1,0:T(8,128)S(1)} %get-tuple-element.72), channel_id=1, source_target_pairs={{0,1},{1,0},{2,3},{3,2},{4,5},{5,4},{6,7},{7,6},{8,9},{9,8},{10,11... | collective-permute-start | bytes 786440 | tf_op jit(solution)/shard_map/ppermute | solution.py:178
  5.2 7.3 %collective-permute-start.3 = (f32[2,128,128]{2,1,0:T(8,128)S(1)}, f32[2,128,128]{2,1,0:T(8,128)S(1)}, u32[]{:S(2)}, u32[]{:S(2)}) collective-permute-start(f32[2,128,128]{2,1,0:T(8,128)S(1)} %slice_select_fusion.3), channel_id=1, source_target_pairs={{0,4},{1,5},{4,0},{5,1},{8,12},{9,13},{12,8},{13,9},{2,6},{3,7},{6... | collective-permute-start | bytes 393224 | tf_op jit(solution)/shard_map/ppermute | solution.py:188
  8.3 6.5 %collective-permute-start.2 = (f32[2,128,128]{2,1,0:T(8,128)S(1)}, f32[2,128,128]{2,1,0:T(8,128)S(1)}, u32[]{:S(2)}, u32[]{:S(2)}) collective-permute-start(f32[2,128,128]{2,1,0:T(8,128)S(1)} %slice_select_fusion.2), channel_id=1, source_target_pairs={{0,4},{1,5},{4,0},{5,1},{8,12},{9,13},{12,8},{13,9},{2,6},{3,7},{6... | collective-permute-start | bytes 393224 | tf_op jit(solution)/shard_map/ppermute | solution.py:188
  12.5 4.7 %collective-permute-start.5 = (f32[2,128,128]{2,1,0:T(8,128)S(1)}, f32[2,128,128]{2,1,0:T(8,128)S(1)}, u32[]{:S(2)}, u32[]{:S(2)}) collective-permute-start(f32[2,128,128]{2,1,0:T(8,128)S(1)} %select_add_fusion.8), channel_id=1, source_target_pairs={{0,1},{1,0},{4,8},{5,9},{8,4},{9,5},{12,13},{13,12},{2,3},{3,2},{6... | collective-permute-start | bytes 393224 | tf_op jit(solution)/shard_map/ppermute | solution.py:188
  14.9 6.0 %collective-permute-start.4 = (f32[2,128,128]{2,1,0:T(8,128)S(1)}, f32[2,128,128]{2,1,0:T(8,128)S(1)}, u32[]{:S(2)}, u32[]{:S(2)}) collective-permute-start(f32[2,128,128]{2,1,0:T(8,128)S(1)} %select_add_fusion.9), channel_id=1, source_target_pairs={{0,1},{1,0},{4,8},{5,9},{8,4},{9,5},{12,13},{13,12},{2,3},{3,2},{6... | collective-permute-start | bytes 393224 | tf_op jit(solution)/shard_map/ppermute | solution.py:188
  17.3 7.7 %collective-permute-start.7 = (f32[2,128,128]{2,1,0:T(8,128)S(1)}, f32[2,128,128]{2,1,0:T(8,128)S(1)}, u32[]{:S(2)}, u32[]{:S(2)}) collective-permute-start(f32[2,128,128]{2,1,0:T(8,128)S(1)} %select_add_fusion.6), channel_id=1, source_target_pairs={{0,4},{1,5},{4,0},{5,1},{8,12},{9,13},{12,8},{13,9},{2,6},{3,7},{6... | collective-permute-start | bytes 393224 | tf_op jit(solution)/shard_map/ppermute | solution.py:188
  20.9 5.5 %collective-permute-start.6 = (f32[2,128,128]{2,1,0:T(8,128)S(1)}, f32[2,128,128]{2,1,0:T(8,128)S(1)}, u32[]{:S(2)}, u32[]{:S(2)}) collective-permute-start(f32[2,128,128]{2,1,0:T(8,128)S(1)} %select_add_fusion.7), channel_id=1, source_target_pairs={{0,4},{1,5},{4,0},{5,1},{8,12},{9,13},{12,8},{13,9},{2,6},{3,7},{6... | collective-permute-start | bytes 393224 | tf_op jit(solution)/shard_map/ppermute | solution.py:188
  25.1 1.6 %collective-permute-start.9 = (f32[4,128,128]{2,1,0:T(8,128)S(1)}, f32[4,128,128]{2,1,0:T(8,128)S(1)}, u32[]{:S(2)}, u32[]{:S(2)}) collective-permute-start(f32[4,128,128]{2,1,0:T(8,128)S(1)} %pad_maximum_fusion.2), channel_id=1, source_target_pairs={{0,1},{1,0},{2,3},{3,2},{4,5},{5,4},{6,7},{7,6},{8,9},{9,8},{10,11... | collective-permute-start | bytes 786440 | tf_op jit(solution)/shard_map/ppermute | solution.py:178
  26.5 1.6 %collective-permute-start.8 = (f32[4,128,128]{2,1,0:T(8,128)S(1)}, f32[4,128,128]{2,1,0:T(8,128)S(1)}, u32[]{:S(2)}, u32[]{:S(2)}) collective-permute-start(f32[4,128,128]{2,1,0:T(8,128)S(1)} %pad_maximum_fusion.1), channel_id=1, source_target_pairs={{0,1},{1,0},{2,3},{3,2},{4,5},{5,4},{6,7},{7,6},{8,9},{9,8},{10,11... | collective-permute-start | bytes 786440 | tf_op jit(solution)/shard_map/ppermute | solution.py:178

commit v11 on v10

--- a/solution.py
+++ b/solution.py
@@ -9,7 +9,7 @@
 
 DH = 128
 CHUNKS = 2
-PLAN = (4, 1, 3, 0, 0)
+PLAN = (0, 1, 1, 2, 2, 2)
 F32 = jnp.float32
 BF16 = jnp.bfloat16
 VMEM = pl.BlockSpec(memory_space=pltpu.VMEM)
@@ -27,73 +27,91 @@
     return slice(head * DH, (head + 1) * DH)
 
 
-def states_kernel(parts, core, q_hbm, k_hbm, v_hbm, g_hbm, q, k, v, g, *rest):
+def states_kernel(parts, later, place, q_hbm, k_hbm, v_hbm, g_hbm, *rest):
+    q, k, v, g = rest[4 * later : 4 * later + 4]
+    rest = rest[4 * later + 4 :]
     keep, give, sems = rest[: len(parts)], rest[len(parts) : 2 * len(parts)], rest[-1]
     width = q.shape[1] // 2
-    loads = []
-    for pair in (((k_hbm, k), (v_hbm, v)), ((q_hbm, q), (g_hbm, g))):
+
+    def fill(outs, x, y, half):
+        h = 0
+        for out in outs:
+            for i in range(out.shape[0]):
+                c = slice(half * width + h * DH, half * width + (h + 1) * DH)
+                out[i] = product(x[:, c], y[:, c], 0, 0)
+                h += 1
+
+    def run(x_hbm, y_hbm, x, y):
+        loads = []
         for half in (0, 1):
             c = slice(half * width, (half + 1) * width)
-            copies = [
-                pltpu.make_async_copy(
-                    source.at[:, c], target.at[:, c], sems.at[2 * len(loads) + i]
+            for i, (source, target) in enumerate(((x_hbm, x), (y_hbm, y))):
+                loads.append(
+                    pltpu.make_async_copy(
+                        source.at[:, c], target.at[:, c], sems.at[2 * half + i]
+                    )
                 )
-                for i, (source, target) in enumerate(pair)
-            ]
-            loads.append(copies)
-            for copy in copies:
-                copy.start()
-
-    def fill(outs, x, y, place, half):
-        h = 0
-        for out, count in zip(outs, parts):
-            for i in range(count):
-                c = slice(half * width + h * DH, half * width + (h + 1) * DH)
-                out[place * count + i] = product(x[:, c], y[:, c], 0, 0)
-                h += 1
-
-    for n, copies in enumerate(loads):
-        place, half = divmod(n, 2)
-        x, y = ((k, v), (q, g))[place]
-        for copy in copies:
-            copy.wait()
-
-        @pl.when(core[0] == half)
-        def _():
-            fill(keep, x, y, place, half)
-
-        @pl.when(core[0] != half)
-        def _():
-            fill(give, x, y, place, half)
-
-
-def states(core, parts, args):
-    outs = [pltpu.VMEM((2 * n, DH, DH), F32) for n in parts] * 2
+                loads[-1].start()
+        for half in (0, 1):
+            for copy in loads[2 * half : 2 * half + 2]:
+                copy.wait()
+
+            @pl.when(place[0] == half)
+            def _():
+                fill(keep, x, y, half)
+
+            @pl.when(place[0] != half)
+            def _():
+                fill(give, x, y, half)
+
+    @pl.when(place[1] == later)
+    def _():
+        run(k_hbm, v_hbm, k, v)
+
+    @pl.when(place[1] != later)
+    def _():
+        run(q_hbm, g_hbm, q, g)
+
+
+def states(place, parts, args, filled):
+    outs = [pltpu.VMEM((n, DH, DH), F32) for n in parts] * 2
     result = pl.pallas_call(
-        functools.partial(states_kernel, parts),
-        in_specs=[SMEM] + [HBM] * 4,
+        functools.partial(states_kernel, parts, 1 if filled else 0),
+        in_specs=[SMEM] + [HBM] * 4 + [VMEM] * len(filled),
         out_specs=[VMEM] * (4 + len(outs)),
         out_shape=[pltpu.VMEM(args[0].shape, BF16)] * 4 + outs,
-        scratch_shapes=[pltpu.SemaphoreType.DMA((8,))],
+        scratch_shapes=[pltpu.SemaphoreType.DMA((4,))],
+        input_output_aliases={5 + i: i for i in range(len(filled))},
         compiler_params=pltpu.CompilerParams(vmem_limit_bytes=8 << 20),
         name="states",
-    )(core, *[pltpu.with_memory_space_constraint(x, pltpu.HBM) for x in args])
+    )(place, *[pltpu.with_memory_space_constraint(x, pltpu.HBM) for x in args], *filled)
     return result[:4], list(result[4 : 4 + len(parts)]), list(result[4 + len(parts) :])
 
 
 def intra_kernel(first, heads, q, k, v, g, *rest):
     dq, dk, dv = rest[-3:]
     rows = q.shape[0]
-    row = lax.broadcasted_iota(jnp.int32, (rows, rows), 0)
-    col = lax.broadcasted_iota(jnp.int32, (rows, rows), 1)
+    top = rows // 2
+    row = lax.broadcasted_iota(jnp.int32, (rows, top), 0)
+    col = lax.broadcasted_iota(jnp.int32, (rows, top), 1)
+    below = row >= col
+    row = lax.broadcasted_iota(jnp.int32, (top, rows), 0)
+    col = lax.broadcasted_iota(jnp.int32, (top, rows), 1)
+    above = row <= col
     for h in range(first, first + heads):
         c = head_columns(h)
         qh, kh, vh, gh = q[:, c], k[:, c], v[:, c], g[:, c]
-        grad_scores = jnp.where(row >= col, product(gh, vh, 1, 1), 0.0).astype(BF16)
-        dq[:, c] = product(grad_scores, kh, 1, 0)
-        dk[:, c] = product(grad_scores, qh, 0, 0)
-        attn_scores = jnp.where(row <= col, product(kh, qh, 1, 1), 0.0).astype(BF16)
-        dv[:, c] = product(attn_scores, gh, 1, 0)
+        q1, k0, k1, v0, v1, g1 = qh[top:], kh[:top], kh[top:], vh[:top], vh[top:], gh[top:]
+        left = jnp.where(below, product(gh, v0, 1, 1), 0.0).astype(BF16)
+        right = jnp.where(below[:top], product(g1, v1, 1, 1), 0.0).astype(BF16)
+        dq[:top, c] = product(left[:top], k0, 1, 0)
+        dq[top:, c] = product(jnp.concatenate([left[top:], right], axis=1), kh, 1, 0)
+        dk[:top, c] = product(left, qh, 0, 0)
+        dk[top:, c] = product(right, q1, 0, 0)
+        upper = jnp.where(above, product(k0, qh, 1, 1), 0.0).astype(BF16)
+        lower = jnp.where(above[:, :top], product(k1, q1, 1, 1), 0.0).astype(BF16)
+        dv[:top, c] = product(upper, gh, 1, 0)
+        dv[top:, c] = product(lower, g1, 1, 0)
 
 
 def intra(first, heads, q, k, v, g, filled):
@@ -133,15 +151,16 @@
         if group not in groups:
             write(*group)
     for group, both in zip(groups, states):
-        start, count = place(*group), group[2]
+        owner, first, count = group
+        start = place(*group)
         for i in range(count):
             c = pl.ds(pl.multiple_of(start + i * DH, DH), DH)
             before, behind = both[i].astype(BF16), both[count + i].astype(BF16)
             staged[0][:, c] = (dqi[:, c] + product(g[:, c], before, 1, 1)).astype(BF16)
             staged[1][:, c] = (dki[:, c] + product(v[:, c], behind, 1, 1)).astype(BF16)
             staged[2][:, c] = (dvi[:, c] + product(k[:, c], behind, 1, 0)).astype(BF16)
-        if group in send:
-            write(*group)
+            if group in send:
+                write(owner, first + i, 1)
     for copy in copies:
         copy.wait()
 
@@ -161,7 +180,7 @@
         + [VMEM] * len(staged),
         out_specs=([HBM] * 3 if send else []) + [VMEM] * 3,
         out_shape=shapes,
-        scratch_shapes=[pltpu.SemaphoreType.DMA((3 * max(len(send), 1),))],
+        scratch_shapes=[pltpu.SemaphoreType.DMA((3 * max(sum(count for _, _, count in send), 1),))],
         input_output_aliases={len(inputs) + i: behind + i for i in range(len(filled))},
         compiler_params=pltpu.CompilerParams(vmem_limit_bytes=8 << 20),
         name="final",
@@ -196,12 +215,17 @@
     parts = tuple(
         heads // 2 * (c + 1) // chunks - heads // 2 * c // chunks for c in range(chunks)
     )
-    slots = 1 + (chips - 2) * chunks
+    slots = (chips - 1) * chunks
     plan = PLAN if (heads, slots) == (sum(PLAN), len(PLAN)) else (0,) * (slots - 1) + (heads,)
+    early = chip < chips // 2
+    same = (core == 0) == early
+    place = jnp.stack([core, 1 - early.astype(jnp.int32)])
     at = [chip == c for c in range(chips)]
-    core, first_core, *rest = lax.optimization_barrier((core.reshape(1), core == 0, *at, *args))
-    at, args = rest[:chips], rest[chips:]
-    args, keep, give = states(core, parts, args)
+    core, place, first_core, same, *rest = lax.optimization_barrier(
+        (core.reshape(1), place, core == 0, same, *at, *args)
+    )
+    at, given = rest[:chips], rest[chips:]
+    args, keep, give = states(place, parts, given, ())
     got = [swap(x) for x in give]
     total = [None] * chunks
     local, done = (), 0
@@ -219,8 +243,6 @@
     arrived = [None] * chunks
     event, outs, staged, waiting, own, other = None, (), (), [], [], []
     for step in range(chips):
-        if step == 1:
-            event = local_piece(plan[0], event)
         for c, n in enumerate(parts):
             if step == 0:
                 if c:
@@ -230,20 +252,24 @@
                 (arrived[c],) = after(arrived[c : c + 1], event)
                 prefix[c] = jnp.where(at[step], arrived[c], prefix[c])
                 suffix[c] = jnp.where(at[chips - 1 - step], arrived[c], suffix[c])
+            if step == chips // 2:
+                total[c] = keep_late[c] + got_late[c]
             if step == chips - 1:
                 zero = jnp.zeros_like(prefix[c])
+                kept = jnp.where(same, keep[c], keep_late[c])
+                gotten = jnp.where(same, got_late[c], got[c])
                 own.append(
                     jnp.concatenate(
                         [
-                            prefix[c] + jnp.where(first_core, zero, got[c][:n]),
-                            suffix[c] + jnp.where(first_core, got[c][n:], zero),
+                            prefix[c] + jnp.where(first_core, zero, gotten),
+                            suffix[c] + jnp.where(first_core, gotten, zero),
                         ]
                     )
                 )
                 lend = jnp.concatenate(
                     [
-                        prefix[c] + jnp.where(first_core, keep[c][:n], zero),
-                        suffix[c] + jnp.where(first_core, zero, keep[c][n:]),
+                        prefix[c] + jnp.where(first_core, kept, zero),
+                        suffix[c] + jnp.where(first_core, zero, kept),
                     ]
                 )
                 other.append(swap(lend))
@@ -257,13 +283,14 @@
                 )
                 event = staged[0]
                 continue
-            sent = jnp.where(at[step], total[c][:n], total[c][n:])
-            if step:
-                sent = sent + arrived[c]
+            sent = total[c] + arrived[c] if step else total[c]
             arrived[c] = exchange(sent, chips, step)
             event = sent
-            if step:
-                event = local_piece(plan[1 + (step - 1) * chunks + c], sent)
+            if step == 0 and c == chunks - 1:
+                args, keep_late, give_late = states(place, parts, given, after(args, event))
+                got_late = [swap(x) for x in give_late]
+                event = keep_late[0]
+            event = local_piece(plan[step * chunks + c], event)
     last_group = (True, sum(parts[:-1]), parts[-1])
     send = (*waiting, last_group)
     outs, _ = final((last_group,), send, core, args, local, other[-1:], outs, staged)

time: 29.6 us -> 29.2 us (0.986)
  waiting for transfers between devices: 6.45 us -> 3.32 us
  Pallas kernels: 12.4 us -> 14.2 us
  starting transfers between devices: 9.38 us -> 9.95 us
    ppermute x6, waiting for transfers between devices: 5.31 us -> 2.36 us  [exchange(): return lax.ppermute(value, ('seq', 'sub'), pairs)]
    pallas_call x1 -> x2, Pallas kernels: 2.82 us -> 5.3 us  [states(): pl.pallas_call(functools.partial(states_kernel, parts, 1 if filled else 0...]
    ppermute x4 -> x6, starting transfers between devices: 0.73 us -> 1.31 us  [swap(): return lax.ppermute(value, 'sub', [(0, 1), (1, 0)])]
    pallas_call x3 -> x5, Pallas kernels: 6.25 us -> 5.69 us  [intra(): pl.pallas_call(functools.partial(intra_kernel, first, heads), in_specs=[V...]
    ppermute x4 -> x6, waiting for transfers between devices: 1.14 us -> 0.96 us  [swap(): return lax.ppermute(value, 'sub', [(0, 1), (1, 0)])]
  transfers between devices with their start and end apart: 10 -> 12, of which waited for: 5 -> 4; matrix products, arithmetic and copies ran while one was open for 2% -> 1% of each run, Pallas kernels for 28% -> 36%
where the time goes in v11:
time: 29.2 us; the launch traced here: 29 us
  Pallas kernels  14.2 us (49%)
  starting transfers between devices  9.95 us (34%)
  waiting for transfers between devices  3.32 us (11%)
  between operations  1.02 us (3%)
  other arithmetic  0.47 us (2%)
    ppermute x6, starting transfers between devices, exchange(): return lax.ppermute(value, ('seq', 'sub'), pairs)  8.64 us
    pallas_call x5, Pallas kernels, intra(): pl.pallas_call(functools.partial(intra_kernel, first, heads), in_specs=[V...  5.69 us
    pallas_call x2, Pallas kernels, states(): pl.pallas_call(functools.partial(states_kernel, parts, 1 if filled else 0...  5.3 us
    pallas_call x3, Pallas kernels, final(): pl.pallas_call(functools.partial(final_kernel, groups, send), in_specs=[S...  3.25 us
    ppermute x6, waiting for transfers between devices, exchange(): return lax.ppermute(value, ('seq', 'sub'), pairs)  2.36 us
    ppermute x6, starting transfers between devices, swap(): return lax.ppermute(value, 'sub', [(0, 1), (1, 0)])  1.31 us
    ppermute x6, waiting for transfers between devices, swap(): return lax.ppermute(value, 'sub', [(0, 1), (1, 0)])  0.96 us
  transfers between devices with their start and end apart: 12, of which 4 were waited for; matrix products, arithmetic and copies ran while one was open for 1% of the time, Pallas kernels for 36%

profile of v11, /device:TPU:0, one launch (start us, length us, event | category | flops | bytes accessed | tf_op | source)
XLA Modules:
  0.0 29.0 jit_solution(12139381768145646285)
XLA Ops:
  0.7 0.1 pad_add_fusion.place
  0.7 2.6 %states.2 = (bf16[512,1024]{1,0:T(8,128)(2,1)S(1)}, bf16[512,1024]{1,0:T(8,128)(2,1)S(1)}, bf16[512,1024]{1,0:T(8,128)(2,1)S(1)}, bf16[512,1024]{1,0:T(8,128)(2,...) custom-call(s32[2]{0:T(128)S(1)} %pad_add_fusion.place, ...), custom_call_target="tpu_custom_call" | custom-call | tf_op jit(solution)/shard_map/states/pallas_call | solution.py:78
  3.3 0.5 %collective-permute-start.1 = (f32[2,128,128]{2,1,0:T(8,128)S(1)}, f32[2,128,128]{2,1,0:T(8,128)S(1)}, u32[]{:S(2)}, u32[]{:S(2)}) collective-permute-start(f32[2,128,128]{2,1,0:T(8,128)S(1)} %get-tuple-element.102), channel_id=1, source_target_pairs={{0,1},{1,0},{2,3},{3,2},{4,5},{5,4},{6,7},{7,6},{8,9},{9,8},{10,11... | collective-permute-start | bytes 393224 | tf_op jit(solution)/shard_map/ppermute | solution.py:197
  3.8 0.1 collective-permute-start
  3.9 0.9 %collective-permute-done.1 = f32[2,128,128]{2,1,0:T(8,128)S(1)} collective-permute-done((f32[2,128,128]{2,1,0:T(8,128)S(1)}, f32[2,128,128]{2,1,0:T(8,128)S(1)}, u32[]{:S(2)}, u32[]{:S(2)}) %collective-permute-start.1) | collective-permute-done | bytes 131104 | tf_op jit(solution)/shard_map/ppermute | solution.py:197
  4.8 3.0 %collective-permute-start.4 = (f32[2,128,128]{2,1,0:T(8,128)S(1)}, f32[2,128,128]{2,1,0:T(8,128)S(1)}, u32[]{:S(2)}, u32[]{:S(2)}) collective-permute-start(f32[2,128,128]{2,1,0:T(8,128)S(1)} %add.48), channel_id=1, source_target_pairs={{0,4},{1,5},{4,0},{5,1},{8,12},{9,13},{12,8},{13,9},{2,6},{3,7},{6... | collective-permute-start | bytes 393224 | tf_op jit(solution)/shard_map/ppermute | solution.py:207
  7.8 0.2 collective-permute-start.3
  8.0 2.7 %states.3 = (bf16[512,1024]{1,0:T(8,128)(2,1)S(1)}, bf16[512,1024]{1,0:T(8,128)(2,1)S(1)}, bf16[512,1024]{1,0:T(8,128)(2,1)S(1)}, bf16[512,1024]{1,0:T(8,128)(2,...) custom-call(s32[2]{0:T(128)S(1)} %pad_add_fusion.place, ...), custom_call_target="tpu_custom_call", output_to_operand_aliasing={{0}: (5, {}), {1}: (6, {}), {2}: (7, {}), {3}: (8, {})} | custom-call | tf_op jit(solution)/shard_map/states/pallas_call | solution.py:78
  10.7 0.8 %intra.5 = (f32[512,1024]{1,0:T(8,128)S(1)}, f32[512,1024]{1,0:T(8,128)S(1)}, f32[512,1024]{1,0:T(8,128)S(1)}) custom-call(bf16[512,1024]{1,0:T(8,128)(2,1)S(1)} %get-tuple-element.146.q, bf16[512,1024]{1,0:T(8,128)(2,1)S(1)} %get-tuple-element.147.k, bf16[512,1024]{1,0:T(8,128)(2,1)S(1)} %get-tuple-element.148.v, bf16[512,1024]{1,0:T(8,128)(2,1)S(1)} %get-tuple-element.149.g), custom_call_target="tpu_custom_call" | custom-call | tf_op jit(solution)/shard_map/intra/pallas_call | solution.py:118
  11.5 0.6 %collective-permute-done.4 = f32[2,128,128]{2,1,0:T(8,128)S(1)} collective-permute-done((f32[2,128,128]{2,1,0:T(8,128)S(1)}, f32[2,128,128]{2,1,0:T(8,128)S(1)}, u32[]{:S(2)}, u32[]{:S(2)}) %collective-permute-start.4) | collective-permute-done | bytes 131104 | tf_op jit(solution)/shard_map/ppermute | solution.py:207
  12.1 0.1 collective-permute-start.7
  12.2 0.5 %collective-permute-start.6 = (f32[2,128,128]{2,1,0:T(8,128)S(1)}, f32[2,128,128]{2,1,0:T(8,128)S(1)}, u32[]{:S(2)}, u32[]{:S(2)}) collective-permute-start(f32[2,128,128]{2,1,0:T(8,128)S(1)} %get-tuple-element.129), channel_id=1, source_target_pairs={{0,1},{1,0},{2,3},{3,2},{4,5},{5,4},{6,7},{7,6},{8,9},{9,8},{10,11... | collective-permute-start | bytes 393224 | tf_op jit(solution)/shard_map/ppermute | solution.py:197
  12.7 0.1 collective-permute-start.2
  12.8 0.8 %intra.6 = (f32[512,1024]{1,0:T(8,128)S(1)}, f32[512,1024]{1,0:T(8,128)S(1)}, f32[512,1024]{1,0:T(8,128)S(1)}) custom-call(bf16[512,1024]{1,0:T(8,128)(2,1)S(1)} %get-tuple-element.146.q, bf16[512,1024]{1,0:T(8,128)(2,1)S(1)} %get-tuple-element.147.k, ...), custom_call_target="tpu_custom_call", output_to_operand_aliasing={{0}: (4, {}), {1}: (5, {}), {2}: (6, {})} | custom-call | tf_op jit(solution)/shard_map/intra/pallas_call | solution.py:118
  13.5 0.9 %collective-permute-done.3 = f32[2,128,128]{2,1,0:T(8,128)S(1)} collective-permute-done((f32[2,128,128]{2,1,0:T(8,128)S(1)}, f32[2,128,128]{2,1,0:T(8,128)S(1)}, u32[]{:S(2)}, u32[]{:S(2)}) %collective-permute-start.3) | collective-permute-done | bytes 131104 | tf_op jit(solution)/shard_map/ppermute | solution.py:207
  14.5 1.4 %intra.7 = (f32[512,1024]{1,0:T(8,128)S(1)}, f32[512,1024]{1,0:T(8,128)S(1)}, f32[512,1024]{1,0:T(8,128)S(1)}) custom-call(bf16[512,1024]{1,0:T(8,128)(2,1)S(1)} %get-tuple-element.146.q, bf16[512,1024]{1,0:T(8,128)(2,1)S(1)} %get-tuple-element.147.k, ...), custom_call_target="tpu_custom_call", output_to_operand_aliasing={{0}: (4, {}), {1}: (5, {}), {2}: (6, {})} | custom-call | tf_op jit(solution)/shard_map/intra/pallas_call | solution.py:118
  15.9 3.4 %collective-permute-start.9 = (f32[2,128,128]{2,1,0:T(8,128)S(1)}, f32[2,128,128]{2,1,0:T(8,128)S(1)}, u32[]{:S(2)}, u32[]{:S(2)}) collective-permute-start(f32[2,128,128]{2,1,0:T(8,128)S(1)} %add_add_fusion), channel_id=1, source_target_pairs={{0,4},{1,5},{4,0},{5,1},{8,12},{9,13},{12,8},{13,9},{2,6},{3,7},{6... | collective-permute-start | bytes 393224 | tf_op jit(solution)/shard_map/ppermute | solution.py:207
  19.3 1.4 %intra.8 = (f32[512,1024]{1,0:T(8,128)S(1)}, f32[512,1024]{1,0:T(8,128)S(1)}, f32[512,1024]{1,0:T(8,128)S(1)}) custom-call(bf16[512,1024]{1,0:T(8,128)(2,1)S(1)} %get-tuple-element.146.q, bf16[512,1024]{1,0:T(8,128)(2,1)S(1)} %get-tuple-element.147.k, ...), custom_call_target="tpu_custom_call", output_to_operand_aliasing={{0}: (4, {}), {1}: (5, {}), {2}: (6, {})} | custom-call | tf_op jit(solution)/shard_map/intra/pallas_call | solution.py:118
  20.8 2.0 %collective-permute-start.8 = (f32[2,128,128]{2,1,0:T(8,128)S(1)}, f32[2,128,128]{2,1,0:T(8,128)S(1)}, u32[]{:S(2)}, u32[]{:S(2)}) collective-permute-start(f32[2,128,128]{2,1,0:T(8,128)S(1)} %add_add_fusion.1), channel_id=1, source_target_pairs={{0,4},{1,5},{4,0},{5,1},{8,12},{9,13},{12,8},{13,9},{2,6},{3,7},{6... | collective-permute-start | bytes 393224 | tf_op jit(solution)/shard_map/ppermute | solution.py:207
  22.7 1.4 %intra.9 = (f32[512,1024]{1,0:T(8,128)S(1)}, f32[512,1024]{1,0:T(8,128)S(1)}, f32[512,1024]{1,0:T(8,128)S(1)}) custom-call(bf16[512,1024]{1,0:T(8,128)(2,1)S(1)} %get-tuple-element.146.q, bf16[512,1024]{1,0:T(8,128)(2,1)S(1)} %get-tuple-element.147.k, ...), custom_call_target="tpu_custom_call", output_to_operand_aliasing={{0}: (4, {}), {1}: (5, {}), {2}: (6, {})} | custom-call | tf_op jit(solution)/shard_map/intra/pallas_call | solution.py:118
  24.4 0.5 %final.3 = (bf16[512,1024]{1,0:T(8,128)(2,1)S(1)}, bf16[512,1024]{1,0:T(8,128)(2,1)S(1)}, bf16[512,1024]{1,0:T(8,128)(2,1)S(1)}) custom-call(s32[1]{0:T(128)} %bitcast.core, bf16[512,1024]{1,0:T(8,128)(2,1)S(1)} %get-tuple-element.147.k, bf16[512,1024]{1,0:T(8,128)(2,1)S(1)} %get-tuple-element.148.v, bf16[512,1024]{1,0:T(8,128)(2,1)S(1)} %get-tuple-element.149.g, ...), custom_call_target="tpu_custom_call" | custom-call | tf_op jit(solution)/shard_map/final/pallas_call | solution.py:175
  24.9 0.9 %collective-permute-done.8 = f32[2,128,128]{2,1,0:T(8,128)S(1)} collective-permute-done((f32[2,128,128]{2,1,0:T(8,128)S(1)}, f32[2,128,128]{2,1,0:T(8,128)S(1)}, u32[]{:S(2)}, u32[]{:S(2)}) %collective-permute-start.8) | collective-permute-done | bytes 131104 | tf_op jit(solution)/shard_map/ppermute | solution.py:207
  26.0 1.4 %final.4 = (bf16[512,1024]{1,0:T(8,128)(2,1)}, bf16[512,1024]{1,0:T(8,128)(2,1)}, bf16[512,1024]{1,0:T(8,128)(2,1)}, bf16[512,1024]{1,0:T(8,128)(2,1)S(1)}, bf16...) custom-call(s32[1]{0:T(128)} %bitcast.core, ...), custom_call_target="tpu_custom_call", output_to_operand_aliasing={{3}: (9, {}), {4}: (10, {}), {5}: (11, {})} | custom-call | tf_op jit(solution)/shard_map/final/pallas_call | solution.py:175
  27.5 1.3 %final.5 = (bf16[512,1024]{1,0:T(8,128)(2,1)}, bf16[512,1024]{1,0:T(8,128)(2,1)}, bf16[512,1024]{1,0:T(8,128)(2,1)}, bf16[512,1024]{1,0:T(8,128)(2,1)S(1)}, bf16...) custom-call(s32[1]{0:T(128)} %bitcast.core, ...), custom_call_target="tpu_custom_call", output_to_operand_aliasing={{0}: (8, {}), {1}: (9, {}), {2}: (10, {}), {3}: (11, {}), {... | custom-call | tf_op jit(solution)/shard_map/final/pallas_call | solution.py:175
  (25 shorter events, 0.7 us)
Async XLA Ops:
  3.3 1.5 %collective-permute-start.1 = (f32[2,128,128]{2,1,0:T(8,128)S(1)}, f32[2,128,128]{2,1,0:T(8,128)S(1)}, u32[]{:S(2)}, u32[]{:S(2)}) collective-permute-start(f32[2,128,128]{2,1,0:T(8,128)S(1)} %get-tuple-element.102), channel_id=1, source_target_pairs={{0,1},{1,0},{2,3},{3,2},{4,5},{5,4},{6,7},{7,6},{8,9},{9,8},{10,11... | collective-permute-start | bytes 393224 | tf_op jit(solution)/shard_map/ppermute | solution.py:197
  3.8 4.0 %collective-permute-start = (f32[2,128,128]{2,1,0:T(8,128)S(1)}, f32[2,128,128]{2,1,0:T(8,128)S(1)}, u32[]{:S(2)}, u32[]{:S(2)}) collective-permute-start(f32[2,128,128]{2,1,0:T(8,128)S(1)} %get-tuple-element.100), channel_id=1, source_target_pairs={{0,1},{1,0},{2,3},{3,2},{4,5},{5,4},{6,7},{7,6},{8,9},{9,8},{10,11... | collective-permute-start | bytes 393224 | tf_op jit(solution)/shard_map/ppermute | solution.py:197
  4.8 7.3 %collective-permute-start.4 = (f32[2,128,128]{2,1,0:T(8,128)S(1)}, f32[2,128,128]{2,1,0:T(8,128)S(1)}, u32[]{:S(2)}, u32[]{:S(2)}) collective-permute-start(f32[2,128,128]{2,1,0:T(8,128)S(1)} %add.48), channel_id=1, source_target_pairs={{0,4},{1,5},{4,0},{5,1},{8,12},{9,13},{12,8},{13,9},{2,6},{3,7},{6... | collective-permute-start | bytes 393224 | tf_op jit(solution)/shard_map/ppermute | solution.py:207
  7.8 6.6 %collective-permute-start.3 = (f32[2,128,128]{2,1,0:T(8,128)S(1)}, f32[2,128,128]{2,1,0:T(8,128)S(1)}, u32[]{:S(2)}, u32[]{:S(2)}) collective-permute-start(f32[2,128,128]{2,1,0:T(8,128)S(1)} %add.49), channel_id=1, source_target_pairs={{0,4},{1,5},{4,0},{5,1},{8,12},{9,13},{12,8},{13,9},{2,6},{3,7},{6... | collective-permute-start | bytes 393224 | tf_op jit(solution)/shard_map/ppermute | solution.py:207
  12.1 3.8 %collective-permute-start.7 = (f32[2,128,128]{2,1,0:T(8,128)S(1)}, f32[2,128,128]{2,1,0:T(8,128)S(1)}, u32[]{:S(2)}, u32[]{:S(2)}) collective-permute-start(f32[2,128,128]{2,1,0:T(8,128)S(1)} %add.51), channel_id=1, source_target_pairs={{0,1},{1,0},{4,8},{5,9},{8,4},{9,5},{12,13},{13,12},{2,3},{3,2},{6... | collective-permute-start | bytes 393224 | tf_op jit(solution)/shard_map/ppermute | solution.py:207
  12.2 3.7 %collective-permute-start.6 = (f32[2,128,128]{2,1,0:T(8,128)S(1)}, f32[2,128,128]{2,1,0:T(8,128)S(1)}, u32[]{:S(2)}, u32[]{:S(2)}) collective-permute-start(f32[2,128,128]{2,1,0:T(8,128)S(1)} %get-tuple-element.129), channel_id=1, source_target_pairs={{0,1},{1,0},{2,3},{3,2},{4,5},{5,4},{6,7},{7,6},{8,9},{9,8},{10,11... | collective-permute-start | bytes 393224 | tf_op jit(solution)/shard_map/ppermute | solution.py:197
  12.7 8.1 %collective-permute-start.2 = (f32[2,128,128]{2,1,0:T(8,128)S(1)}, f32[2,128,128]{2,1,0:T(8,128)S(1)}, u32[]{:S(2)}, u32[]{:S(2)}) collective-permute-start(f32[2,128,128]{2,1,0:T(8,128)S(1)} %get-tuple-element.113), channel_id=1, source_target_pairs={{0,1},{1,0},{2,3},{3,2},{4,5},{5,4},{6,7},{7,6},{8,9},{9,8},{10,11... | collective-permute-start | bytes 393224 | tf_op jit(solution)/shard_map/ppermute | solution.py:197
  14.4 6.3 %collective-permute-start.5 = (f32[2,128,128]{2,1,0:T(8,128)S(1)}, f32[2,128,128]{2,1,0:T(8,128)S(1)}, u32[]{:S(2)}, u32[]{:S(2)}) collective-permute-start(f32[2,128,128]{2,1,0:T(8,128)S(1)} %add.52), channel_id=1, source_target_pairs={{0,1},{1,0},{4,8},{5,9},{8,4},{9,5},{12,13},{13,12},{2,3},{3,2},{6... | collective-permute-start | bytes 393224 | tf_op jit(solution)/shard_map/ppermute | solution.py:207
  15.9 8.2 %collective-permute-start.9 = (f32[2,128,128]{2,1,0:T(8,128)S(1)}, f32[2,128,128]{2,1,0:T(8,128)S(1)}, u32[]{:S(2)}, u32[]{:S(2)}) collective-permute-start(f32[2,128,128]{2,1,0:T(8,128)S(1)} %add_add_fusion), channel_id=1, source_target_pairs={{0,4},{1,5},{4,0},{5,1},{8,12},{9,13},{12,8},{13,9},{2,6},{3,7},{6... | collective-permute-start | bytes 393224 | tf_op jit(solution)/shard_map/ppermute | solution.py:207
  20.8 5.0 %collective-permute-start.8 = (f32[2,128,128]{2,1,0:T(8,128)S(1)}, f32[2,128,128]{2,1,0:T(8,128)S(1)}, u32[]{:S(2)}, u32[]{:S(2)}) collective-permute-start(f32[2,128,128]{2,1,0:T(8,128)S(1)} %add_add_fusion.1), channel_id=1, source_target_pairs={{0,4},{1,5},{4,0},{5,1},{8,12},{9,13},{12,8},{13,9},{2,6},{3,7},{6... | collective-permute-start | bytes 393224 | tf_op jit(solution)/shard_map/ppermute | solution.py:207
  24.2 1.8 %collective-permute-start.11 = (f32[4,128,128]{2,1,0:T(8,128)S(1)}, f32[4,128,128]{2,1,0:T(8,128)S(1)}, u32[]{:S(2)}, u32[]{:S(2)}) collective-permute-start(f32[4,128,128]{2,1,0:T(8,128)S(1)} %pad_maximum_fusion.2), channel_id=1, source_target_pairs={{0,1},{1,0},{2,3},{3,2},{4,5},{5,4},{6,7},{7,6},{8,9},{9,8},{10,11... | collective-permute-start | bytes 786440 | tf_op jit(solution)/shard_map/ppermute | solution.py:197
  25.9 1.6 %collective-permute-start.10 = (f32[4,128,128]{2,1,0:T(8,128)S(1)}, f32[4,128,128]{2,1,0:T(8,128)S(1)}, u32[]{:S(2)}, u32[]{:S(2)}) collective-permute-start(f32[4,128,128]{2,1,0:T(8,128)S(1)} %pad_maximum_fusion.1), channel_id=1, source_target_pairs={{0,1},{1,0},{2,3},{3,2},{4,5},{5,4},{6,7},{7,6},{8,9},{9,8},{10,11... | collective-permute-start | bytes 786440 | tf_op jit(solution)/shard_map/ppermute | solution.py:197

commit v12 on v11

--- a/solution.py
+++ b/solution.py
@@ -42,27 +42,24 @@
                 h += 1
 
     def run(x_hbm, y_hbm, x, y):
-        loads = []
-        for half in (0, 1):
-            c = slice(half * width, (half + 1) * width)
-            for i, (source, target) in enumerate(((x_hbm, x), (y_hbm, y))):
-                loads.append(
-                    pltpu.make_async_copy(
-                        source.at[:, c], target.at[:, c], sems.at[2 * half + i]
-                    )
-                )
-                loads[-1].start()
-        for half in (0, 1):
-            for copy in loads[2 * half : 2 * half + 2]:
-                copy.wait()
-
-            @pl.when(place[0] == half)
-            def _():
-                fill(keep, x, y, half)
-
-            @pl.when(place[0] != half)
-            def _():
-                fill(give, x, y, half)
+        loads = [
+            pltpu.make_async_copy(source, target, sems.at[i])
+            for i, (source, target) in enumerate(((x_hbm, x), (y_hbm, y)))
+        ]
+        for copy in loads:
+            copy.start()
+        for copy in loads:
+            copy.wait()
+
+        @pl.when(place[0] == 0)
+        def _():
+            fill(give, x, y, 1)
+            fill(keep, x, y, 0)
+
+        @pl.when(place[0] != 0)
+        def _():
+            fill(give, x, y, 0)
+            fill(keep, x, y, 1)
 
     @pl.when(place[1] == later)
     def _():
@@ -80,7 +77,7 @@
         in_specs=[SMEM] + [HBM] * 4 + [VMEM] * len(filled),
         out_specs=[VMEM] * (4 + len(outs)),
         out_shape=[pltpu.VMEM(args[0].shape, BF16)] * 4 + outs,
-        scratch_shapes=[pltpu.SemaphoreType.DMA((4,))],
+        scratch_shapes=[pltpu.SemaphoreType.DMA((2,))],
         input_output_aliases={5 + i: i for i in range(len(filled))},
         compiler_params=pltpu.CompilerParams(vmem_limit_bytes=8 << 20),
         name="states",

time: 29.2 us -> 29.3 us (level)
  no operation moved by 1% of the time
where the time goes in v12:
time: 29.3 us; the launch traced here: 29.1 us
  Pallas kernels  14.4 us (49%)
  starting transfers between devices  9.94 us (34%)
  waiting for transfers between devices  3.25 us (11%)
  between operations  1.02 us (3%)
  other arithmetic  0.47 us (2%)
    ppermute x6, starting transfers between devices, exchange(): return lax.ppermute(value, ('seq', 'sub'), pairs)  8.63 us
    pallas_call x5, Pallas kernels, intra(): pl.pallas_call(functools.partial(intra_kernel, first, heads), in_specs=[V...  5.71 us
    pallas_call x2, Pallas kernels, states(): pl.pallas_call(functools.partial(states_kernel, parts, 1 if filled else 0...  5.44 us
    pallas_call x3, Pallas kernels, final(): pl.pallas_call(functools.partial(final_kernel, groups, send), in_specs=[S...  3.26 us
    ppermute x6, waiting for transfers between devices, exchange(): return lax.ppermute(value, ('seq', 'sub'), pairs)  2.29 us
    ppermute x6, starting transfers between devices, swap(): return lax.ppermute(value, 'sub', [(0, 1), (1, 0)])  1.31 us
    ppermute x6, waiting for transfers between devices, swap(): return lax.ppermute(value, 'sub', [(0, 1), (1, 0)])  0.96 us
  transfers between devices with their start and end apart: 12, of which 4 were waited for; matrix products, arithmetic and copies ran while one was open for 1% of the time, Pallas kernels for 36%

profile of v12, /device:TPU:0, one launch (start us, length us, event | category | flops | bytes accessed | tf_op | source)
XLA Modules:
  0.0 29.1 jit_solution(9682015050977022145)
XLA Ops:
  0.7 0.1 pad_add_fusion.place
  0.7 2.6 %states.2 = (bf16[512,1024]{1,0:T(8,128)(2,1)S(1)}, bf16[512,1024]{1,0:T(8,128)(2,1)S(1)}, bf16[512,1024]{1,0:T(8,128)(2,1)S(1)}, bf16[512,1024]{1,0:T(8,128)(2,...) custom-call(s32[2]{0:T(128)S(1)} %pad_add_fusion.place, ...), custom_call_target="tpu_custom_call" | custom-call | tf_op jit(solution)/shard_map/states/pallas_call | solution.py:75
  3.4 0.5 %collective-permute-start.1 = (f32[2,128,128]{2,1,0:T(8,128)S(1)}, f32[2,128,128]{2,1,0:T(8,128)S(1)}, u32[]{:S(2)}, u32[]{:S(2)}) collective-permute-start(f32[2,128,128]{2,1,0:T(8,128)S(1)} %get-tuple-element.102), channel_id=1, source_target_pairs={{0,1},{1,0},{2,3},{3,2},{4,5},{5,4},{6,7},{7,6},{8,9},{9,8},{10,11... | collective-permute-start | bytes 393224 | tf_op jit(solution)/shard_map/ppermute | solution.py:194
  3.9 0.1 collective-permute-start
  3.9 0.9 %collective-permute-done.1 = f32[2,128,128]{2,1,0:T(8,128)S(1)} collective-permute-done((f32[2,128,128]{2,1,0:T(8,128)S(1)}, f32[2,128,128]{2,1,0:T(8,128)S(1)}, u32[]{:S(2)}, u32[]{:S(2)}) %collective-permute-start.1) | collective-permute-done | bytes 131104 | tf_op jit(solution)/shard_map/ppermute | solution.py:194
  4.9 3.0 %collective-permute-start.4 = (f32[2,128,128]{2,1,0:T(8,128)S(1)}, f32[2,128,128]{2,1,0:T(8,128)S(1)}, u32[]{:S(2)}, u32[]{:S(2)}) collective-permute-start(f32[2,128,128]{2,1,0:T(8,128)S(1)} %add.48), channel_id=1, source_target_pairs={{0,4},{1,5},{4,0},{5,1},{8,12},{9,13},{12,8},{13,9},{2,6},{3,7},{6... | collective-permute-start | bytes 393224 | tf_op jit(solution)/shard_map/ppermute | solution.py:204
  7.9 0.2 collective-permute-start.3
  8.1 2.8 %states.3 = (bf16[512,1024]{1,0:T(8,128)(2,1)S(1)}, bf16[512,1024]{1,0:T(8,128)(2,1)S(1)}, bf16[512,1024]{1,0:T(8,128)(2,1)S(1)}, bf16[512,1024]{1,0:T(8,128)(2,...) custom-call(s32[2]{0:T(128)S(1)} %pad_add_fusion.place, ...), custom_call_target="tpu_custom_call", output_to_operand_aliasing={{0}: (5, {}), {1}: (6, {}), {2}: (7, {}), {3}: (8, {})} | custom-call | tf_op jit(solution)/shard_map/states/pallas_call | solution.py:75
  10.9 0.8 %intra.5 = (f32[512,1024]{1,0:T(8,128)S(1)}, f32[512,1024]{1,0:T(8,128)S(1)}, f32[512,1024]{1,0:T(8,128)S(1)}) custom-call(bf16[512,1024]{1,0:T(8,128)(2,1)S(1)} %get-tuple-element.146.q, bf16[512,1024]{1,0:T(8,128)(2,1)S(1)} %get-tuple-element.147.k, bf16[512,1024]{1,0:T(8,128)(2,1)S(1)} %get-tuple-element.148.v, bf16[512,1024]{1,0:T(8,128)(2,1)S(1)} %get-tuple-element.149.g), custom_call_target="tpu_custom_call" | custom-call | tf_op jit(solution)/shard_map/intra/pallas_call | solution.py:115
  11.7 0.5 %collective-permute-done.4 = f32[2,128,128]{2,1,0:T(8,128)S(1)} collective-permute-done((f32[2,128,128]{2,1,0:T(8,128)S(1)}, f32[2,128,128]{2,1,0:T(8,128)S(1)}, u32[]{:S(2)}, u32[]{:S(2)}) %collective-permute-start.4) | collective-permute-done | bytes 131104 | tf_op jit(solution)/shard_map/ppermute | solution.py:204
  12.3 0.5 %collective-permute-start.6 = (f32[2,128,128]{2,1,0:T(8,128)S(1)}, f32[2,128,128]{2,1,0:T(8,128)S(1)}, u32[]{:S(2)}, u32[]{:S(2)}) collective-permute-start(f32[2,128,128]{2,1,0:T(8,128)S(1)} %get-tuple-element.129), channel_id=1, source_target_pairs={{0,1},{1,0},{2,3},{3,2},{4,5},{5,4},{6,7},{7,6},{8,9},{9,8},{10,11... | collective-permute-start | bytes 393224 | tf_op jit(solution)/shard_map/ppermute | solution.py:194
  12.8 0.1 collective-permute-start.2
  12.8 0.8 %intra.6 = (f32[512,1024]{1,0:T(8,128)S(1)}, f32[512,1024]{1,0:T(8,128)S(1)}, f32[512,1024]{1,0:T(8,128)S(1)}) custom-call(bf16[512,1024]{1,0:T(8,128)(2,1)S(1)} %get-tuple-element.146.q, bf16[512,1024]{1,0:T(8,128)(2,1)S(1)} %get-tuple-element.147.k, ...), custom_call_target="tpu_custom_call", output_to_operand_aliasing={{0}: (4, {}), {1}: (5, {}), {2}: (6, {})} | custom-call | tf_op jit(solution)/shard_map/intra/pallas_call | solution.py:115
  13.6 0.9 %collective-permute-done.3 = f32[2,128,128]{2,1,0:T(8,128)S(1)} collective-permute-done((f32[2,128,128]{2,1,0:T(8,128)S(1)}, f32[2,128,128]{2,1,0:T(8,128)S(1)}, u32[]{:S(2)}, u32[]{:S(2)}) %collective-permute-start.3) | collective-permute-done | bytes 131104 | tf_op jit(solution)/shard_map/ppermute | solution.py:204
  14.6 1.4 %intra.7 = (f32[512,1024]{1,0:T(8,128)S(1)}, f32[512,1024]{1,0:T(8,128)S(1)}, f32[512,1024]{1,0:T(8,128)S(1)}) custom-call(bf16[512,1024]{1,0:T(8,128)(2,1)S(1)} %get-tuple-element.146.q, bf16[512,1024]{1,0:T(8,128)(2,1)S(1)} %get-tuple-element.147.k, ...), custom_call_target="tpu_custom_call", output_to_operand_aliasing={{0}: (4, {}), {1}: (5, {}), {2}: (6, {})} | custom-call | tf_op jit(solution)/shard_map/intra/pallas_call | solution.py:115
  16.0 3.4 %collective-permute-start.9 = (f32[2,128,128]{2,1,0:T(8,128)S(1)}, f32[2,128,128]{2,1,0:T(8,128)S(1)}, u32[]{:S(2)}, u32[]{:S(2)}) collective-permute-start(f32[2,128,128]{2,1,0:T(8,128)S(1)} %add_add_fusion), channel_id=1, source_target_pairs={{0,4},{1,5},{4,0},{5,1},{8,12},{9,13},{12,8},{13,9},{2,6},{3,7},{6... | collective-permute-start | bytes 393224 | tf_op jit(solution)/shard_map/ppermute | solution.py:204
  19.4 1.4 %intra.8 = (f32[512,1024]{1,0:T(8,128)S(1)}, f32[512,1024]{1,0:T(8,128)S(1)}, f32[512,1024]{1,0:T(8,128)S(1)}) custom-call(bf16[512,1024]{1,0:T(8,128)(2,1)S(1)} %get-tuple-element.146.q, bf16[512,1024]{1,0:T(8,128)(2,1)S(1)} %get-tuple-element.147.k, ...), custom_call_target="tpu_custom_call", output_to_operand_aliasing={{0}: (4, {}), {1}: (5, {}), {2}: (6, {})} | custom-call | tf_op jit(solution)/shard_map/intra/pallas_call | solution.py:115
  20.9 1.9 %collective-permute-start.8 = (f32[2,128,128]{2,1,0:T(8,128)S(1)}, f32[2,128,128]{2,1,0:T(8,128)S(1)}, u32[]{:S(2)}, u32[]{:S(2)}) collective-permute-start(f32[2,128,128]{2,1,0:T(8,128)S(1)} %add_add_fusion.1), channel_id=1, source_target_pairs={{0,4},{1,5},{4,0},{5,1},{8,12},{9,13},{12,8},{13,9},{2,6},{3,7},{6... | collective-permute-start | bytes 393224 | tf_op jit(solution)/shard_map/ppermute | solution.py:204
  22.8 1.4 %intra.9 = (f32[512,1024]{1,0:T(8,128)S(1)}, f32[512,1024]{1,0:T(8,128)S(1)}, f32[512,1024]{1,0:T(8,128)S(1)}) custom-call(bf16[512,1024]{1,0:T(8,128)(2,1)S(1)} %get-tuple-element.146.q, bf16[512,1024]{1,0:T(8,128)(2,1)S(1)} %get-tuple-element.147.k, ...), custom_call_target="tpu_custom_call", output_to_operand_aliasing={{0}: (4, {}), {1}: (5, {}), {2}: (6, {})} | custom-call | tf_op jit(solution)/shard_map/intra/pallas_call | solution.py:115
  24.3 0.1 collective-permute-start.11
  24.4 0.5 %final.3 = (bf16[512,1024]{1,0:T(8,128)(2,1)S(1)}, bf16[512,1024]{1,0:T(8,128)(2,1)S(1)}, bf16[512,1024]{1,0:T(8,128)(2,1)S(1)}) custom-call(s32[1]{0:T(128)} %bitcast.core, bf16[512,1024]{1,0:T(8,128)(2,1)S(1)} %get-tuple-element.147.k, bf16[512,1024]{1,0:T(8,128)(2,1)S(1)} %get-tuple-element.148.v, bf16[512,1024]{1,0:T(8,128)(2,1)S(1)} %get-tuple-element.149.g, ...), custom_call_target="tpu_custom_call" | custom-call | tf_op jit(solution)/shard_map/final/pallas_call | solution.py:172
  25.0 0.9 %collective-permute-done.8 = f32[2,128,128]{2,1,0:T(8,128)S(1)} collective-permute-done((f32[2,128,128]{2,1,0:T(8,128)S(1)}, f32[2,128,128]{2,1,0:T(8,128)S(1)}, u32[]{:S(2)}, u32[]{:S(2)}) %collective-permute-start.8) | collective-permute-done | bytes 131104 | tf_op jit(solution)/shard_map/ppermute | solution.py:204
  26.1 1.4 %final.4 = (bf16[512,1024]{1,0:T(8,128)(2,1)}, bf16[512,1024]{1,0:T(8,128)(2,1)}, bf16[512,1024]{1,0:T(8,128)(2,1)}, bf16[512,1024]{1,0:T(8,128)(2,1)S(1)}, bf16...) custom-call(s32[1]{0:T(128)} %bitcast.core, ...), custom_call_target="tpu_custom_call", output_to_operand_aliasing={{3}: (9, {}), {4}: (10, {}), {5}: (11, {})} | custom-call | tf_op jit(solution)/shard_map/final/pallas_call | solution.py:172
  27.6 1.3 %final.5 = (bf16[512,1024]{1,0:T(8,128)(2,1)}, bf16[512,1024]{1,0:T(8,128)(2,1)}, bf16[512,1024]{1,0:T(8,128)(2,1)}, bf16[512,1024]{1,0:T(8,128)(2,1)S(1)}, bf16...) custom-call(s32[1]{0:T(128)} %bitcast.core, ...), custom_call_target="tpu_custom_call", output_to_operand_aliasing={{0}: (8, {}), {1}: (9, {}), {2}: (10, {}), {3}: (11, {}), {... | custom-call | tf_op jit(solution)/shard_map/final/pallas_call | solution.py:172
  (25 shorter events, 0.7 us)
Async XLA Ops:
  3.4 1.5 %collective-permute-start.1 = (f32[2,128,128]{2,1,0:T(8,128)S(1)}, f32[2,128,128]{2,1,0:T(8,128)S(1)}, u32[]{:S(2)}, u32[]{:S(2)}) collective-permute-start(f32[2,128,128]{2,1,0:T(8,128)S(1)} %get-tuple-element.102), channel_id=1, source_target_pairs={{0,1},{1,0},{2,3},{3,2},{4,5},{5,4},{6,7},{7,6},{8,9},{9,8},{10,11... | collective-permute-start | bytes 393224 | tf_op jit(solution)/shard_map/ppermute | solution.py:194
  3.9 4.0 %collective-permute-start = (f32[2,128,128]{2,1,0:T(8,128)S(1)}, f32[2,128,128]{2,1,0:T(8,128)S(1)}, u32[]{:S(2)}, u32[]{:S(2)}) collective-permute-start(f32[2,128,128]{2,1,0:T(8,128)S(1)} %get-tuple-element.100), channel_id=1, source_target_pairs={{0,1},{1,0},{2,3},{3,2},{4,5},{5,4},{6,7},{7,6},{8,9},{9,8},{10,11... | collective-permute-start | bytes 393224 | tf_op jit(solution)/shard_map/ppermute | solution.py:194
  4.9 7.3 %collective-permute-start.4 = (f32[2,128,128]{2,1,0:T(8,128)S(1)}, f32[2,128,128]{2,1,0:T(8,128)S(1)}, u32[]{:S(2)}, u32[]{:S(2)}) collective-permute-start(f32[2,128,128]{2,1,0:T(8,128)S(1)} %add.48), channel_id=1, source_target_pairs={{0,4},{1,5},{4,0},{5,1},{8,12},{9,13},{12,8},{13,9},{2,6},{3,7},{6... | collective-permute-start | bytes 393224 | tf_op jit(solution)/shard_map/ppermute | solution.py:204
  7.9 6.6 %collective-permute-start.3 = (f32[2,128,128]{2,1,0:T(8,128)S(1)}, f32[2,128,128]{2,1,0:T(8,128)S(1)}, u32[]{:S(2)}, u32[]{:S(2)}) collective-permute-start(f32[2,128,128]{2,1,0:T(8,128)S(1)} %add.49), channel_id=1, source_target_pairs={{0,4},{1,5},{4,0},{5,1},{8,12},{9,13},{12,8},{13,9},{2,6},{3,7},{6... | collective-permute-start | bytes 393224 | tf_op jit(solution)/shard_map/ppermute | solution.py:204
  12.2 3.8 %collective-permute-start.7 = (f32[2,128,128]{2,1,0:T(8,128)S(1)}, f32[2,128,128]{2,1,0:T(8,128)S(1)}, u32[]{:S(2)}, u32[]{:S(2)}) collective-permute-start(f32[2,128,128]{2,1,0:T(8,128)S(1)} %add.51), channel_id=1, source_target_pairs={{0,1},{1,0},{4,8},{5,9},{8,4},{9,5},{12,13},{13,12},{2,3},{3,2},{6... | collective-permute-start | bytes 393224 | tf_op jit(solution)/shard_map/ppermute | solution.py:204
  12.3 3.7 %collective-permute-start.6 = (f32[2,128,128]{2,1,0:T(8,128)S(1)}, f32[2,128,128]{2,1,0:T(8,128)S(1)}, u32[]{:S(2)}, u32[]{:S(2)}) collective-permute-start(f32[2,128,128]{2,1,0:T(8,128)S(1)} %get-tuple-element.129), channel_id=1, source_target_pairs={{0,1},{1,0},{2,3},{3,2},{4,5},{5,4},{6,7},{7,6},{8,9},{9,8},{10,11... | collective-permute-start | bytes 393224 | tf_op jit(solution)/shard_map/ppermute | solution.py:194
  12.8 8.1 %collective-permute-start.2 = (f32[2,128,128]{2,1,0:T(8,128)S(1)}, f32[2,128,128]{2,1,0:T(8,128)S(1)}, u32[]{:S(2)}, u32[]{:S(2)}) collective-permute-start(f32[2,128,128]{2,1,0:T(8,128)S(1)} %get-tuple-element.113), channel_id=1, source_target_pairs={{0,1},{1,0},{2,3},{3,2},{4,5},{5,4},{6,7},{7,6},{8,9},{9,8},{10,11... | collective-permute-start | bytes 393224 | tf_op jit(solution)/shard_map/ppermute | solution.py:194
  14.5 6.3 %collective-permute-start.5 = (f32[2,128,128]{2,1,0:T(8,128)S(1)}, f32[2,128,128]{2,1,0:T(8,128)S(1)}, u32[]{:S(2)}, u32[]{:S(2)}) collective-permute-start(f32[2,128,128]{2,1,0:T(8,128)S(1)} %add.52), channel_id=1, source_target_pairs={{0,1},{1,0},{4,8},{5,9},{8,4},{9,5},{12,13},{13,12},{2,3},{3,2},{6... | collective-permute-start | bytes 393224 | tf_op jit(solution)/shard_map/ppermute | solution.py:204
  16.0 8.1 %collective-permute-start.9 = (f32[2,128,128]{2,1,0:T(8,128)S(1)}, f32[2,128,128]{2,1,0:T(8,128)S(1)}, u32[]{:S(2)}, u32[]{:S(2)}) collective-permute-start(f32[2,128,128]{2,1,0:T(8,128)S(1)} %add_add_fusion), channel_id=1, source_target_pairs={{0,4},{1,5},{4,0},{5,1},{8,12},{9,13},{12,8},{13,9},{2,6},{3,7},{6... | collective-permute-start | bytes 393224 | tf_op jit(solution)/shard_map/ppermute | solution.py:204
  20.9 5.0 %collective-permute-start.8 = (f32[2,128,128]{2,1,0:T(8,128)S(1)}, f32[2,128,128]{2,1,0:T(8,128)S(1)}, u32[]{:S(2)}, u32[]{:S(2)}) collective-permute-start(f32[2,128,128]{2,1,0:T(8,128)S(1)} %add_add_fusion.1), channel_id=1, source_target_pairs={{0,4},{1,5},{4,0},{5,1},{8,12},{9,13},{12,8},{13,9},{2,6},{3,7},{6... | collective-permute-start | bytes 393224 | tf_op jit(solution)/shard_map/ppermute | solution.py:204
  24.3 1.8 %collective-permute-start.11 = (f32[4,128,128]{2,1,0:T(8,128)S(1)}, f32[4,128,128]{2,1,0:T(8,128)S(1)}, u32[]{:S(2)}, u32[]{:S(2)}) collective-permute-start(f32[4,128,128]{2,1,0:T(8,128)S(1)} %pad_maximum_fusion.2), channel_id=1, source_target_pairs={{0,1},{1,0},{2,3},{3,2},{4,5},{5,4},{6,7},{7,6},{8,9},{9,8},{10,11... | collective-permute-start | bytes 786440 | tf_op jit(solution)/shard_map/ppermute | solution.py:194
  26.0 1.6 %collective-permute-start.10 = (f32[4,128,128]{2,1,0:T(8,128)S(1)}, f32[4,128,128]{2,1,0:T(8,128)S(1)}, u32[]{:S(2)}, u32[]{:S(2)}) collective-permute-start(f32[4,128,128]{2,1,0:T(8,128)S(1)} %pad_maximum_fusion.1), channel_id=1, source_target_pairs={{0,1},{1,0},{2,3},{3,2},{4,5},{5,4},{6,7},{7,6},{8,9},{9,8},{10,11... | collective-permute-start | bytes 786440 | tf_op jit(solution)/shard_map/ppermute | solution.py:194
